TPU v7x, 32 devices: a whole 2x2x4 slice. The times are simulated.
32 devices in a mesh: band: 4 (over z), dom: 8 (over y, x, core).
Axes of the slice: x: 2, y: 2, z: 4, core: 2. Of those that a mesh axis runs over, the one named last changes fastest.
Arguments:
- response: float32 [4, 256, 32, 8, 128], P(None, 'band', 'dom'), may hold values from -6 to 6
- occupied: float32 [256, 32, 8, 128], P('band', 'dom'), may hold values from -6 to 6
- locked_set: bfloat16 [4096, 32, 8, 128], P(None, 'dom'), may hold values from -0.03125 to 0.03125
- potential: float32 [32, 8, 128], P('dom'), may hold values from -1.5 to 0
- perturbation: float32 [4, 32, 8, 128], P(None, 'dom'), may hold values from -30 to 30
- xc_kernel: float32 [32, 8, 128], P('dom'), may hold values from 0.005 to 0.03
- energies: float32 [256], P('band'), may hold values from -1 to -0.2
- first_step: float32 [4, 256], P(None, 'band'), may hold values from 0.03 to 0.1
- second_step: float32 [4, 256], P(None, 'band'), may hold values from 0.03 to 0.1
Outputs:
- new_response: float32 [4, 256, 32, 8, 128], P(None, 'band', 'dom')
- response_potential: float32 [4, 32, 8, 128], P(None, 'dom')
All inputs are finite; a program needn't handle non-finite values.
Results may differ from a plain program's by a relative error of at most 0.007.
Values may be sent and summed in bfloat16 or wider, within the bound.
No kernel may reach another device: no remote copies, remote signals or barrier semaphores. Data moves between devices by JAX's collectives and lax.ppermute only.
A program may use at most 256 MiB of HBM per device.

v0:
```python
import jax
import jax.numpy as jnp
from jax import lax
from jax.sharding import PartitionSpec as P

near_weight = 4.0 / 3.0
far_weight = -1.0 / 12.0
centre_weight = -7.5
block_count = 4


def with_halo(block, sides, width):
    for axis, dim in sides:
        count = lax.axis_size(axis)
        forward = [(i, i + 1) for i in range(count - 1)]
        forward.append((count - 1, 0))
        backward = [(target, source) for source, target in forward]
        low = lax.ppermute(
            lax.slice_in_dim(block, block.shape[dim] - width, None, axis=dim), axis, forward
        )
        high = lax.ppermute(lax.slice_in_dim(block, 0, width, axis=dim), axis, backward)
        block = jnp.concatenate([low, block, high], axis=dim)
    return block


def laplace_local(grid_field):
    padded = with_halo(grid_field.astype(jnp.bfloat16), (("dom", 2),), 2).astype(grid_field.dtype)
    result = centre_weight * grid_field
    result = result + near_weight * (padded[:, :, 3:-1] + padded[:, :, 1:-3])
    result = result + far_weight * (padded[:, :, 4:] + padded[:, :, :-4])
    result = result + near_weight * (jnp.roll(grid_field, 1, -1) + jnp.roll(grid_field, -1, -1))
    result = result + far_weight * (jnp.roll(grid_field, 2, -1) + jnp.roll(grid_field, -2, -1))
    zpadded = jnp.pad(grid_field, ((0, 0), (0, 0), (0, 0), (2, 2), (0, 0)))
    result = result + near_weight * (zpadded[:, :, :, 3:-1] + zpadded[:, :, :, 1:-3])
    result = result + far_weight * (zpadded[:, :, :, 4:] + zpadded[:, :, :, :-4])
    return result


def hamiltonian(grid_field, potential, energies):
    return (
        -0.5 * laplace_local(grid_field)
        + potential * grid_field
        - energies[None, :, None, None, None] * grid_field
    )


def project(rhs_field, locked_flat):
    columns = rhs_field.shape[0] * rhs_field.shape[1]
    flattened = rhs_field.reshape(columns, -1)
    rounded = flattened.astype(jnp.bfloat16)
    block_rows = locked_flat.shape[0] // block_count
    removed = jnp.zeros(flattened.shape, jnp.float32)
    for block_index in range(block_count):
        locked_block = locked_flat[block_index * block_rows : (block_index + 1) * block_rows]
        partial_margin = lax.dot_general(
            locked_block, rounded, (((1,), (1,)), ((), ())), preferred_element_type=jnp.float32
        )
        margin_b = lax.psum(partial_margin.astype(jnp.bfloat16), "dom")
        removed = removed + lax.dot_general(
            margin_b, locked_block, (((0,), (0,)), ((), ())), preferred_element_type=jnp.float32
        )
    return (flattened - removed).reshape(rhs_field.shape)


def local(
    response,
    occupied,
    locked_set,
    potential,
    perturbation,
    xc_kernel,
    energies,
    first_step,
    second_step,
):
    locked_flat = locked_set.reshape(locked_set.shape[0], -1)
    first_rhs = -(perturbation[:, None] * occupied[None]) - hamiltonian(
        response, potential, energies
    )
    first_res = project(first_rhs, locked_flat)
    middle = response + first_step[:, :, None, None, None] * first_res
    first_local = jnp.sum(first_res * first_res, axis=(2, 3, 4))
    first_norm = lax.psum(first_local, "dom")
    density_local = 2.0 * jnp.sum(occupied[None] * middle, axis=1)
    density = lax.psum(density_local.astype(jnp.bfloat16), "band").astype(jnp.float32)
    response_potential = perturbation - xc_kernel[None] * density
    second_rhs = -(response_potential[:, None] * occupied[None]) - hamiltonian(
        middle, potential, energies
    )
    second_res = project(second_rhs, locked_flat)
    second_local = jnp.sum(second_res * second_res, axis=(2, 3, 4))
    second_norm = lax.psum(second_local, "dom")
    fletcher_ratio = second_norm / first_norm
    direction = second_res + fletcher_ratio[:, :, None, None, None] * first_res
    new_response = middle + second_step[:, :, None, None, None] * direction
    return (new_response, response_potential)


def solution(mesh):
    placed = (
        P(None, "band", "dom", None, None),
        P("band", "dom", None, None),
        P(None, "dom", None, None),
        P("dom", None, None),
        P(None, "dom", None, None),
        P("dom", None, None),
        P("band"),
        P(None, "band"),
        P(None, "band"),
    )
    return jax.shard_map(
        local,
        mesh=mesh,
        in_specs=placed,
        out_specs=(P(None, "band", "dom", None, None), P(None, "dom", None, None)),
        check_vma=False,
    )
```

profile of v0, /device:TPU:0, one launch (start us, length us, event | category | flops | bytes accessed | tf_op | source)
XLA Modules:
  0.0 426.8 jit_solution(712102161685229960)
XLA Ops:
  7.2 2.9 convert_element_type.87
  11.0 2.9 collective-permute-start.1
  13.9 4.8 %fusion.165 = (f32[4,64,4,8,1]{4,3,2,1,0:T(8,128)}, f32[4,64,4,8,1]{4,3,2,1,0:T(8,128)}) fusion(f32[4,64,4,8,128]{4,3,2,1,0:T(8,128)S(1)} %copy-done.2), kind=kLoop, calls=%fused_computation.140 | loop fusion | bytes 131072 | tf_op jit(solution)/shard_map/jit(_roll_static)/slice | solution.py:31
  18.7 4.8 %fusion.166 = (f32[4,64,4,8,127]{4,3,2,1,0:T(8,128)}, f32[4,64,4,8,127]{4,3,2,1,0:T(8,128)}) fusion(f32[4,64,4,8,128]{4,3,2,1,0:T(8,128)S(1)} %copy-done.2), kind=kLoop, calls=%fused_computation.141 | loop fusion | bytes 16646144 | tf_op jit(solution)/shard_map/jit(_roll_static)/slice | solution.py:31
  23.4 22.7 %fusion.160 = (bf16[1024,4,8,128]{3,2,1,0:T(8,128)(2,1)}, bf16[1024,4,8,128]{3,2,1,0:T(8,128)(2,1)}, bf16[1024,4,8,128]{3,2,1,0:T(8,128)(2,1)}, bf16[1024,4,8,128]{3,2,1,0:T(8,128)(2,1)}) fusion(bf16[4096,4,8,128]{3,2,1,0:T(8,128)(2,1)} %param.11), kind=kLoop, calls=%fused_computation.135 | loop fusion | bytes 67108864 | tf_op jit(solution)/shard_map/slice | solution.py:54
  46.1 4.9 %fusion.167 = (f32[4,64,4,8,2]{4,3,2,1,0:T(8,128)}, f32[4,64,4,8,2]{4,3,2,1,0:T(8,128)}) fusion(f32[4,64,4,8,128]{4,3,2,1,0:T(8,128)S(1)} %copy-done.2), kind=kLoop, calls=%fused_computation.142 | loop fusion | bytes 262144 | tf_op jit(solution)/shard_map/jit(_roll_static)/slice | solution.py:32
  51.0 4.8 %fusion.168 = (f32[4,64,4,8,126]{4,3,2,1,0:T(8,128)}, f32[4,64,4,8,126]{4,3,2,1,0:T(8,128)}) fusion(f32[4,64,4,8,128]{4,3,2,1,0:T(8,128)S(1)} %copy-done.2), kind=kLoop, calls=%fused_computation.143 | loop fusion | bytes 16515072 | tf_op jit(solution)/shard_map/jit(_roll_static)/slice | solution.py:32
  55.8 0.6 maximum_convert_fusion
  56.4 0.6 copy-done.7
  57.0 15.2 %fusion.158 = (bf16[4,64,4,8,128]{4,3,2,1,0:T(8,128)(2,1)S(1)}, f32[4,64,4,8,128]{4,3,2,1,0:T(8,128)}) fusion(f32[4,64,4,8,128]{4,3,2,1,0:T(8,128)S(1)} %copy-done.2, f32[64]{0:T(128)S(1)} %copy-done.22, f32[4,8,128]{2,1,0:T(8,128)S(1)} %copy-done.18, f32[4,64,4,8,2]{4,3,2,1,0:T(8,128)} %get-tuple-element.35, f32[4,64,4,8,126]{4,3,2,1,0:T(8,128)} %get-tuple-element.37, ...), kind=kLoop, calls=%fused_computation.134 | loop fusion | flops 33554432 | bytes 45170944 | tf_op jit(solution)/shard_map/convert_element_type | solution.py:50
  72.1 2.5 convert_element_type.90
  74.7 9.6 %fusion.135 = bf16[1024,256]{0,1:T(8,128)(2,1)} fusion(bf16[256,4096]{1,0:T(8,128)(2,1)} %convert_element_type.90, bf16[128,8,32,128]{3,2,1,0:T(8,128)(2,1)} %bitcast.142), kind=kOutput, calls=%fused_computation.124 | convolution fusion | flops 2147745792 | bytes 11010048 | tf_op jit(solution)/shard_map/dot_general | solution.py:55
  84.3 9.1 %fusion.141 = bf16[1024,256]{0,1:T(8,128)(2,1)} fusion(bf16[256,4096]{1,0:T(8,128)(2,1)S(1)} %copy-done.8, bf16[128,8,32,128]{3,2,1,0:T(8,128)(2,1)} %bitcast.150), kind=kOutput, calls=%fused_computation.126 | convolution fusion | flops 2147745792 | bytes 11010048 | tf_op jit(solution)/shard_map/dot_general | solution.py:55
  93.3 18.5 %fusion.147 = bf16[1024,256]{0,1:T(8,128)(2,1)} fusion(bf16[256,4096]{1,0:T(8,128)(2,1)S(1)} %copy-done.8, bf16[128,8,32,128]{3,2,1,0:T(8,128)(2,1)S(1)} %bitcast.171), kind=kOutput, calls=%fused_computation.128 | convolution fusion | flops 2147745792 | bytes 11010048 | tf_op jit(solution)/shard_map/dot_general | solution.py:55
  111.8 5.4 %fusion.153 = bf16[1024,256]{0,1:T(8,128)(2,1)} fusion(bf16[256,4096]{1,0:T(8,128)(2,1)S(1)} %copy-done.8, bf16[128,8,32,128]{3,2,1,0:T(8,128)(2,1)S(1)} %bitcast.158), kind=kOutput, calls=%fused_computation.130 | convolution fusion | flops 2147745792 | bytes 11010048 | tf_op jit(solution)/shard_map/dot_general | solution.py:55
  117.3 4.9 %reshape.40 = f32[256,4096]{1,0:T(8,128)} reshape(f32[4,64,4,8,128]{4,3,2,1,0:T(8,128)} %get-tuple-element.17) | data formatting | bytes 8388608 | tf_op jit(solution)/shard_map/reshape | solution.py:49
  122.3 58.0 %all-reduce.10.cloned.1.call-done = (bf16[1024,256]{0,1:T(8,128)(2,1)}, bf16[1024,256]{0,1:T(8,128)(2,1)}, bf16[1024,256]{0,1:T(8,128)(2,1)}, bf16[1024,256]{0,1:T(8,128)(2,1)}) async-done(((bf16[1024,256]{0,1:T(8,128)(2,1)}, bf16[1024,256]{0,1:T(8,128)(2,1)}, bf16[1024,256]{0,1:T(8,128)(2,1)}, bf16[1024,256]{0,1:T(8,128)(2,1)}), (bf16[1024,256]{0,1:T(8,128)(2,1)}, bf16[1024,256]{0,1:T(8,128)(2,1)}, ...) | async-done | bytes 2097168 | tf_op jit(solution)/shard_map/psum | solution.py:58
  180.3 6.6 %fusion.20 = f32[256,4096]{1,0:T(8,128)S(1)} fusion(bf16[1024,256]{0,1:T(8,128)(2,1)} %get-tuple-element.8, bf16[128,8,32,128]{3,2,1,0:T(8,128)(2,1)} %bitcast.167), kind=kOutput, calls=%fused_computation.28 | convolution fusion | flops 2147483648 | bytes 13107200 | tf_op jit(solution)/shard_map/dot_general | solution.py:59
  186.9 6.7 %fusion.48 = f32[256,4096]{1,0:T(8,128)S(1)} fusion(f32[256,4096]{1,0:T(8,128)S(1)} %fusion.20, bf16[1024,256]{0,1:T(8,128)(2,1)S(1)} %copy-done.15, bf16[128,8,32,128]{3,2,1,0:T(8,128)(2,1)} %bitcast.154), kind=kOutput, calls=%fused_computation.56 | convolution fusion | flops 2148532224 | bytes 17301504 | tf_op jit(solution)/shard_map/dot_general | solution.py:59
  193.7 6.7 %fusion.54 = f32[256,4096]{1,0:T(8,128)S(1)} fusion(f32[256,4096]{1,0:T(8,128)S(1)} %fusion.48, bf16[1024,256]{0,1:T(8,128)(2,1)S(1)} %copy-done.14, bf16[128,8,32,128]{3,2,1,0:T(8,128)(2,1)} %bitcast.151), kind=kOutput, calls=%fused_computation.58 | convolution fusion | flops 2148532224 | bytes 17301504 | tf_op jit(solution)/shard_map/dot_general | solution.py:59
  200.5 4.4 %multiply_reduce_fusion = (f32[256]{0:T(256)S(1)}, f32[256,4096]{1,0:T(8,128)S(1)}) fusion(f32[256,4096]{1,0:T(8,128)S(1)} %copy-done.6, f32[256,4096]{1,0:T(8,128)S(1)} %fusion.54, bf16[1024,256]{0,1:T(8,128)(2,1)S(1)} %copy-done.11, bf16[128,8,32,128]{3,2,1,0:T(8,128)(2,1)S(1)} %bitcast.146), kind=kOutput, calls=%fused_computation.111 | convolution fusion | flops 2151677696 | bytes 21496832 | tf_op jit(solution)/shard_map/dot_general | solution.py:59
  204.9 0.8 copy.15
  205.7 2.6 copy-done.3
  208.3 0.8 multiply_reduce_fusion.2
  209.1 0.5 convert_element_type.101
  209.6 4.8 %fusion.161 = (f32[4,64,4,8,1]{4,3,2,1,0:T(8,128)}, f32[4,64,4,8,1]{4,3,2,1,0:T(8,128)}) fusion(f32[4,64,4,8,128]{4,3,2,1,0:T(8,128)S(1)} %get-tuple-element.15), kind=kLoop, calls=%fused_computation.136 | loop fusion | bytes 131072 | tf_op jit(solution)/shard_map/jit(_roll_static)/slice | solution.py:31
  214.4 4.9 %fusion.162 = (f32[4,64,4,8,127]{4,3,2,1,0:T(8,128)}, f32[4,64,4,8,127]{4,3,2,1,0:T(8,128)}) fusion(f32[4,64,4,8,128]{4,3,2,1,0:T(8,128)S(1)} %get-tuple-element.15), kind=kLoop, calls=%fused_computation.137 | loop fusion | bytes 16646144 | tf_op jit(solution)/shard_map/jit(_roll_static)/slice | solution.py:31
  219.3 1.7 fusion.169
  221.0 2.6 collective-permute-start.3
  223.6 19.0 %psum.81 = bf16[4,4,8,128]{3,2,1,0:T(8,128)(2,1)S(1)} all-reduce(bf16[4,4,8,128]{3,2,1,0:T(8,128)(2,1)S(1)} %multiply_convert_fusion), channel_id=1, replica_groups=mesh['band'=4,'dom'=8] {'band'}, use_global_device_ids=true, to_apply=%region_5.6 | all-reduce | flops 16384 | bytes 65536 | tf_op jit(solution)/shard_map/psum | solution.py:85
  242.7 8.1 %fusion.163 = (f32[4,64,4,8,2]{4,3,2,1,0:T(8,128)}, f32[4,64,4,8,2]{4,3,2,1,0:T(8,128)}) fusion(f32[4,64,4,8,128]{4,3,2,1,0:T(8,128)} %copy-done), kind=kLoop, calls=%fused_computation.138 | loop fusion | bytes 262144 | tf_op jit(solution)/shard_map/jit(_roll_static)/slice | solution.py:32
  250.8 4.8 %fusion.164 = (f32[4,64,4,8,126]{4,3,2,1,0:T(8,128)}, f32[4,64,4,8,126]{4,3,2,1,0:T(8,128)}) fusion(f32[4,64,4,8,128]{4,3,2,1,0:T(8,128)S(1)} %copy-done.1), kind=kLoop, calls=%fused_computation.139 | loop fusion | bytes 16515072 | tf_op jit(solution)/shard_map/jit(_roll_static)/slice | solution.py:32
  255.6 1.9 maximum_convert_fusion.1
  257.5 15.1 %fusion.156 = (bf16[4,64,4,8,128]{4,3,2,1,0:T(8,128)(2,1)S(1)}, f32[4,64,4,8,128]{4,3,2,1,0:T(8,128)}) fusion(f32[4,64,4,8,128]{4,3,2,1,0:T(8,128)S(1)} %copy-done.1, f32[64]{0:T(128)S(1)} %copy-done.22, f32[4,8,128]{2,1,0:T(8,128)S(1)} %copy-done.18, f32[4,64,4,8,2]{4,3,2,1,0:T(8,128)} %get-tuple-element.27, f32[4,64,4,8,126]{4,3,2,1,0:T(8,128)} %get-tuple-element.29, ...), kind=kLoop, calls=%fused_computation.133 | loop fusion | flops 33554432 | bytes 45170944 | tf_op jit(solution)/shard_map/convert_element_type | solution.py:50
  272.7 2.4 convert_element_type.104
  275.1 9.6 %fusion.132 = bf16[1024,256]{0,1:T(8,128)(2,1)} fusion(bf16[256,4096]{1,0:T(8,128)(2,1)} %convert_element_type.104, bf16[128,8,32,128]{3,2,1,0:T(8,128)(2,1)} %bitcast.143), kind=kOutput, calls=%fused_computation.123 | convolution fusion | flops 2147745792 | bytes 11010048 | tf_op jit(solution)/shard_map/dot_general | solution.py:55
  284.7 9.0 %fusion.138 = bf16[1024,256]{0,1:T(8,128)(2,1)} fusion(bf16[256,4096]{1,0:T(8,128)(2,1)S(1)} %copy-done.9, bf16[128,8,32,128]{3,2,1,0:T(8,128)(2,1)} %bitcast.152), kind=kOutput, calls=%fused_computation.125 | convolution fusion | flops 2147745792 | bytes 11010048 | tf_op jit(solution)/shard_map/dot_general | solution.py:55
  293.8 5.7 %fusion.150 = bf16[1024,256]{0,1:T(8,128)(2,1)} fusion(bf16[256,4096]{1,0:T(8,128)(2,1)S(1)} %copy-done.9, bf16[128,8,32,128]{3,2,1,0:T(8,128)(2,1)S(1)} %bitcast.161), kind=kOutput, calls=%fused_computation.129 | convolution fusion | flops 2147745792 | bytes 11010048 | tf_op jit(solution)/shard_map/dot_general | solution.py:55
  299.4 5.4 %fusion.144 = bf16[1024,256]{0,1:T(8,128)(2,1)} fusion(bf16[256,4096]{1,0:T(8,128)(2,1)S(1)} %copy-done.9, bf16[128,8,32,128]{3,2,1,0:T(8,128)(2,1)S(1)} %bitcast.174), kind=kOutput, calls=%fused_computation.127 | convolution fusion | flops 2147745792 | bytes 11010048 | tf_op jit(solution)/shard_map/dot_general | solution.py:55
  305.0 5.3 %reshape.42 = f32[256,4096]{1,0:T(8,128)} reshape(f32[4,64,4,8,128]{4,3,2,1,0:T(8,128)} %get-tuple-element.13) | data formatting | bytes 8388608 | tf_op jit(solution)/shard_map/reshape | solution.py:49
  310.2 53.0 %all-reduce.8.cloned.1.call-done = (bf16[1024,256]{0,1:T(8,128)(2,1)}, bf16[1024,256]{0,1:T(8,128)(2,1)}, bf16[1024,256]{0,1:T(8,128)(2,1)}, bf16[1024,256]{0,1:T(8,128)(2,1)}) async-done(((bf16[1024,256]{0,1:T(8,128)(2,1)}, bf16[1024,256]{0,1:T(8,128)(2,1)}, bf16[1024,256]{0,1:T(8,128)(2,1)}, bf16[1024,256]{0,1:T(8,128)(2,1)}), (bf16[1024,256]{0,1:T(8,128)(2,1)}, bf16[1024,256]{0,1:T(8,128)(2,1)}, ...) | async-done | bytes 2097168 | tf_op jit(solution)/shard_map/psum | solution.py:58
  363.2 6.6 %fusion.16 = f32[256,4096]{1,0:T(8,128)S(1)} fusion(bf16[1024,256]{0,1:T(8,128)(2,1)} %get-tuple-element.4, bf16[128,8,32,128]{3,2,1,0:T(8,128)(2,1)} %bitcast.168), kind=kOutput, calls=%fused_computation.24 | convolution fusion | flops 2147483648 | bytes 13107200 | tf_op jit(solution)/shard_map/dot_general | solution.py:59
  369.8 6.7 %fusion.51 = f32[256,4096]{1,0:T(8,128)S(1)} fusion(f32[256,4096]{1,0:T(8,128)S(1)} %fusion.16, bf16[1024,256]{0,1:T(8,128)(2,1)S(1)} %copy-done.13, bf16[128,8,32,128]{3,2,1,0:T(8,128)(2,1)} %bitcast.155), kind=kOutput, calls=%fused_computation.57 | convolution fusion | flops 2148532224 | bytes 17301504 | tf_op jit(solution)/shard_map/dot_general | solution.py:59
  376.6 6.7 %fusion.57 = f32[256,4096]{1,0:T(8,128)S(1)} fusion(f32[256,4096]{1,0:T(8,128)S(1)} %fusion.51, bf16[1024,256]{0,1:T(8,128)(2,1)S(1)} %copy-done.12, bf16[128,8,32,128]{3,2,1,0:T(8,128)(2,1)} %bitcast.153), kind=kOutput, calls=%fused_computation.59 | convolution fusion | flops 2148532224 | bytes 17301504 | tf_op jit(solution)/shard_map/dot_general | solution.py:59
  383.4 12.1 %multiply_reduce_fusion.1 = (f32[256]{0:T(256)S(1)}, f32[256,4096]{1,0:T(8,128)}) fusion(f32[256,4096]{1,0:T(8,128)S(1)} %copy-done.5, f32[256,4096]{1,0:T(8,128)S(1)} %fusion.57, bf16[1024,256]{0,1:T(8,128)(2,1)S(1)} %copy-done.10, bf16[128,8,32,128]{3,2,1,0:T(8,128)(2,1)S(1)} %bitcast.149), kind=kOutput, calls=%fused_computation.112 | convolution fusion | flops 2151677696 | bytes 21496832 | tf_op jit(solution)/shard_map/dot_general | solution.py:59
  395.5 4.9 %copy.16 = f32[32,8,32,128]{3,2,1,0:T(8,128)} copy(f32[32,8,32,128]{3,1,2,0:T(8,128)} %bitcast.165) | data formatting | bytes 8388608
  400.5 11.9 %all-reduce.2 = (f32[4,64]{1,0:T(4,128)S(1)}, f32[4,64]{1,0:T(4,128)S(1)}) all-reduce(f32[4,64]{1,0:T(4,128)S(1)} %reduce_sum.33, f32[4,64]{1,0:T(4,128)S(1)} %reduce_sum.35), channel_id=1, replica_groups=mesh['band'=4,'dom'=8] {'dom'}, use_global_device_ids=true, to_apply=%region_11.12 | all-reduce | flops 512 | bytes 4096 | tf_op jit(solution)/shard_map/psum | solution.py:92
  412.4 7.1 %multiply_add_fusion = f32[4,64,4,8,128]{4,3,2,1,0:T(8,128)} fusion(f32[4,64,4,8,128]{4,3,2,1,0:T(8,128)} %copy-done, f32[4,64,4,8,128]{4,3,2,1,0:T(8,128)} %bitcast.164, f32[4,64,4,8,128]{4,3,2,1,0:T(8,128)} %bitcast.163, f32[4,64]{1,0:T(4,128)S(1)} %div.3, f32[4,64]{1,0:T(4,128)S(1)} %copy-done.21), kind=kLoop, calls=%fused_computation.110 | loop fusion | flops 4194304 | bytes 16779264 | tf_op jit(solution)/shard_map/add | solution.py:95
  (90 shorter events, 1.4 us)
Async XLA Ops:
  7.2 173.1 %all-reduce.10.cloned.1.call-start = ((), (), s32[]{:S(2)}) async-start(), calls=%async_computation.1 | async-start | bytes 4194304 | tf_op jit(solution)/shard_map/psum | solution.py:58
  7.2 6.7 %copy-start.2 = (f32[4,64,4,8,128]{4,3,2,1,0:T(8,128)S(1)}, f32[4,64,4,8,128]{4,3,2,1,0:T(8,128)}, u32[]{:S(2)}) copy-start(f32[4,64,4,8,128]{4,3,2,1,0:T(8,128)} %param.9) | copy-start | bytes 12582916
  10.5 45.3 %collective-permute-start = (bf16[4,64,2,8,128]{4,3,2,1,0:T(8,128)(2,1)S(1)}, bf16[4,64,2,8,128]{4,3,2,1,0:T(8,128)(2,1)S(1)}, u32[]{:S(2)}, u32[]{:S(2)}) collective-permute-start(bf16[4,64,2,8,128]{4,3,2,1,0:T(8,128)(2,1)S(1)} %get-tuple-element.40), channel_id=1, source_target_pairs={{0,1},{1,2},{2,3},{3,4},{4,5},{5,6},{6,7},{7,0},{8,9},{9,10},{10,1... | collective-permute-start | bytes 3145736 | tf_op jit(solution)/shard_map/ppermute | solution.py:18
  11.0 44.8 %collective-permute-start.1 = (bf16[4,64,2,8,128]{4,3,2,1,0:T(8,128)(2,1)S(1)}, bf16[4,64,2,8,128]{4,3,2,1,0:T(8,128)(2,1)S(1)}, u32[]{:S(2)}, u32[]{:S(2)}) collective-permute-start(bf16[4,64,2,8,128]{4,3,2,1,0:T(8,128)(2,1)S(1)} %get-tuple-element.41), channel_id=1, source_target_pairs={{1,0},{2,1},{3,2},{4,3},{5,4},{6,5},{7,6},{0,7},{9,8},{10,9},{11,1... | collective-permute-start | bytes 3145736 | tf_op jit(solution)/shard_map/ppermute | solution.py:21
  55.7 1.2 copy-start.7
  55.7 1.2 copy-start.16
  55.7 1.2 copy-start.18
  55.7 1.2 copy-start.22
  74.6 9.6 %copy-start.8 = (bf16[256,4096]{1,0:T(8,128)(2,1)S(1)}, bf16[256,4096]{1,0:T(8,128)(2,1)}, u32[]{:S(2)}) copy-start(bf16[256,4096]{1,0:T(8,128)(2,1)} %convert_element_type.90) | copy-start | bytes 6291460
  74.7 18.7 %slice-start.8 = ((s8[8388608]{0:T(1024)(128)(4,1)}), s8[4194304]{0:T(1024)(128)(4,1)S(1)}, s32[]{:S(2)}) async-start(s8[8388608]{0:T(1024)(128)(4,1)} %bitcast.169), calls=%async_computation.10 | async-start | bytes 8388608
  84.3 9.1 %slice-start.9 = ((s8[8388608]{0:T(1024)(128)(4,1)}), s8[4194304]{0:T(1024)(128)(4,1)S(1)}, s32[]{:S(2)}) async-start(s8[8388608]{0:T(1024)(128)(4,1)} %bitcast.169), calls=%async_computation.11 | async-start | bytes 8388608
  84.3 27.5 %slice-start.4 = ((s8[8388608]{0:T(1024)(128)(4,1)}), s8[4194304]{0:T(1024)(128)(4,1)S(1)}, s32[]{:S(2)}) async-start(s8[8388608]{0:T(1024)(128)(4,1)} %bitcast.156), calls=%async_computation.6 | async-start | bytes 8388608
  93.3 18.5 %slice-start.5 = ((s8[8388608]{0:T(1024)(128)(4,1)}), s8[4194304]{0:T(1024)(128)(4,1)S(1)}, s32[]{:S(2)}) async-start(s8[8388608]{0:T(1024)(128)(4,1)} %bitcast.156), calls=%async_computation.7 | async-start | bytes 8388608
  117.3 245.9 %all-reduce.8.cloned.1.call-start = ((), (), s32[]{:S(2)}) async-start(), calls=%async_computation | async-start | bytes 4194304 | tf_op jit(solution)/shard_map/psum | solution.py:58
  180.3 6.6 %copy-start.15 = (bf16[1024,256]{0,1:T(8,128)(2,1)S(1)}, bf16[1024,256]{0,1:T(8,128)(2,1)}, u32[]{:S(2)}) copy-start(bf16[1024,256]{0,1:T(8,128)(2,1)} %get-tuple-element.9) | copy-start | bytes 1572868
  186.9 6.8 %copy-start.14 = (bf16[1024,256]{0,1:T(8,128)(2,1)S(1)}, bf16[1024,256]{0,1:T(8,128)(2,1)}, u32[]{:S(2)}) copy-start(bf16[1024,256]{0,1:T(8,128)(2,1)} %get-tuple-element.10) | copy-start | bytes 1572868
  186.9 13.5 %slice-start = ((s8[8388608]{0:T(1024)(128)(4,1)}), s8[4194304]{0:T(1024)(128)(4,1)S(1)}, s32[]{:S(2)}) async-start(s8[8388608]{0:T(1024)(128)(4,1)} %bitcast.144), calls=%async_computation.2 | async-start | bytes 8388608
  193.7 6.8 %slice-start.1 = ((s8[8388608]{0:T(1024)(128)(4,1)}), s8[4194304]{0:T(1024)(128)(4,1)S(1)}, s32[]{:S(2)}) async-start(s8[8388608]{0:T(1024)(128)(4,1)} %bitcast.144), calls=%async_computation.3 | async-start | bytes 8388608
  193.7 6.8 %copy-start.6 = (f32[256,4096]{1,0:T(8,128)S(1)}, f32[256,4096]{1,0:T(8,128)}, u32[]{:S(2)}) copy-start(f32[256,4096]{1,0:T(8,128)} %reshape.40) | copy-start | bytes 12582916
  193.7 6.8 %copy-start.11 = (bf16[1024,256]{0,1:T(8,128)(2,1)S(1)}, bf16[1024,256]{0,1:T(8,128)(2,1)}, u32[]{:S(2)}) copy-start(bf16[1024,256]{0,1:T(8,128)(2,1)} %get-tuple-element.11) | copy-start | bytes 1572868
  204.9 3.4 copy-start.3
  204.9 3.3 copy-start.20
  205.7 3.4 copy-start.4
  209.1 5.3 %copy-start = (f32[4,64,4,8,128]{4,3,2,1,0:T(8,128)}, f32[4,64,4,8,128]{4,3,2,1,0:T(8,128)S(1)}, u32[]{:S(2)}) copy-start(f32[4,64,4,8,128]{4,3,2,1,0:T(8,128)S(1)} %get-tuple-element.15) | copy-start | bytes 12582916
  219.3 23.4 %copy-start.19 = (f32[4,8,128]{2,1,0:T(8,128)S(1)}, f32[4,8,128]{2,1,0:T(8,128)}, u32[]{:S(2)}) copy-start(f32[4,8,128]{2,1,0:T(8,128)} %param.14) | copy-start | bytes 49156
  221.0 34.6 %collective-permute-start.2 = (bf16[4,64,2,8,128]{4,3,2,1,0:T(8,128)(2,1)}, bf16[4,64,2,8,128]{4,3,2,1,0:T(8,128)(2,1)}, u32[]{:S(2)}, u32[]{:S(2)}) collective-permute-start(bf16[4,64,2,8,128]{4,3,2,1,0:T(8,128)(2,1)} %get-tuple-element.38), channel_id=1, source_target_pairs={{0,1},{1,2},{2,3},{3,4},{4,5},{5,6},{6,7},{7,0},{8,9},{9,10},{10,1... | collective-permute-start | bytes 3145736 | tf_op jit(solution)/shard_map/ppermute | solution.py:18
  221.0 34.6 %collective-permute-start.3 = (bf16[4,64,2,8,128]{4,3,2,1,0:T(8,128)(2,1)}, bf16[4,64,2,8,128]{4,3,2,1,0:T(8,128)(2,1)}, u32[]{:S(2)}, u32[]{:S(2)}) collective-permute-start(bf16[4,64,2,8,128]{4,3,2,1,0:T(8,128)(2,1)} %get-tuple-element.39), channel_id=1, source_target_pairs={{1,0},{2,1},{3,2},{4,3},{5,4},{6,5},{7,6},{0,7},{9,8},{10,9},{11,1... | collective-permute-start | bytes 3145736 | tf_op jit(solution)/shard_map/ppermute | solution.py:21
  242.7 14.8 %copy-start.17 = (f32[4,4,8,128]{3,2,1,0:T(8,128)}, f32[4,4,8,128]{3,2,1,0:T(8,128)S(1)}, u32[]{:S(2)}) copy-start(f32[4,4,8,128]{3,2,1,0:T(8,128)S(1)} %multiply_subtract_fusion) | copy-start | bytes 196612
  242.7 8.1 %copy-start.1 = (f32[4,64,4,8,128]{4,3,2,1,0:T(8,128)S(1)}, f32[4,64,4,8,128]{4,3,2,1,0:T(8,128)}, u32[]{:S(2)}) copy-start(f32[4,64,4,8,128]{4,3,2,1,0:T(8,128)} %copy-done) | copy-start | bytes 12582916
  275.1 9.6 %copy-start.9 = (bf16[256,4096]{1,0:T(8,128)(2,1)S(1)}, bf16[256,4096]{1,0:T(8,128)(2,1)}, u32[]{:S(2)}) copy-start(bf16[256,4096]{1,0:T(8,128)(2,1)} %convert_element_type.104) | copy-start | bytes 6291460
  275.1 18.7 %slice-start.6 = ((s8[8388608]{0:T(1024)(128)(4,1)}), s8[4194304]{0:T(1024)(128)(4,1)S(1)}, s32[]{:S(2)}) async-start(s8[8388608]{0:T(1024)(128)(4,1)} %bitcast.159), calls=%async_computation.8 | async-start | bytes 8388608
  284.7 9.0 %slice-start.7 = ((s8[8388608]{0:T(1024)(128)(4,1)}), s8[4194304]{0:T(1024)(128)(4,1)S(1)}, s32[]{:S(2)}) async-start(s8[8388608]{0:T(1024)(128)(4,1)} %bitcast.159), calls=%async_computation.9 | async-start | bytes 8388608
  284.7 14.7 %slice-start.10 = ((s8[8388608]{0:T(1024)(128)(4,1)}), s8[4194304]{0:T(1024)(128)(4,1)S(1)}, s32[]{:S(2)}) async-start(s8[8388608]{0:T(1024)(128)(4,1)} %bitcast.172), calls=%async_computation.12 | async-start | bytes 8388608
  293.8 5.7 %slice-start.11 = ((s8[8388608]{0:T(1024)(128)(4,1)}), s8[4194304]{0:T(1024)(128)(4,1)S(1)}, s32[]{:S(2)}) async-start(s8[8388608]{0:T(1024)(128)(4,1)} %bitcast.172), calls=%async_computation.13 | async-start | bytes 8388608
  363.2 6.6 %copy-start.13 = (bf16[1024,256]{0,1:T(8,128)(2,1)S(1)}, bf16[1024,256]{0,1:T(8,128)(2,1)}, u32[]{:S(2)}) copy-start(bf16[1024,256]{0,1:T(8,128)(2,1)} %get-tuple-element.5) | copy-start | bytes 1572868
  369.8 6.8 %copy-start.12 = (bf16[1024,256]{0,1:T(8,128)(2,1)S(1)}, bf16[1024,256]{0,1:T(8,128)(2,1)}, u32[]{:S(2)}) copy-start(bf16[1024,256]{0,1:T(8,128)(2,1)} %get-tuple-element.6) | copy-start | bytes 1572868
  369.8 13.5 %slice-start.2 = ((s8[8388608]{0:T(1024)(128)(4,1)}), s8[4194304]{0:T(1024)(128)(4,1)S(1)}, s32[]{:S(2)}) async-start(s8[8388608]{0:T(1024)(128)(4,1)} %bitcast.147), calls=%async_computation.4 | async-start | bytes 8388608
  376.6 6.8 %slice-start.3 = ((s8[8388608]{0:T(1024)(128)(4,1)}), s8[4194304]{0:T(1024)(128)(4,1)S(1)}, s32[]{:S(2)}) async-start(s8[8388608]{0:T(1024)(128)(4,1)} %bitcast.147), calls=%async_computation.5 | async-start | bytes 8388608
  376.6 6.8 %copy-start.5 = (f32[256,4096]{1,0:T(8,128)S(1)}, f32[256,4096]{1,0:T(8,128)}, u32[]{:S(2)}) copy-start(f32[256,4096]{1,0:T(8,128)} %reshape.42) | copy-start | bytes 12582916
  376.6 6.8 %copy-start.10 = (bf16[1024,256]{0,1:T(8,128)(2,1)S(1)}, bf16[1024,256]{0,1:T(8,128)(2,1)}, u32[]{:S(2)}) copy-start(bf16[1024,256]{0,1:T(8,128)(2,1)} %get-tuple-element.7) | copy-start | bytes 1572868
  395.5 16.8 %copy-start.21 = (f32[4,64]{1,0:T(4,128)S(1)}, f32[4,64]{1,0:T(4,128)}, u32[]{:S(2)}) copy-start(f32[4,64]{1,0:T(4,128)} %param.17) | copy-start | bytes 3076
Sparse Core Ops, SparseCore 0:
  117.4 62.8 all-reduce.9
  305.0 58.1 all-reduce.7
where the time goes:
time: 435 us; the launch traced here: 427 us
  matrix products  129 us (30%)
  waiting for transfers between devices  111 us (26%)
  local copies, waits for them, and re-layouts  90.7 us (21%)
  other arithmetic  44.2 us (10%)
  blocking collectives  30.9 us (7%)
  between operations  15 us (3%)
  starting transfers between devices  6.17 us (1%)
    psum x2, waiting for transfers between devices, project(): margin_b = lax.psum(partial_margin.astype(jnp.bfloat16), 'dom')  111 us
    dot_general x8, matrix products, project(): lax.dot_general(locked_block, rounded, (((1,), (1,)), ((), ())), preferre...  72.3 us
    dot_general x8, matrix products, project(): lax.dot_general(margin_b, locked_block, (((0,), (0,)), ((), ())), preferr...  56.6 us
    convert_element_type x2, other arithmetic, project(): rounded = flattened.astype(jnp.bfloat16)  30.3 us
    slice x1, local copies, waits for them, and re-layouts, project(): locked_flat[block_index * block_rows:(block_index + 1) * block_rows]  22.7 us
    slice x4, local copies, waits for them, and re-layouts, laplace_local(): jnp.roll(grid_field, 2, -1) + jnp.roll(grid_field, -2, -1)  22.5 us
    slice x4, local copies, waits for them, and re-layouts, laplace_local(): jnp.roll(grid_field, 1, -1) + jnp.roll(grid_field, -1, -1)  19.2 us
    psum x1, blocking collectives, local(): lax.psum(density_local.astype(jnp.bfloat16), 'band').astype(jnp.float32)  19 us
  transfers between devices with their start and end apart: 6, of which 2 were waited for; matrix products, arithmetic and copies ran while one was open for 15% of the time, Pallas kernels for 0%

commit v1 on v0

v1 whole, which is shorter than its diff:
```python
import jax
import jax.numpy as jnp
from jax import lax
from jax.experimental import pallas as pl
from jax.experimental.pallas import tpu as pltpu
from jax.sharding import PartitionSpec as P

f32 = jnp.float32
bf16 = jnp.bfloat16
near_half = 2.0 / 3.0
far_half = -1.0 / 24.0
centre_half = -3.75
halo_parts = 1
MIB = 1 << 20


def onchip(array):
    return pltpu.with_memory_space_constraint(array, pltpu.VMEM)


def run(body, args, outs, scratch=(), aliases=None, limit=8, name=None):
    kinds = {"v": pltpu.VMEM, "s": pltpu.SMEM, "a": pl.ANY}
    results = pl.pallas_call(
        body,
        in_specs=[pl.BlockSpec(memory_space=kinds[kind]) for _, kind in args],
        out_specs=[pl.BlockSpec(memory_space=pltpu.VMEM) for _ in outs],
        out_shape=[
            pltpu.VMEM(shape, dtype) if kept and name == "relay" else jax.ShapeDtypeStruct(shape, dtype)
            for shape, dtype, kept in outs
        ],
        scratch_shapes=list(scratch),
        input_output_aliases=aliases or {},
        compiler_params=pltpu.CompilerParams(vmem_limit_bytes=limit * MIB),
        name=name,
    )(*[array for array, _ in args])
    return [onchip(r) if kept and name == "relay" else r for r, (_, _, kept) in zip(results, outs)]


def tree_sum(terms):
    while len(terms) > 1:
        terms = [terms[i] + terms[i + 1] for i in range(0, len(terms), 2)]
    return terms[0]


def per_row(scalars, row, width):
    line = scalars[row : row + 1, :]
    return jnp.broadcast_to(line, (width, line.shape[1])).T


def dot_nt(a, b):
    return lax.dot_general(a, b, (((1,), (1,)), ((), ())), preferred_element_type=f32)


def dot_nn(a, b):
    return lax.dot_general(a, b, (((1,), (0,)), ((), ())), preferred_element_type=f32)


def local(
    response,
    occupied,
    locked_set,
    potential,
    perturbation,
    xc_kernel,
    energies,
    first_step,
    second_step,
):
    perts, orbs, planes, gz, gy = response.shape
    locked = locked_set.shape[0]
    columns = perts * orbs
    cells = planes * gz * gy
    stripe = planes * gy
    doms = lax.axis_size("dom")
    bands = lax.axis_size("band")
    chips = doms // 2
    half = locked // 2
    piece = half // chips
    part_z = gz // halo_parts
    part_cells = part_z * stripe
    part_edge = part_z * 2 * gy
    position = lax.axis_index("dom")
    where = jnp.stack([position & 1, position >> 1])

    def col(z, x):
        return (z * planes + x) * gy

    def edge(z, k):
        return (z * 2 + k) * gy

    def swap(array, mask, axis):
        count = lax.axis_size(axis)
        return lax.ppermute(array, axis, [(i, i ^ mask) for i in range(count)])

    ahead = [(i, (i + 1) % doms) for i in range(doms)]
    behind = [((i + 1) % doms, i) for i in range(doms)]

    scalars = jnp.stack(
        [jnp.tile(energies, perts), first_step.reshape(columns), second_step.reshape(columns)]
    )

    def flatten_body(source, early, placed, flat, *edges):
        def rows_step(p, carry):
            rows = pl.ds(pl.multiple_of(p * orbs, orbs), orbs)
            for x in range(planes):
                wide = source[rows, x].reshape(orbs, gz * gy)
                for z in range(gz):
                    value = wide[:, z * gy : (z + 1) * gy]
                    flat[rows, col(z, x) : col(z, x) + gy] = value
                    part, inner = divmod(z, part_z)
                    if x < 2:
                        at = edge(inner, x)
                        edges[2 * part][rows, at : at + gy] = value.astype(bf16)
                    if x >= planes - 2:
                        at = edge(inner, x - planes + 2)
                        edges[2 * part + 1][rows, at : at + gy] = value.astype(bf16)
            return carry

        lax.fori_loop(0, source.shape[0] // orbs, rows_step, 0)

    flat_response, *edges1 = run(
        flatten_body,
        [(response.reshape(columns, planes, gz, gy), "v"), (scalars, "a"), (where, "a")],
        [((columns, cells), f32, True)]
        + [((columns, part_edge), bf16, False)] * (2 * halo_parts),
        limit=8,
        name="flatten",
    )

    def halos_of(edges):
        received = []
        for part in range(halo_parts):
            low = lax.ppermute(edges[2 * part + 1], "dom", ahead)
            high = lax.ppermute(edges[2 * part], "dom", behind)
            received.append((low, high))
        return received

    halos1 = halos_of(edges1)


    def setup_body(occ, pot, pert, xc, occ_flat, pot_flat, pert_flat, xc_flat):
        for x in range(planes):
            wide = occ[:, x].reshape(orbs, gz * gy)
            for z in range(gz):
                cut = slice(col(z, x), col(z, x) + gy)
                occ_flat[:, cut] = wide[:, z * gy : (z + 1) * gy]
                pot_flat[0:1, cut] = pot[x, z : z + 1, :]
                xc_flat[0:1, cut] = xc[x, z : z + 1, :]
                for p in range(perts):
                    pert_flat[p, 0:1, cut] = pert[p, x, z : z + 1, :]

    flat_occupied, flat_potential, flat_perturbation, flat_xc = run(
        setup_body,
        [(occupied, "v"), (potential, "v"), (perturbation, "v"), (xc_kernel, "v")],
        [
            ((orbs, cells), f32, True),
            ((1, cells), f32, True),
            ((perts, 1, cells), f32, True),
            ((1, cells), f32, True),
        ],
        limit=2,
        name="setup",
    )

    chunk = min(256, locked)
    chunks = locked // chunk

    def relay_body(source, target, held, sems):
        def copy(i):
            slot = lax.rem(i, 3)
            rows = pl.ds(pl.multiple_of(i * chunk, chunk), chunk)
            return pltpu.make_async_copy(source.at[rows], held.at[slot], sems.at[slot])

        copy(0).start()
        copy(1).start()

        def step(i, carry):
            @pl.when(i + 2 < chunks)
            def _():
                copy(i + 2).start()

            copy(i).wait()
            slot = lax.rem(i, 3)
            rows = pl.ds(pl.multiple_of(i * chunk, chunk), chunk)
            for x in range(planes):
                wide = held[slot, :, x].reshape(chunk, gz * gy)
                for z in range(gz):
                    target[rows, col(z, x) : col(z, x) + gy] = wide[:, z * gy : (z + 1) * gy]
            return carry

        lax.fori_loop(0, chunks, step, 0)

    (locked_flat,) = run(
        relay_body,
        [(locked_set, "a")],
        [((locked, cells), bf16, True)],
        scratch=[
            pltpu.VMEM((3, chunk, planes, gz, gy), bf16),
            pltpu.SemaphoreType.DMA((3,)),
        ],
        limit=7,
        name="relay",
    )

    def stencil_body(field, pot, scal, out, energy):
        energy[...] = per_row(scal, 0, gy)
        block = 32

        def rows_step(i, carry):
            rows = pl.ds(pl.multiple_of(i * block, block), block)
            base = energy[rows, :] + centre_half

            def at(z, x):
                return field[rows, col(z, x) : col(z, x) + gy]

            for z in range(gz):
                for x in range(planes):
                    here = at(z, x)
                    near = pltpu.roll(here, 1, 1) + pltpu.roll(here, gy - 1, 1)
                    far = pltpu.roll(here, 2, 1) + pltpu.roll(here, gy - 2, 1)
                    for d in (-1, 1):
                        if 0 <= x + d < planes:
                            near = near + at(z, x + d)
                        if 0 <= z + d < gz:
                            near = near + at(z + d, x)
                        if 0 <= x + 2 * d < planes:
                            far = far + at(z, x + 2 * d)
                        if 0 <= z + 2 * d < gz:
                            far = far + at(z + 2 * d, x)
                    own = base - pot[0:1, col(z, x) : col(z, x) + gy]
                    out[rows, col(z, x) : col(z, x) + gy] = (
                        own * here + near_half * near + far_half * far
                    )
            return carry

        lax.fori_loop(0, columns // block, rows_step, 0)

    def stencil(field):
        (out,) = run(
            stencil_body,
            [(field, "v"), (flat_potential, "v"), (scalars, "v")],
            [((columns, cells), f32, True)],
            scratch=[pltpu.VMEM((columns, gy), f32)],
            limit=1,
            name="stencil",
        )
        return out

    def finish_rhs(part, partial, low, high, occ, pot, rhs, rounded):
        first = part * part_z

        def rows_step(p, carry):
            rows = pl.ds(pl.multiple_of(p * orbs, orbs), orbs)
            for inner in range(part_z):
                for x in range(planes):
                    at = col(first + inner, x)
                    value = partial[rows, at : at + gy] - pot[p, 0:1, at : at + gy] * occ[
                        :, at : at + gy
                    ]

                    def halo(ref, k):
                        start = edge(inner, k)
                        return ref[rows, start : start + gy].astype(f32)

                    if x == 0:
                        value = value + (near_half * halo(low, 1) + far_half * halo(low, 0))
                    if x == 1:
                        value = value + far_half * halo(low, 1)
                    if x == planes - 2:
                        value = value + far_half * halo(high, 0)
                    if x == planes - 1:
                        value = value + (near_half * halo(high, 0) + far_half * halo(high, 1))
                    rhs[rows, at : at + gy] = value
                    rounded[rows, at : at + gy] = value.astype(bf16)
            return carry

        lax.fori_loop(0, perts, rows_step, 0)

    def margins(partial, halos, pot):
        low, high = halos[0]

        def other_body(where_ref, part_ref, low_ref, high_ref, occ, pot_ref, lock, rhs, rounded, out):
            finish_rhs(0, part_ref, low_ref, high_ref, occ, pot_ref, rhs, rounded)
            start = (1 - where_ref[0]) * half
            for m in range(chips):
                rows = pl.ds(pl.multiple_of(start + (where_ref[1] ^ m) * piece, piece), piece)
                out[:, m * piece : (m + 1) * piece] = dot_nt(rounded[...], lock[rows, :]).astype(bf16)

        rhs, rounded, other = run(
            other_body,
            [
                (where, "s"),
                (partial, "v"),
                (low, "v"),
                (high, "v"),
                (flat_occupied, "v"),
                (pot, "v"),
                (locked_flat, "v"),
            ],
            [
                ((columns, cells), f32, True),
                ((columns, cells), bf16, True),
                ((columns, half), bf16, False),
            ],
            aliases={1: 0},
            limit=2,
            name="margin_other",
        )
        arrived = swap(other, 1, "dom")

        def own_body(where_ref, rounded_ref, lock, arrived_ref, kept, *sent):
            start = where_ref[0] * half
            for m in reversed(range(chips)):
                rows = pl.ds(pl.multiple_of(start + (where_ref[1] ^ m) * piece, piece), piece)
                value = dot_nt(rounded_ref[...], lock[rows, :])
                value = value + arrived_ref[:, m * piece : (m + 1) * piece].astype(f32)
                if m == 0:
                    kept[...] = value
                else:
                    sent[m - 1][...] = value.astype(bf16)

        kept, *sent = run(
            own_body,
            [(where, "s"), (rounded, "v"), (locked_flat, "v"), (arrived, "v")],
            [((columns, piece), f32, False)]
            + [((columns, piece), bf16, False)] * (chips - 1),
            limit=2,
            name="margin_own",
        )
        arrivals = [swap(sent[m - 1], 2 * m, "dom") for m in range(1, chips)]

        def add_body(*refs):
            out = refs[-1]
            out[...] = tree_sum([r[...].astype(f32) for r in refs[:-1]]).astype(bf16)

        (mine,) = run(
            add_body,
            [(kept, "v")] + [(r, "v") for r in arrivals],
            [((columns, piece), bf16, False)],
            limit=2,
            name="add_pieces",
        )
        gathered = [mine] + [swap(mine, 2 * m, "dom") for m in range(1, chips)]
        return rhs, gathered

    def collect(where_ref, pieces, held):
        for m, ref in enumerate(pieces):
            at = pl.ds(pl.multiple_of((where_ref[1] ^ m) * piece, piece), piece)
            held[:, at] = ref[...]

    def remove_own(gathered):
        def body(where_ref, *refs):
            pieces, (lock, acc, held) = refs[:chips], refs[chips:]
            collect(where_ref, pieces, held)
            rows = pl.ds(pl.multiple_of(where_ref[0] * half, half), half)

            def step(z, carry):
                at = pl.ds(pl.multiple_of(z * stripe, stripe), stripe)
                acc[:, at] = dot_nn(held[...], lock[rows, at])
                return carry

            lax.fori_loop(0, gz, step, 0)

        (acc,) = run(
            body,
            [(where, "s")] + [(g, "v") for g in gathered] + [(locked_flat, "v")],
            [((columns, cells), f32, True)],
            scratch=[pltpu.VMEM((columns, half), bf16)],
            limit=2,
            name="remove_own",
        )
        return acc

    def line_of(lanes):
        return jnp.sum(lanes.T, axis=0, keepdims=True)

    def squares(value):
        total = value[:, :gy] * value[:, :gy]
        for x in range(1, planes):
            total = total + value[:, x * gy : (x + 1) * gy] * value[:, x * gy : (x + 1) * gy]
        return total

    def first_finish(others, acc, rhs, field):
        def body(where_ref, *refs):
            pieces = refs[:chips]
            lock, acc_ref, rhs_ref, field_ref, occ, scal = refs[chips : chips + 6]
            res, mid, low, high, dens, norm = refs[chips + 6 : chips + 12]
            held, step_rows, lanes = refs[chips + 12 :]
            collect(where_ref, pieces, held)
            step_rows[...] = per_row(scal, 1, gy)
            lanes[...] = jnp.zeros_like(lanes)
            rows = pl.ds(pl.multiple_of((1 - where_ref[0]) * half, half), half)

            def step(z, carry):
                at = pl.ds(pl.multiple_of(z * stripe, stripe), stripe)
                removed = acc_ref[:, at] + dot_nn(held[...], lock[rows, at])
                value = rhs_ref[:, at] - removed
                res[:, at] = value
                lanes[...] += squares(value)
                for x in range(planes):
                    cut = slice(x * gy, (x + 1) * gy)
                    spot = pl.ds(pl.multiple_of(z * stripe + x * gy, gy), gy)
                    new = field_ref[:, spot] + step_rows[...] * value[:, cut]
                    mid[:, spot] = new
                    weight = 2.0 * occ[:, spot]
                    sums = [
                        jnp.sum(weight * new[p * orbs : (p + 1) * orbs], axis=0, keepdims=True)
                        for p in range(perts)
                    ]
                    dens[:, spot] = jnp.concatenate(sums, axis=0).astype(bf16)
                    if x < 2:
                        place = pl.ds(pl.multiple_of((z * 2 + x) * gy, gy), gy)
                        low[:, place] = new.astype(bf16)
                    if x >= planes - 2:
                        place = pl.ds(pl.multiple_of((z * 2 + x - planes + 2) * gy, gy), gy)
                        high[:, place] = new.astype(bf16)
                return carry

            lax.fori_loop(0, gz, step, 0)
            norm[...] = line_of(lanes[...])

        return run(
            body,
            [(where, "s")]
            + [(g, "v") for g in others]
            + [
                (locked_flat, "v"),
                (acc, "v"),
                (rhs, "v"),
                (field, "v"),
                (flat_occupied, "v"),
                (scalars, "v"),
            ],
            [
                ((columns, cells), f32, True),
                ((columns, cells), f32, True),
                ((columns, gz * 2 * gy), bf16, False),
                ((columns, gz * 2 * gy), bf16, False),
                ((perts, cells), bf16, False),
                ((1, columns), f32, False),
            ],
            scratch=[
                pltpu.VMEM((columns, half), bf16),
                pltpu.VMEM((columns, gy), f32),
                pltpu.VMEM((columns, gy), f32),
            ],
            aliases={chips + 3: 0, chips + 4: 1},
            limit=5,
            name="first_finish",
        )

    def second_finish(others, acc, rhs):
        def body(where_ref, *refs):
            pieces = refs[:chips]
            lock, acc_ref, rhs_ref, res, norm, held, lanes = refs[chips:]
            collect(where_ref, pieces, held)
            lanes[...] = jnp.zeros_like(lanes)
            rows = pl.ds(pl.multiple_of((1 - where_ref[0]) * half, half), half)

            def step(z, carry):
                at = pl.ds(pl.multiple_of(z * stripe, stripe), stripe)
                removed = acc_ref[:, at] + dot_nn(held[...], lock[rows, at])
                value = rhs_ref[:, at] - removed
                res[:, at] = value
                lanes[...] += squares(value)
                return carry

            lax.fori_loop(0, gz, step, 0)
            norm[...] = line_of(lanes[...])

        return run(
            body,
            [(where, "s")]
            + [(g, "v") for g in others]
            + [(locked_flat, "v"), (acc, "v"), (rhs, "v")],
            [((columns, cells), f32, True), ((1, columns), f32, False)],
            scratch=[pltpu.VMEM((columns, half), bf16), pltpu.VMEM((columns, gy), f32)],
            aliases={chips + 3: 0},
            limit=2,
            name="second_finish",
        )

    def across(array, axis):
        return [array] + [swap(array, m, axis) for m in range(1, lax.axis_size(axis))]

    def norm_terms(norm):
        other = swap(norm, 1, "dom")

        def body(one, two, out):
            out[...] = one[...] + two[...]

        (pair,) = run(
            body, [(norm, "v"), (other, "v")], [((1, columns), f32, False)], limit=1, name="pair"
        )
        return [pair] + [swap(pair, 2 * m, "dom") for m in range(1, chips)]

    partial1 = stencil(flat_response)
    rhs1, gathered1 = margins(partial1, halos1, flat_perturbation)
    others1 = [swap(g, 1, "dom") for g in gathered1]
    acc1 = remove_own(gathered1)
    first_res, middle, low_edge, high_edge, dens, norm1 = first_finish(
        others1, acc1, rhs1, flat_response
    )
    halos2 = halos_of([low_edge, high_edge])
    densities = across(dens, "band")
    norms1 = norm_terms(norm1)

    def potential_body(*refs):
        parts, squares1 = refs[:bands], refs[bands : bands + chips]
        pert, xc, flat, native, norm = refs[bands + chips :]
        norm[...] = tree_sum([r[...] for r in squares1])
        density = tree_sum([r[...].astype(f32) for r in parts])
        for z in range(gz):
            for x in range(planes):
                cut = slice(col(z, x), col(z, x) + gy)
                for p in range(perts):
                    value = pert[p, 0:1, cut] - xc[0:1, cut] * density[p : p + 1, cut]
                    flat[p, 0:1, cut] = value
                    native[p, x, z : z + 1, :] = value

    flat_rp, response_potential, first_norm = run(
        potential_body,
        [(d, "v") for d in densities]
        + [(n, "v") for n in norms1]
        + [(flat_perturbation, "v"), (flat_xc, "v")],
        [
            ((perts, 1, cells), f32, True),
            ((perts, planes, gz, gy), f32, False),
            ((1, columns), f32, True),
        ],
        limit=1,
        name="potential",
    )

    partial2 = stencil(middle)
    rhs2, gathered2 = margins(partial2, halos2, flat_rp)
    others2 = [swap(g, 1, "dom") for g in gathered2]
    acc2 = remove_own(gathered2)
    second_res, norm2 = second_finish(others2, acc2, rhs2)
    norms2 = norm_terms(norm2)

    def final_body(*refs):
        twos = refs[:chips]
        one, mid, res1, res2, scal, out, steps, blends = refs[chips:]
        ratio = tree_sum([r[...] for r in twos]) / one[...]
        blend = scal[2:3, :] * ratio
        steps[...] = per_row(scal, 2, gy)
        blends[...] = jnp.broadcast_to(blend, (gy, columns)).T
        block = 64 if columns % 64 == 0 else columns

        def rows_step(i, carry):
            rows = pl.ds(pl.multiple_of(i * block, block), block)
            step, mix = steps[rows, :], blends[rows, :]
            for x in range(planes):
                values = []
                for z in range(gz):
                    cut = slice(col(z, x), col(z, x) + gy)
                    values.append(mid[rows, cut] + step * res2[rows, cut] + mix * res1[rows, cut])
                out[rows, x] = jnp.concatenate(values, axis=1).reshape(block, gz, gy)
            return carry

        lax.fori_loop(0, columns // block, rows_step, 0)

    (new_response,) = run(
        final_body,
        [(n, "v") for n in norms2]
        + [(first_norm, "v"), (middle, "v"), (first_res, "v"), (second_res, "v"), (scalars, "v")],
        [((columns, planes, gz, gy), f32, False)],
        scratch=[pltpu.VMEM((columns, gy), f32), pltpu.VMEM((columns, gy), f32)],
        limit=5,
        name="final",
    )
    return new_response.reshape(response.shape), response_potential


def solution(mesh):
    placed = (
        P(None, "band", "dom", None, None),
        P("band", "dom", None, None),
        P(None, "dom", None, None),
        P("dom", None, None),
        P(None, "dom", None, None),
        P("dom", None, None),
        P("band"),
        P(None, "band"),
        P(None, "band"),
    )
    return jax.shard_map(
        local,
        mesh=mesh,
        in_specs=placed,
        out_specs=(P(None, "band", "dom", None, None), P(None, "dom", None, None)),
        check_vma=False,
    )
```

time: 435 us -> 282 us (0.65); the launches traced: 427 us -> 282 us
  matrix products: 129 us -> 0 us
  Pallas kernels: 0 us -> 85.7 us
  other arithmetic: 44.2 us -> 0.08 us
  waiting for transfers between devices: 111 us -> 72.3 us
  blocking collectives: 30.9 us -> 0 us
  starting transfers between devices: 6.17 us -> 33.2 us
  between operations: 15 us -> 0.95 us
    dot_general x16 -> x0, matrix products: 129 us -> none  [the longest x8 72.3 us: project(): lax.dot_general(locked_block, rounded, (((1,), (1,)), ((), ())), preferre...]
    psum x2 -> x0, waiting for transfers between devices: 111 us -> none  [project(): margin_b = lax.psum(partial_margin.astype(jnp.bfloat16), 'dom')]
    pallas_call x0 -> x19, Pallas kernels: none -> 85.7 us  [run(): pl.pallas_call(body, in_specs=[pl.BlockSpec(memory_space=kinds[kind]) for...]
    unnamed x72 -> x26, local copies, waits for them, and re-layouts: 8.97 us -> 87.1 us
    ppermute x4 -> x37, waiting for transfers between devices: 0.01 us -> 72.3 us  [the longest x33 72.3 us: swap(): return lax.ppermute(array, axis, [(i, i ^ mask) for i in range(count)])]
    slice x11 -> x0, local copies, waits for them, and re-layouts: 66.4 us -> none  [the longest x1 22.7 us: project(): locked_flat[block_index * block_rows:(block_index + 1) * block_rows]]
    convert_element_type x7 -> x0, other arithmetic: 36.2 us -> none  [the longest x2 30.3 us: project(): rounded = flattened.astype(jnp.bfloat16)]
    psum x2 -> x0, blocking collectives: 30.9 us -> none  [the longest x1 19 us: local(): lax.psum(density_local.astype(jnp.bfloat16), 'band').astype(jnp.float32)]
  transfers between devices with their start and end apart: 6 -> 37, of which waited for: 2 -> 17; matrix products, arithmetic and copies ran while one was open for 15% -> 0% of each run, Pallas kernels for 0% -> 14%
where the time goes in v1:
time: 282 us
  local copies, waits for them, and re-layouts  89.3 us (32%)
  Pallas kernels  85.7 us (30%)
  waiting for transfers between devices  72.3 us (26%)
  starting transfers between devices  33.2 us (12%)
    unnamed x26, local copies, waits for them, and re-layouts  87.1 us
    pallas_call x19, Pallas kernels, run(): pl.pallas_call(body, in_specs=[pl.BlockSpec(memory_space=kinds[kind]) for...  85.7 us
    ppermute x33, waiting for transfers between devices, swap(): return lax.ppermute(array, axis, [(i, i ^ mask) for i in range(count)])  72.3 us
    ppermute x33, starting transfers between devices, swap(): return lax.ppermute(array, axis, [(i, i ^ mask) for i in range(count)])  27 us
  transfers between devices with their start and end apart: 37, of which 17 were waited for; matrix products, arithmetic and copies ran while one was open for 0% of the time, Pallas kernels for 14%

profile of v1, /device:TPU:0, one launch (start us, length us, event | category | flops | bytes accessed | tf_op | source)
XLA Modules:
  0.0 281.7 jit_solution(14261759085668325109)
XLA Ops:
  3.0 2.2 copy-done.8
  5.2 1.3 flatten.1
  7.0 3.0 %collective-permute-start.1 = (bf16[256,2048]{1,0:T(8,128)(2,1)S(1)}, bf16[256,2048]{1,0:T(8,128)(2,1)S(1)}, u32[]{:S(2)}, u32[]{:S(2)}) collective-permute-start(bf16[256,2048]{1,0:T(8,128)(2,1)S(1)} %get-tuple-element.37), channel_id=1, source_target_pairs={{1,0},{2,1},{3,2},{4,3},{5,4},{6,5},{7,6},{0,7},{9,8},{10,9},{11,1... | collective-permute-start | bytes 3145736 | tf_op jit(solution)/shard_map/ppermute | solution.py:134
  9.9 15.4 %relay.1.lock.refs_4_ = bf16[4096,4096]{1,0:T(8,128)(2,1)S(1)} custom-call(bf16[4096,4,8,128]{3,2,1,0:T(8,128)(2,1)} %source.1), custom_call_target="tpu_custom_call" | custom-call | tf_op jit(solution)/shard_map/relay/pallas_call | solution.py:23
  25.4 11.1 %copy-done = bf16[4096,4096]{1,0:T(8,128)(2,1)} copy-done((bf16[4096,4096]{1,0:T(8,128)(2,1)}, bf16[4096,4096]{1,0:T(8,128)(2,1)S(1)}, u32[]{:S(2)}) %copy-start) | copy-done | bytes 33554456
  36.8 5.0 %stencil.2.part_ref = f32[256,4096]{1,0:T(8,128)S(1)} custom-call(f32[256,4096]{1,0:T(8,128)S(1)} %get-tuple-element.34.field.refs_7_, f32[1,4096]{1,0:T(1,128)S(1)} %get-tuple-element.35.pot, f32[3,256]{1,0:T(4,128)S(1)} %pad_maximum_fusion.early.scal.refs_9_.refs_8_), custom_call_target="tpu_custom_call" | custom-call | tf_op jit(solution)/shard_map/stencil/pallas_call | solution.py:23
  41.8 10.5 %copy-done.1 = bf16[4096,4096]{1,0:T(8,128)(2,1)S(1)} copy-done((bf16[4096,4096]{1,0:T(8,128)(2,1)S(1)}, bf16[4096,4096]{1,0:T(8,128)(2,1)}, u32[]{:S(2)}) %copy-start.1) | copy-done | bytes 33554456
  52.4 6.4 %margin_other.2 = (f32[256,4096]{1,0:T(8,128)S(1)}, bf16[256,4096]{1,0:T(8,128)(2,1)S(1)}, bf16[256,2048]{1,0:T(8,128)(2,1)S(1)}) custom-call(s32[2]{0:T(128)S(1)} %pad_add_fusion.placed.where_ref, f32[256,4096]{1,0:T(8,128)S(1)} %stencil.2.part_ref, bf16[256,2048]{1,0:T(8,128)(2,1)S(1)} %collective-permute-done.low_ref, ...), custom_call_target="tpu_custom_call", output_to_operand_aliasing={{0}: (1, {})} | custom-call | tf_op jit(solution)/shard_map/margin_other/pallas_call | solution.py:23
  58.9 2.6 collective-permute-done.2.arrived_ref
  61.5 10.5 %copy-done.2 = bf16[4096,4096]{1,0:T(8,128)(2,1)S(1)} copy-done((bf16[4096,4096]{1,0:T(8,128)(2,1)S(1)}, bf16[4096,4096]{1,0:T(8,128)(2,1)}, u32[]{:S(2)}) %copy-start.2) | copy-done | bytes 33554456
  72.1 5.1 %margin_own.2 = (f32[256,512]{1,0:T(8,128)S(1)}, bf16[256,512]{1,0:T(8,128)(2,1)S(1)}, bf16[256,512]{1,0:T(8,128)(2,1)S(1)}, bf16[256,512]{1,0:T(8,128)(2,1)S(1)}) custom-call(s32[2]{0:T(128)S(1)} %pad_add_fusion.placed.where_ref, bf16[256,4096]{1,0:T(8,128)(2,1)S(1)} %get-tuple-element.40.rounded_ref, bf16[4096,4096]{1,0:T(8,128)(2,1)S(1)} %copy-done.2, ...), custom_call_target="tpu_custom_call" | custom-call | tf_op jit(solution)/shard_map/margin_own/pallas_call | solution.py:23
  77.1 1.4 collective-permute-start.3
  78.5 1.5 collective-permute-start.4
  80.9 5.5 %collective-permute-done.3.refs_1_ = bf16[256,512]{1,0:T(8,128)(2,1)S(1)} collective-permute-done((bf16[256,512]{1,0:T(8,128)(2,1)S(1)}, bf16[256,512]{1,0:T(8,128)(2,1)S(1)}, u32[]{:S(2)}, u32[]{:S(2)}) %collective-permute-start.3) | collective-permute-done | bytes 262176 | tf_op jit(solution)/shard_map/ppermute | solution.py:93
  86.3 4.9 %collective-permute-done.4.refs_2_ = bf16[256,512]{1,0:T(8,128)(2,1)S(1)} collective-permute-done((bf16[256,512]{1,0:T(8,128)(2,1)S(1)}, bf16[256,512]{1,0:T(8,128)(2,1)S(1)}, u32[]{:S(2)}, u32[]{:S(2)}) %collective-permute-start.4) | collective-permute-done | bytes 262176 | tf_op jit(solution)/shard_map/ppermute | solution.py:93
  91.2 1.6 collective-permute-done.5.refs_3_
  93.0 1.8 collective-permute-start.11
  95.1 1.4 collective-permute-start.7
  96.5 6.7 %collective-permute-done.11.refs_3_ = bf16[256,512]{1,0:T(8,128)(2,1)S(1)} collective-permute-done((bf16[256,512]{1,0:T(8,128)(2,1)S(1)}, bf16[256,512]{1,0:T(8,128)(2,1)S(1)}, u32[]{:S(2)}, u32[]{:S(2)}) %collective-permute-start.11) | collective-permute-done | bytes 262176 | tf_op jit(solution)/shard_map/ppermute | solution.py:93
  103.2 3.3 %collective-permute-done.9.refs_2_ = bf16[256,512]{1,0:T(8,128)(2,1)S(1)} collective-permute-done((bf16[256,512]{1,0:T(8,128)(2,1)S(1)}, bf16[256,512]{1,0:T(8,128)(2,1)S(1)}, u32[]{:S(2)}, u32[]{:S(2)}) %collective-permute-start.9) | collective-permute-done | bytes 262176 | tf_op jit(solution)/shard_map/ppermute | solution.py:93
  107.0 10.5 %copy-done.3 = bf16[4096,4096]{1,0:T(8,128)(2,1)S(1)} copy-done((bf16[4096,4096]{1,0:T(8,128)(2,1)S(1)}, bf16[4096,4096]{1,0:T(8,128)(2,1)}, u32[]{:S(2)}) %copy-start.3) | copy-done | bytes 33554456
  117.5 6.4 %remove_own.2.refs_5_ = f32[256,4096]{1,0:T(8,128)S(1)} custom-call(s32[2]{0:T(128)S(1)} %pad_add_fusion.placed.where_ref, bf16[256,512]{1,0:T(8,128)(2,1)S(1)} %add_pieces.2.refs_0_, bf16[256,512]{1,0:T(8,128)(2,1)S(1)} %collective-permute-done.7.refs_1_, bf16[256,512]{1,0:T(8,128)(2,1)S(1)} %collective-permute-done.9.refs_2_, ...), custom_call_target="tpu_custom_call" | custom-call | tf_op jit(solution)/shard_map/remove_own/pallas_call | solution.py:23
  123.9 10.5 %copy-done.4 = bf16[4096,4096]{1,0:T(8,128)(2,1)S(1)} copy-done((bf16[4096,4096]{1,0:T(8,128)(2,1)S(1)}, bf16[4096,4096]{1,0:T(8,128)(2,1)}, u32[]{:S(2)}) %copy-start.4) | copy-done | bytes 33554456
  134.5 8.4 %first_finish.1 = (f32[256,4096]{1,0:T(8,128)S(1)}, f32[256,4096]{1,0:T(8,128)S(1)}, bf16[256,2048]{1,0:T(8,128)(2,1)S(1)}, bf16[256,2048]{1,0:T(8,128)(2,1)S(1)...) custom-call(s32[2]{0:T(128)S(1)} %pad_add_fusion.placed.where_ref, ...), custom_call_target="tpu_custom_call", output_to_operand_aliasing={{0}: (7, {}), {1}: (8, {})} | custom-call | tf_op jit(solution)/shard_map/first_finish/pallas_call | solution.py:23
  143.0 2.6 collective-permute-start.14
  146.8 1.4 collective-permute-start.21
  148.9 1.4 collective-permute-start.19
  150.3 19.1 %collective-permute-done.21.refs_7_ = f32[1,256]{1,0:T(1,128)S(1)} collective-permute-done((f32[1,256]{1,0:T(1,128)S(1)}, f32[1,256]{1,0:T(1,128)S(1)}, u32[]{:S(2)}, u32[]{:S(2)}) %collective-permute-start.21) | collective-permute-done | bytes 1056 | tf_op jit(solution)/shard_map/ppermute | solution.py:93
  169.4 3.6 %collective-permute-start.17 = (bf16[4,4096]{1,0:T(4,128)(2,1)S(1)}, bf16[4,4096]{1,0:T(4,128)(2,1)S(1)}, u32[]{:S(2)}, u32[]{:S(2)}) collective-permute-start(bf16[4,4096]{1,0:T(4,128)(2,1)S(1)} %get-tuple-element.50.refs_0_), channel_id=1, source_target_pairs={{0,24},{8,16},{16,8},{24,0},{1,25},{9,17},{17,9},{25,1},{2,26},{10... | collective-permute-start | bytes 98312 | tf_op jit(solution)/shard_map/ppermute | solution.py:93
  173.8 5.0 %stencil.3.part_ref = f32[256,4096]{1,0:T(8,128)S(1)} custom-call(f32[256,4096]{1,0:T(8,128)S(1)} %get-tuple-element.47.field.refs_5_, f32[1,4096]{1,0:T(1,128)S(1)} %get-tuple-element.35.pot, f32[3,256]{1,0:T(4,128)S(1)} %pad_maximum_fusion.early.scal.refs_9_.refs_8_), custom_call_target="tpu_custom_call" | custom-call | tf_op jit(solution)/shard_map/stencil/pallas_call | solution.py:23
  179.5 10.5 %copy-done.5 = bf16[4096,4096]{1,0:T(8,128)(2,1)S(1)} copy-done((bf16[4096,4096]{1,0:T(8,128)(2,1)S(1)}, bf16[4096,4096]{1,0:T(8,128)(2,1)}, u32[]{:S(2)}) %copy-start.5) | copy-done | bytes 33554456
  190.1 6.6 %margin_other.3 = (f32[256,4096]{1,0:T(8,128)S(1)}, bf16[256,4096]{1,0:T(8,128)(2,1)S(1)}, bf16[256,2048]{1,0:T(8,128)(2,1)S(1)}) custom-call(s32[2]{0:T(128)S(1)} %pad_add_fusion.placed.where_ref, f32[256,4096]{1,0:T(8,128)S(1)} %stencil.3.part_ref, bf16[256,2048]{1,0:T(8,128)(2,1)S(1)} %collective-permute-done.13.low_ref, ...), custom_call_target="tpu_custom_call", output_to_operand_aliasing={{0}: (1, {})} | custom-call | tf_op jit(solution)/shard_map/margin_other/pallas_call | solution.py:23
  196.8 2.6 collective-permute-done.22.arrived_ref
  199.4 10.5 %copy-done.6 = bf16[4096,4096]{1,0:T(8,128)(2,1)S(1)} copy-done((bf16[4096,4096]{1,0:T(8,128)(2,1)S(1)}, bf16[4096,4096]{1,0:T(8,128)(2,1)}, u32[]{:S(2)}) %copy-start.6) | copy-done | bytes 33554456
  210.0 5.1 %margin_own.3 = (f32[256,512]{1,0:T(8,128)S(1)}, bf16[256,512]{1,0:T(8,128)(2,1)S(1)}, bf16[256,512]{1,0:T(8,128)(2,1)S(1)}, bf16[256,512]{1,0:T(8,128)(2,1)S(1)}) custom-call(s32[2]{0:T(128)S(1)} %pad_add_fusion.placed.where_ref, bf16[256,4096]{1,0:T(8,128)(2,1)S(1)} %get-tuple-element.54.rounded_ref, bf16[4096,4096]{1,0:T(8,128)(2,1)S(1)} %copy-done.6, ...), custom_call_target="tpu_custom_call" | custom-call | tf_op jit(solution)/shard_map/margin_own/pallas_call | solution.py:23
  215.4 1.5 collective-permute-start.24
  216.8 1.8 collective-permute-start.25
  218.6 5.7 %collective-permute-done.23.refs_1_ = bf16[256,512]{1,0:T(8,128)(2,1)S(1)} collective-permute-done((bf16[256,512]{1,0:T(8,128)(2,1)S(1)}, bf16[256,512]{1,0:T(8,128)(2,1)S(1)}, u32[]{:S(2)}, u32[]{:S(2)}) %collective-permute-start.23) | collective-permute-done | bytes 262176 | tf_op jit(solution)/shard_map/ppermute | solution.py:93
  224.2 5.2 %collective-permute-done.25.refs_3_ = bf16[256,512]{1,0:T(8,128)(2,1)S(1)} collective-permute-done((bf16[256,512]{1,0:T(8,128)(2,1)S(1)}, bf16[256,512]{1,0:T(8,128)(2,1)S(1)}, u32[]{:S(2)}, u32[]{:S(2)}) %collective-permute-start.25) | collective-permute-done | bytes 262176 | tf_op jit(solution)/shard_map/ppermute | solution.py:93
  229.6 1.8 collective-permute-start.31
  233.1 6.7 %collective-permute-done.31.refs_3_ = bf16[256,512]{1,0:T(8,128)(2,1)S(1)} collective-permute-done((bf16[256,512]{1,0:T(8,128)(2,1)S(1)}, bf16[256,512]{1,0:T(8,128)(2,1)S(1)}, u32[]{:S(2)}, u32[]{:S(2)}) %collective-permute-start.31) | collective-permute-done | bytes 262176 | tf_op jit(solution)/shard_map/ppermute | solution.py:93
  239.8 3.6 %collective-permute-done.29.refs_2_ = bf16[256,512]{1,0:T(8,128)(2,1)S(1)} collective-permute-done((bf16[256,512]{1,0:T(8,128)(2,1)S(1)}, bf16[256,512]{1,0:T(8,128)(2,1)S(1)}, u32[]{:S(2)}, u32[]{:S(2)}) %collective-permute-start.29) | collective-permute-done | bytes 262176 | tf_op jit(solution)/shard_map/ppermute | solution.py:93
  243.9 10.5 %copy-done.7 = bf16[4096,4096]{1,0:T(8,128)(2,1)S(1)} copy-done((bf16[4096,4096]{1,0:T(8,128)(2,1)S(1)}, bf16[4096,4096]{1,0:T(8,128)(2,1)}, u32[]{:S(2)}) %copy-start.7) | copy-done | bytes 33554456
  254.4 6.4 %remove_own.3.refs_5_ = f32[256,4096]{1,0:T(8,128)S(1)} custom-call(s32[2]{0:T(128)S(1)} %pad_add_fusion.placed.where_ref, bf16[256,512]{1,0:T(8,128)(2,1)S(1)} %add_pieces.3.refs_0_, bf16[256,512]{1,0:T(8,128)(2,1)S(1)} %collective-permute-done.27.refs_1_, bf16[256,512]{1,0:T(8,128)(2,1)S(1)} %collective-permute-done.29.refs_2_, ...), custom_call_target="tpu_custom_call" | custom-call | tf_op jit(solution)/shard_map/remove_own/pallas_call | solution.py:23
  260.8 6.7 %second_finish.1 = (f32[256,4096]{1,0:T(8,128)S(1)}, f32[1,256]{1,0:T(1,128)S(1)}) custom-call(s32[2]{0:T(128)S(1)} %pad_add_fusion.placed.where_ref, bf16[256,512]{1,0:T(8,128)(2,1)S(1)} %collective-permute-done.26.refs_0_, bf16[256,512]{1,0:T(8,128)(2,1)S(1)} %collective-permute-done.28.refs_1_, ...), custom_call_target="tpu_custom_call", output_to_operand_aliasing={{0}: (7, {})} | custom-call | tf_op jit(solution)/shard_map/second_finish/pallas_call | solution.py:23
  269.9 1.5 collective-permute-start.35
  273.5 1.5 collective-permute-done.34.refs_1_
  274.9 6.7 %final.1 = f32[256,4,8,128]{3,2,1,0:T(8,128)} custom-call(f32[1,256]{1,0:T(1,128)S(1)} %pair.3.refs_0_, f32[1,256]{1,0:T(1,128)S(1)} %collective-permute-done.34.refs_1_, f32[1,256]{1,0:T(1,128)S(1)} %collective-permute-done.35.refs_2_, f32[1,256]{1,0:T(1,128)S(1)} %collective-permute-done.36.refs_3_, f32[1,256]{1,0:T(1,128)S(1)} %get-tuple-element.62.refs_4_, ...), custom_call_target="tpu_custom_call" | custom-call | tf_op jit(solution)/shard_map/final/pallas_call | solution.py:23
  (77 shorter events, 15.8 us)
Async XLA Ops:
  6.4 35.3 %collective-permute-start = (bf16[256,2048]{1,0:T(8,128)(2,1)S(1)}, bf16[256,2048]{1,0:T(8,128)(2,1)S(1)}, u32[]{:S(2)}, u32[]{:S(2)}) collective-permute-start(bf16[256,2048]{1,0:T(8,128)(2,1)S(1)} %get-tuple-element.36), channel_id=1, source_target_pairs={{0,1},{1,2},{2,3},{3,4},{4,5},{5,6},{6,7},{7,0},{8,9},{9,10},{10,1... | collective-permute-start | bytes 3145736 | tf_op jit(solution)/shard_map/ppermute | solution.py:133
  6.9 29.5 %copy-start.9 = (f32[64,4,8,128]{3,2,1,0:T(8,128)S(1)}, f32[64,4,8,128]{3,2,1,0:T(8,128)}, u32[]{:S(2)}) copy-start(f32[64,4,8,128]{3,2,1,0:T(8,128)} %occ.1) | copy-start | bytes 3145732
  7.0 29.5 %copy-start.10 = (f32[4,4,8,128]{3,2,1,0:T(8,128)S(1)}, f32[4,4,8,128]{3,2,1,0:T(8,128)}, u32[]{:S(2)}) copy-start(f32[4,4,8,128]{3,2,1,0:T(8,128)} %pert.1) | copy-start | bytes 196612
  7.0 29.5 %copy-start.11 = (f32[4,8,128]{2,1,0:T(8,128)S(1)}, f32[4,8,128]{2,1,0:T(8,128)}, u32[]{:S(2)}) copy-start(f32[4,8,128]{2,1,0:T(8,128)} %pot.1) | copy-start | bytes 49156
  7.0 29.5 %copy-start.12 = (f32[4,8,128]{2,1,0:T(8,128)S(1)}, f32[4,8,128]{2,1,0:T(8,128)}, u32[]{:S(2)}) copy-start(f32[4,8,128]{2,1,0:T(8,128)} %xc.1) | copy-start | bytes 49156
  7.0 34.8 %collective-permute-start.1 = (bf16[256,2048]{1,0:T(8,128)(2,1)S(1)}, bf16[256,2048]{1,0:T(8,128)(2,1)S(1)}, u32[]{:S(2)}, u32[]{:S(2)}) collective-permute-start(bf16[256,2048]{1,0:T(8,128)(2,1)S(1)} %get-tuple-element.37), channel_id=1, source_target_pairs={{1,0},{2,1},{3,2},{4,3},{5,4},{6,5},{7,6},{0,7},{9,8},{10,9},{11,1... | collective-permute-start | bytes 3145736 | tf_op jit(solution)/shard_map/ppermute | solution.py:134
  25.4 11.1 %copy-start = (bf16[4096,4096]{1,0:T(8,128)(2,1)}, bf16[4096,4096]{1,0:T(8,128)(2,1)S(1)}, u32[]{:S(2)}) copy-start(bf16[4096,4096]{1,0:T(8,128)(2,1)S(1)} %relay.1.lock.refs_4_) | copy-start | bytes 100663296
  41.8 10.5 %copy-start.1 = (bf16[4096,4096]{1,0:T(8,128)(2,1)S(1)}, bf16[4096,4096]{1,0:T(8,128)(2,1)}, u32[]{:S(2)}) copy-start(bf16[4096,4096]{1,0:T(8,128)(2,1)} %copy-done) | copy-start | bytes 100663296
  58.8 2.7 collective-permute-start.2
  61.5 10.5 %copy-start.2 = (bf16[4096,4096]{1,0:T(8,128)(2,1)S(1)}, bf16[4096,4096]{1,0:T(8,128)(2,1)}, u32[]{:S(2)}) copy-start(bf16[4096,4096]{1,0:T(8,128)(2,1)} %copy-done) | copy-start | bytes 100663296
  77.1 9.2 %collective-permute-start.3 = (bf16[256,512]{1,0:T(8,128)(2,1)S(1)}, bf16[256,512]{1,0:T(8,128)(2,1)S(1)}, u32[]{:S(2)}, u32[]{:S(2)}) collective-permute-start(bf16[256,512]{1,0:T(8,128)(2,1)S(1)} %get-tuple-element.43), channel_id=1, source_target_pairs={{0,2},{1,3},{2,0},{3,1},{4,6},{5,7},{6,4},{7,5},{8,10},{9,11},{10,... | collective-permute-start | bytes 786440 | tf_op jit(solution)/shard_map/ppermute | solution.py:93
  78.5 12.7 %collective-permute-start.4 = (bf16[256,512]{1,0:T(8,128)(2,1)S(1)}, bf16[256,512]{1,0:T(8,128)(2,1)S(1)}, u32[]{:S(2)}, u32[]{:S(2)}) collective-permute-start(bf16[256,512]{1,0:T(8,128)(2,1)S(1)} %get-tuple-element.44), channel_id=1, source_target_pairs={{0,4},{1,5},{2,6},{3,7},{4,0},{5,1},{6,2},{7,3},{8,12},{9,13},{10,... | collective-permute-start | bytes 786440 | tf_op jit(solution)/shard_map/ppermute | solution.py:93
  80.0 12.8 %collective-permute-start.5 = (bf16[256,512]{1,0:T(8,128)(2,1)S(1)}, bf16[256,512]{1,0:T(8,128)(2,1)S(1)}, u32[]{:S(2)}, u32[]{:S(2)}) collective-permute-start(bf16[256,512]{1,0:T(8,128)(2,1)S(1)} %get-tuple-element.45), channel_id=1, source_target_pairs={{0,6},{1,7},{2,4},{3,5},{4,2},{5,3},{6,0},{7,1},{8,14},{9,15},{10,... | collective-permute-start | bytes 786440 | tf_op jit(solution)/shard_map/ppermute | solution.py:93
  93.0 10.2 %collective-permute-start.11 = (bf16[256,512]{1,0:T(8,128)(2,1)S(1)}, bf16[256,512]{1,0:T(8,128)(2,1)S(1)}, u32[]{:S(2)}, u32[]{:S(2)}) collective-permute-start(bf16[256,512]{1,0:T(8,128)(2,1)S(1)} %add_pieces.2.refs_0_), channel_id=1, source_target_pairs={{0,6},{1,7},{2,4},{3,5},{4,2},{5,3},{6,0},{7,1},{8,14},{9,15},{10,... | collective-permute-start | bytes 786440 | tf_op jit(solution)/shard_map/ppermute | solution.py:93
  94.8 11.7 %collective-permute-start.9 = (bf16[256,512]{1,0:T(8,128)(2,1)S(1)}, bf16[256,512]{1,0:T(8,128)(2,1)S(1)}, u32[]{:S(2)}, u32[]{:S(2)}) collective-permute-start(bf16[256,512]{1,0:T(8,128)(2,1)S(1)} %add_pieces.2.refs_0_), channel_id=1, source_target_pairs={{0,4},{1,5},{2,6},{3,7},{4,0},{5,1},{6,2},{7,3},{8,12},{9,13},{10,... | collective-permute-start | bytes 786440 | tf_op jit(solution)/shard_map/ppermute | solution.py:93
  95.1 11.4 %collective-permute-start.7 = (bf16[256,512]{1,0:T(8,128)(2,1)S(1)}, bf16[256,512]{1,0:T(8,128)(2,1)S(1)}, u32[]{:S(2)}, u32[]{:S(2)}) collective-permute-start(bf16[256,512]{1,0:T(8,128)(2,1)S(1)} %add_pieces.2.refs_0_), channel_id=1, source_target_pairs={{0,2},{1,3},{2,0},{3,1},{4,6},{5,7},{6,4},{7,5},{8,10},{9,11},{10,... | collective-permute-start | bytes 786440 | tf_op jit(solution)/shard_map/ppermute | solution.py:93
  96.5 27.4 %collective-permute-start.6 = (bf16[256,512]{1,0:T(8,128)(2,1)S(1)}, bf16[256,512]{1,0:T(8,128)(2,1)S(1)}, u32[]{:S(2)}, u32[]{:S(2)}) collective-permute-start(bf16[256,512]{1,0:T(8,128)(2,1)S(1)} %add_pieces.2.refs_0_), channel_id=1, source_target_pairs={{0,1},{1,0},{2,3},{3,2},{4,5},{5,4},{6,7},{7,6},{8,9},{9,8},{10,11... | collective-permute-start | bytes 786440 | tf_op jit(solution)/shard_map/ppermute | solution.py:93
  103.2 20.7 %collective-permute-start.12 = (bf16[256,512]{1,0:T(8,128)(2,1)S(1)}, bf16[256,512]{1,0:T(8,128)(2,1)S(1)}, u32[]{:S(2)}, u32[]{:S(2)}) collective-permute-start(bf16[256,512]{1,0:T(8,128)(2,1)S(1)} %collective-permute-done.11.refs_3_), channel_id=1, source_target_pairs={{0,1},{1,0},{2,3},{3,2},{4,5},{5,4},{6,7},{7,6},{8,9},{9,8},{10,11... | collective-permute-start | bytes 786440 | tf_op jit(solution)/shard_map/ppermute | solution.py:93
  106.5 17.5 %collective-permute-start.10 = (bf16[256,512]{1,0:T(8,128)(2,1)S(1)}, bf16[256,512]{1,0:T(8,128)(2,1)S(1)}, u32[]{:S(2)}, u32[]{:S(2)}) collective-permute-start(bf16[256,512]{1,0:T(8,128)(2,1)S(1)} %collective-permute-done.9.refs_2_), channel_id=1, source_target_pairs={{0,1},{1,0},{2,3},{3,2},{4,5},{5,4},{6,7},{7,6},{8,9},{9,8},{10,11... | collective-permute-start | bytes 786440 | tf_op jit(solution)/shard_map/ppermute | solution.py:93
  106.5 17.5 %collective-permute-start.8 = (bf16[256,512]{1,0:T(8,128)(2,1)S(1)}, bf16[256,512]{1,0:T(8,128)(2,1)S(1)}, u32[]{:S(2)}, u32[]{:S(2)}) collective-permute-start(bf16[256,512]{1,0:T(8,128)(2,1)S(1)} %collective-permute-done.7.refs_1_), channel_id=1, source_target_pairs={{0,1},{1,0},{2,3},{3,2},{4,5},{5,4},{6,7},{7,6},{8,9},{9,8},{10,11... | collective-permute-start | bytes 786440 | tf_op jit(solution)/shard_map/ppermute | solution.py:93
  107.0 10.5 %copy-start.3 = (bf16[4096,4096]{1,0:T(8,128)(2,1)S(1)}, bf16[4096,4096]{1,0:T(8,128)(2,1)}, u32[]{:S(2)}) copy-start(bf16[4096,4096]{1,0:T(8,128)(2,1)} %copy-done) | copy-start | bytes 100663296
  123.9 10.5 %copy-start.4 = (bf16[4096,4096]{1,0:T(8,128)(2,1)S(1)}, bf16[4096,4096]{1,0:T(8,128)(2,1)}, u32[]{:S(2)}) copy-start(bf16[4096,4096]{1,0:T(8,128)(2,1)} %copy-done) | copy-start | bytes 100663296
  142.9 36.6 %collective-permute-start.13 = (bf16[256,2048]{1,0:T(8,128)(2,1)S(1)}, bf16[256,2048]{1,0:T(8,128)(2,1)S(1)}, u32[]{:S(2)}, u32[]{:S(2)}) collective-permute-start(bf16[256,2048]{1,0:T(8,128)(2,1)S(1)} %get-tuple-element.48), channel_id=1, source_target_pairs={{0,1},{1,2},{2,3},{3,4},{4,5},{5,6},{6,7},{7,0},{8,9},{9,10},{10,1... | collective-permute-start | bytes 3145736 | tf_op jit(solution)/shard_map/ppermute | solution.py:133
  143.0 36.5 %collective-permute-start.14 = (bf16[256,2048]{1,0:T(8,128)(2,1)S(1)}, bf16[256,2048]{1,0:T(8,128)(2,1)S(1)}, u32[]{:S(2)}, u32[]{:S(2)}) collective-permute-start(bf16[256,2048]{1,0:T(8,128)(2,1)S(1)} %get-tuple-element.49), channel_id=1, source_target_pairs={{1,0},{2,1},{3,2},{4,3},{5,4},{6,5},{7,6},{0,7},{9,8},{10,9},{11,1... | collective-permute-start | bytes 3145736 | tf_op jit(solution)/shard_map/ppermute | solution.py:134
  145.6 1.1 collective-permute-start.18
  146.8 22.6 %collective-permute-start.21 = (f32[1,256]{1,0:T(1,128)S(1)}, f32[1,256]{1,0:T(1,128)S(1)}, u32[]{:S(2)}, u32[]{:S(2)}) collective-permute-start(f32[1,256]{1,0:T(1,128)S(1)} %pair.2.refs_4_), channel_id=1, source_target_pairs={{0,6},{1,7},{2,4},{3,5},{4,2},{5,3},{6,0},{7,1},{8,14},{9,15},{10,... | collective-permute-start | bytes 3080 | tf_op jit(solution)/shard_map/ppermute | solution.py:93
  148.2 24.8 %collective-permute-start.20 = (f32[1,256]{1,0:T(1,128)S(1)}, f32[1,256]{1,0:T(1,128)S(1)}, u32[]{:S(2)}, u32[]{:S(2)}) collective-permute-start(f32[1,256]{1,0:T(1,128)S(1)} %pair.2.refs_4_), channel_id=1, source_target_pairs={{0,4},{1,5},{2,6},{3,7},{4,0},{5,1},{6,2},{7,3},{8,12},{9,13},{10,... | collective-permute-start | bytes 3080 | tf_op jit(solution)/shard_map/ppermute | solution.py:93
  148.9 24.1 %collective-permute-start.19 = (f32[1,256]{1,0:T(1,128)S(1)}, f32[1,256]{1,0:T(1,128)S(1)}, u32[]{:S(2)}, u32[]{:S(2)}) collective-permute-start(f32[1,256]{1,0:T(1,128)S(1)} %pair.2.refs_4_), channel_id=1, source_target_pairs={{0,2},{1,3},{2,0},{3,1},{4,6},{5,7},{6,4},{7,5},{8,10},{9,11},{10,... | collective-permute-start | bytes 3080 | tf_op jit(solution)/shard_map/ppermute | solution.py:93
  169.4 9.4 %collective-permute-start.17 = (bf16[4,4096]{1,0:T(4,128)(2,1)S(1)}, bf16[4,4096]{1,0:T(4,128)(2,1)S(1)}, u32[]{:S(2)}, u32[]{:S(2)}) collective-permute-start(bf16[4,4096]{1,0:T(4,128)(2,1)S(1)} %get-tuple-element.50.refs_0_), channel_id=1, source_target_pairs={{0,24},{8,16},{16,8},{24,0},{1,25},{9,17},{17,9},{25,1},{2,26},{10... | collective-permute-start | bytes 98312 | tf_op jit(solution)/shard_map/ppermute | solution.py:93
  173.0 5.8 %collective-permute-start.16 = (bf16[4,4096]{1,0:T(4,128)(2,1)S(1)}, bf16[4,4096]{1,0:T(4,128)(2,1)S(1)}, u32[]{:S(2)}, u32[]{:S(2)}) collective-permute-start(bf16[4,4096]{1,0:T(4,128)(2,1)S(1)} %get-tuple-element.50.refs_0_), channel_id=1, source_target_pairs={{0,16},{8,24},{16,0},{24,8},{1,17},{9,25},{17,1},{25,9},{2,18},{10... | collective-permute-start | bytes 98312 | tf_op jit(solution)/shard_map/ppermute | solution.py:93
  173.0 5.8 %collective-permute-start.15 = (bf16[4,4096]{1,0:T(4,128)(2,1)S(1)}, bf16[4,4096]{1,0:T(4,128)(2,1)S(1)}, u32[]{:S(2)}, u32[]{:S(2)}) collective-permute-start(bf16[4,4096]{1,0:T(4,128)(2,1)S(1)} %get-tuple-element.50.refs_0_), channel_id=1, source_target_pairs={{0,8},{8,0},{16,24},{24,16},{1,9},{9,1},{17,25},{25,17},{2,10},{10... | collective-permute-start | bytes 98312 | tf_op jit(solution)/shard_map/ppermute | solution.py:93
  179.5 10.5 %copy-start.5 = (bf16[4096,4096]{1,0:T(8,128)(2,1)S(1)}, bf16[4096,4096]{1,0:T(8,128)(2,1)}, u32[]{:S(2)}) copy-start(bf16[4096,4096]{1,0:T(8,128)(2,1)} %copy-done) | copy-start | bytes 100663296
  196.7 2.7 collective-permute-start.22
  199.4 10.5 %copy-start.6 = (bf16[4096,4096]{1,0:T(8,128)(2,1)S(1)}, bf16[4096,4096]{1,0:T(8,128)(2,1)}, u32[]{:S(2)}) copy-start(bf16[4096,4096]{1,0:T(8,128)(2,1)} %copy-done) | copy-start | bytes 100663296
  215.0 9.2 %collective-permute-start.23 = (bf16[256,512]{1,0:T(8,128)(2,1)S(1)}, bf16[256,512]{1,0:T(8,128)(2,1)S(1)}, u32[]{:S(2)}, u32[]{:S(2)}) collective-permute-start(bf16[256,512]{1,0:T(8,128)(2,1)S(1)} %get-tuple-element.57), channel_id=1, source_target_pairs={{0,2},{1,3},{2,0},{3,1},{4,6},{5,7},{6,4},{7,5},{8,10},{9,11},{10,... | collective-permute-start | bytes 786440 | tf_op jit(solution)/shard_map/ppermute | solution.py:93
  215.4 8.9 %collective-permute-start.24 = (bf16[256,512]{1,0:T(8,128)(2,1)S(1)}, bf16[256,512]{1,0:T(8,128)(2,1)S(1)}, u32[]{:S(2)}, u32[]{:S(2)}) collective-permute-start(bf16[256,512]{1,0:T(8,128)(2,1)S(1)} %get-tuple-element.58), channel_id=1, source_target_pairs={{0,4},{1,5},{2,6},{3,7},{4,0},{5,1},{6,2},{7,3},{8,12},{9,13},{10,... | collective-permute-start | bytes 786440 | tf_op jit(solution)/shard_map/ppermute | solution.py:93
  216.8 12.6 %collective-permute-start.25 = (bf16[256,512]{1,0:T(8,128)(2,1)S(1)}, bf16[256,512]{1,0:T(8,128)(2,1)S(1)}, u32[]{:S(2)}, u32[]{:S(2)}) collective-permute-start(bf16[256,512]{1,0:T(8,128)(2,1)S(1)} %get-tuple-element.59), channel_id=1, source_target_pairs={{0,6},{1,7},{2,4},{3,5},{4,2},{5,3},{6,0},{7,1},{8,14},{9,15},{10,... | collective-permute-start | bytes 786440 | tf_op jit(solution)/shard_map/ppermute | solution.py:93
  229.6 10.2 %collective-permute-start.31 = (bf16[256,512]{1,0:T(8,128)(2,1)S(1)}, bf16[256,512]{1,0:T(8,128)(2,1)S(1)}, u32[]{:S(2)}, u32[]{:S(2)}) collective-permute-start(bf16[256,512]{1,0:T(8,128)(2,1)S(1)} %add_pieces.3.refs_0_), channel_id=1, source_target_pairs={{0,6},{1,7},{2,4},{3,5},{4,2},{5,3},{6,0},{7,1},{8,14},{9,15},{10,... | collective-permute-start | bytes 786440 | tf_op jit(solution)/shard_map/ppermute | solution.py:93
  231.4 12.0 %collective-permute-start.29 = (bf16[256,512]{1,0:T(8,128)(2,1)S(1)}, bf16[256,512]{1,0:T(8,128)(2,1)S(1)}, u32[]{:S(2)}, u32[]{:S(2)}) collective-permute-start(bf16[256,512]{1,0:T(8,128)(2,1)S(1)} %add_pieces.3.refs_0_), channel_id=1, source_target_pairs={{0,4},{1,5},{2,6},{3,7},{4,0},{5,1},{6,2},{7,3},{8,12},{9,13},{10,... | collective-permute-start | bytes 786440 | tf_op jit(solution)/shard_map/ppermute | solution.py:93
  232.5 10.9 %collective-permute-start.27 = (bf16[256,512]{1,0:T(8,128)(2,1)S(1)}, bf16[256,512]{1,0:T(8,128)(2,1)S(1)}, u32[]{:S(2)}, u32[]{:S(2)}) collective-permute-start(bf16[256,512]{1,0:T(8,128)(2,1)S(1)} %add_pieces.3.refs_0_), channel_id=1, source_target_pairs={{0,2},{1,3},{2,0},{3,1},{4,6},{5,7},{6,4},{7,5},{8,10},{9,11},{10,... | collective-permute-start | bytes 786440 | tf_op jit(solution)/shard_map/ppermute | solution.py:93
  233.1 27.7 %collective-permute-start.26 = (bf16[256,512]{1,0:T(8,128)(2,1)S(1)}, bf16[256,512]{1,0:T(8,128)(2,1)S(1)}, u32[]{:S(2)}, u32[]{:S(2)}) collective-permute-start(bf16[256,512]{1,0:T(8,128)(2,1)S(1)} %add_pieces.3.refs_0_), channel_id=1, source_target_pairs={{0,1},{1,0},{2,3},{3,2},{4,5},{5,4},{6,7},{7,6},{8,9},{9,8},{10,11... | collective-permute-start | bytes 786440 | tf_op jit(solution)/shard_map/ppermute | solution.py:93
  239.8 21.0 %collective-permute-start.32 = (bf16[256,512]{1,0:T(8,128)(2,1)S(1)}, bf16[256,512]{1,0:T(8,128)(2,1)S(1)}, u32[]{:S(2)}, u32[]{:S(2)}) collective-permute-start(bf16[256,512]{1,0:T(8,128)(2,1)S(1)} %collective-permute-done.31.refs_3_), channel_id=1, source_target_pairs={{0,1},{1,0},{2,3},{3,2},{4,5},{5,4},{6,7},{7,6},{8,9},{9,8},{10,11... | collective-permute-start | bytes 786440 | tf_op jit(solution)/shard_map/ppermute | solution.py:93
  243.3 17.5 %collective-permute-start.30 = (bf16[256,512]{1,0:T(8,128)(2,1)S(1)}, bf16[256,512]{1,0:T(8,128)(2,1)S(1)}, u32[]{:S(2)}, u32[]{:S(2)}) collective-permute-start(bf16[256,512]{1,0:T(8,128)(2,1)S(1)} %collective-permute-done.29.refs_2_), channel_id=1, source_target_pairs={{0,1},{1,0},{2,3},{3,2},{4,5},{5,4},{6,7},{7,6},{8,9},{9,8},{10,11... | collective-permute-start | bytes 786440 | tf_op jit(solution)/shard_map/ppermute | solution.py:93
  243.4 17.5 %collective-permute-start.28 = (bf16[256,512]{1,0:T(8,128)(2,1)S(1)}, bf16[256,512]{1,0:T(8,128)(2,1)S(1)}, u32[]{:S(2)}, u32[]{:S(2)}) collective-permute-start(bf16[256,512]{1,0:T(8,128)(2,1)S(1)} %collective-permute-done.27.refs_1_), channel_id=1, source_target_pairs={{0,1},{1,0},{2,3},{3,2},{4,5},{5,4},{6,7},{7,6},{8,9},{9,8},{10,11... | collective-permute-start | bytes 786440 | tf_op jit(solution)/shard_map/ppermute | solution.py:93
  267.5 1.2 collective-permute-start.33
  268.7 4.5 %collective-permute-start.36 = (f32[1,256]{1,0:T(1,128)S(1)}, f32[1,256]{1,0:T(1,128)S(1)}, u32[]{:S(2)}, u32[]{:S(2)}) collective-permute-start(f32[1,256]{1,0:T(1,128)S(1)} %pair.3.refs_0_), channel_id=1, source_target_pairs={{0,6},{1,7},{2,4},{3,5},{4,2},{5,3},{6,0},{7,1},{8,14},{9,15},{10,... | collective-permute-start | bytes 3080 | tf_op jit(solution)/shard_map/ppermute | solution.py:93
  269.9 3.6 %collective-permute-start.35 = (f32[1,256]{1,0:T(1,128)S(1)}, f32[1,256]{1,0:T(1,128)S(1)}, u32[]{:S(2)}, u32[]{:S(2)}) collective-permute-start(f32[1,256]{1,0:T(1,128)S(1)} %pair.3.refs_0_), channel_id=1, source_target_pairs={{0,4},{1,5},{2,6},{3,7},{4,0},{5,1},{6,2},{7,3},{8,12},{9,13},{10,... | collective-permute-start | bytes 3080 | tf_op jit(solution)/shard_map/ppermute | solution.py:93
  271.4 3.6 %collective-permute-start.34 = (f32[1,256]{1,0:T(1,128)S(1)}, f32[1,256]{1,0:T(1,128)S(1)}, u32[]{:S(2)}, u32[]{:S(2)}) collective-permute-start(f32[1,256]{1,0:T(1,128)S(1)} %pair.3.refs_0_), channel_id=1, source_target_pairs={{0,2},{1,3},{2,0},{3,1},{4,6},{5,7},{6,4},{7,5},{8,10},{9,11},{10,... | collective-permute-start | bytes 3080 | tf_op jit(solution)/shard_map/ppermute | solution.py:93
  (2 other events, 12.7 us)

commit v2 on v1

--- a/solution.py
+++ b/solution.py
@@ -14,26 +14,19 @@
 MIB = 1 << 20
 
 
-def onchip(array):
-    return pltpu.with_memory_space_constraint(array, pltpu.VMEM)
-
-
 def run(body, args, outs, scratch=(), aliases=None, limit=8, name=None):
-    kinds = {"v": pltpu.VMEM, "s": pltpu.SMEM, "a": pl.ANY}
+    kinds = {"v": pltpu.VMEM, "s": pltpu.SMEM, "a": pl.ANY, "h": pltpu.HBM}
     results = pl.pallas_call(
         body,
         in_specs=[pl.BlockSpec(memory_space=kinds[kind]) for _, kind in args],
-        out_specs=[pl.BlockSpec(memory_space=pltpu.VMEM) for _ in outs],
-        out_shape=[
-            pltpu.VMEM(shape, dtype) if kept and name == "relay" else jax.ShapeDtypeStruct(shape, dtype)
-            for shape, dtype, kept in outs
-        ],
+        out_specs=[pl.BlockSpec(memory_space=kinds[out[2] if len(out) > 2 else "v"]) for out in outs],
+        out_shape=[jax.ShapeDtypeStruct(out[0], out[1]) for out in outs],
         scratch_shapes=list(scratch),
         input_output_aliases=aliases or {},
         compiler_params=pltpu.CompilerParams(vmem_limit_bytes=limit * MIB),
         name=name,
     )(*[array for array, _ in args])
-    return [onchip(r) if kept and name == "relay" else r for r, (_, _, kept) in zip(results, outs)]
+    return list(results)
 
 
 def tree_sum(terms):
@@ -121,8 +114,8 @@
     flat_response, *edges1 = run(
         flatten_body,
         [(response.reshape(columns, planes, gz, gy), "v"), (scalars, "a"), (where, "a")],
-        [((columns, cells), f32, True)]
-        + [((columns, part_edge), bf16, False)] * (2 * halo_parts),
+        [((columns, cells), f32)]
+        + [((columns, part_edge), bf16)] * (2 * halo_parts),
         limit=8,
         name="flatten",
     )
@@ -153,10 +146,10 @@
         setup_body,
         [(occupied, "v"), (potential, "v"), (perturbation, "v"), (xc_kernel, "v")],
         [
-            ((orbs, cells), f32, True),
-            ((1, cells), f32, True),
-            ((perts, 1, cells), f32, True),
-            ((1, cells), f32, True),
+            ((orbs, cells), f32),
+            ((1, cells), f32),
+            ((perts, 1, cells), f32),
+            ((1, cells), f32),
         ],
         limit=2,
         name="setup",
@@ -165,40 +158,55 @@
     chunk = min(256, locked)
     chunks = locked // chunk
 
-    def relay_body(source, target, held, sems):
-        def copy(i):
+    def relay_body(source, target, held, ready, in_sems, out_sems):
+        def rows_of(i):
+            return pl.ds(pl.multiple_of(i * chunk, chunk), chunk)
+
+        def fetch(i):
             slot = lax.rem(i, 3)
-            rows = pl.ds(pl.multiple_of(i * chunk, chunk), chunk)
-            return pltpu.make_async_copy(source.at[rows], held.at[slot], sems.at[slot])
-
-        copy(0).start()
-        copy(1).start()
+            return pltpu.make_async_copy(source.at[rows_of(i)], held.at[slot], in_sems.at[slot])
+
+        def flush(i):
+            slot = lax.rem(i, 2)
+            return pltpu.make_async_copy(ready.at[slot], target.at[rows_of(i)], out_sems.at[slot])
+
+        fetch(0).start()
+        fetch(1).start()
 
         def step(i, carry):
             @pl.when(i + 2 < chunks)
             def _():
-                copy(i + 2).start()
-
-            copy(i).wait()
-            slot = lax.rem(i, 3)
-            rows = pl.ds(pl.multiple_of(i * chunk, chunk), chunk)
+                fetch(i + 2).start()
+
+            @pl.when(i >= 2)
+            def _():
+                flush(i - 2).wait()
+
+            fetch(i).wait()
             for x in range(planes):
-                wide = held[slot, :, x].reshape(chunk, gz * gy)
+                wide = held[lax.rem(i, 3), :, x].reshape(chunk, gz * gy)
                 for z in range(gz):
-                    target[rows, col(z, x) : col(z, x) + gy] = wide[:, z * gy : (z + 1) * gy]
+                    ready[lax.rem(i, 2), :, col(z, x) : col(z, x) + gy] = wide[
+                        :, z * gy : (z + 1) * gy
+                    ]
+            flush(i).start()
             return carry
 
         lax.fori_loop(0, chunks, step, 0)
+        flush(chunks - 2).wait()
+        flush(chunks - 1).wait()
 
     (locked_flat,) = run(
         relay_body,
-        [(locked_set, "a")],
-        [((locked, cells), bf16, True)],
+        [(locked_set, "h")],
+        [((locked, cells), bf16, "h")],
         scratch=[
             pltpu.VMEM((3, chunk, planes, gz, gy), bf16),
+            pltpu.VMEM((2, chunk, cells), bf16),
             pltpu.SemaphoreType.DMA((3,)),
+            pltpu.SemaphoreType.DMA((2,)),
         ],
-        limit=7,
+        limit=12,
         name="relay",
     )
 
@@ -239,7 +247,7 @@
         (out,) = run(
             stencil_body,
             [(field, "v"), (flat_potential, "v"), (scalars, "v")],
-            [((columns, cells), f32, True)],
+            [((columns, cells), f32)],
             scratch=[pltpu.VMEM((columns, gy), f32)],
             limit=1,
             name="stencil",
@@ -279,12 +287,25 @@
     def margins(partial, halos, pot):
         low, high = halos[0]
 
-        def other_body(where_ref, part_ref, low_ref, high_ref, occ, pot_ref, lock, rhs, rounded, out):
-            finish_rhs(0, part_ref, low_ref, high_ref, occ, pot_ref, rhs, rounded)
-            start = (1 - where_ref[0]) * half
+        def piece_copies(where_ref, start, lock, buf, sems):
+            copies = []
             for m in range(chips):
                 rows = pl.ds(pl.multiple_of(start + (where_ref[1] ^ m) * piece, piece), piece)
-                out[:, m * piece : (m + 1) * piece] = dot_nt(rounded[...], lock[rows, :]).astype(bf16)
+                copies.append(pltpu.make_async_copy(lock.at[rows], buf.at[m], sems.at[m]))
+            return copies
+
+        piece_scratch = [pltpu.VMEM((chips, piece, cells), bf16), pltpu.SemaphoreType.DMA((chips,))]
+
+        def other_body(
+            where_ref, part_ref, low_ref, high_ref, occ, pot_ref, lock, rhs, rounded, out, buf, sems
+        ):
+            copies = piece_copies(where_ref, (1 - where_ref[0]) * half, lock, buf, sems)
+            for copy in copies:
+                copy.start()
+            finish_rhs(0, part_ref, low_ref, high_ref, occ, pot_ref, rhs, rounded)
+            for m in range(chips):
+                copies[m].wait()
+                out[:, m * piece : (m + 1) * piece] = dot_nt(rounded[...], buf[m]).astype(bf16)
 
         rhs, rounded, other = run(
             other_body,
@@ -295,37 +316,48 @@
                 (high, "v"),
                 (flat_occupied, "v"),
                 (pot, "v"),
-                (locked_flat, "v"),
+                (locked_flat, "h"),
             ],
-            [
-                ((columns, cells), f32, True),
-                ((columns, cells), bf16, True),
-                ((columns, half), bf16, False),
-            ],
+            [((columns, cells), f32), ((columns, cells), bf16), ((columns, half), bf16)],
+            scratch=piece_scratch,
             aliases={1: 0},
-            limit=2,
+            limit=20,
             name="margin_other",
         )
         arrived = swap(other, 1, "dom")
 
-        def own_body(where_ref, rounded_ref, lock, arrived_ref, kept, *sent):
-            start = where_ref[0] * half
-            for m in reversed(range(chips)):
-                rows = pl.ds(pl.multiple_of(start + (where_ref[1] ^ m) * piece, piece), piece)
-                value = dot_nt(rounded_ref[...], lock[rows, :])
-                value = value + arrived_ref[:, m * piece : (m + 1) * piece].astype(f32)
+        def own_body(where_ref, rounded_ref, lock, out, buf, sems):
+            copies = piece_copies(where_ref, where_ref[0] * half, lock, buf, sems)
+            for copy in copies:
+                copy.start()
+            for m in range(chips):
+                copies[m].wait()
+                out[:, m * piece : (m + 1) * piece] = dot_nt(rounded_ref[...], buf[m])
+
+        (own,) = run(
+            own_body,
+            [(where, "s"), (rounded, "v"), (locked_flat, "h")],
+            [((columns, half), f32)],
+            scratch=piece_scratch,
+            limit=20,
+            name="margin_own",
+        )
+
+        def pair_body(own_ref, arrived_ref, kept, *sent):
+            for m in range(chips):
+                cut = slice(m * piece, (m + 1) * piece)
+                value = own_ref[:, cut] + arrived_ref[:, cut].astype(f32)
                 if m == 0:
                     kept[...] = value
                 else:
                     sent[m - 1][...] = value.astype(bf16)
 
         kept, *sent = run(
-            own_body,
-            [(where, "s"), (rounded, "v"), (locked_flat, "v"), (arrived, "v")],
-            [((columns, piece), f32, False)]
-            + [((columns, piece), bf16, False)] * (chips - 1),
-            limit=2,
-            name="margin_own",
+            pair_body,
+            [(own, "v"), (arrived, "v")],
+            [((columns, piece), f32)] + [((columns, piece), bf16)] * (chips - 1),
+            limit=6,
+            name="margin_pair",
         )
         arrivals = [swap(sent[m - 1], 2 * m, "dom") for m in range(1, chips)]
 
@@ -336,7 +368,7 @@
         (mine,) = run(
             add_body,
             [(kept, "v")] + [(r, "v") for r in arrivals],
-            [((columns, piece), bf16, False)],
+            [((columns, piece), bf16)],
             limit=2,
             name="add_pieces",
         )
@@ -348,25 +380,35 @@
             at = pl.ds(pl.multiple_of((where_ref[1] ^ m) * piece, piece), piece)
             held[:, at] = ref[...]
 
+    stripe_scratch = [pltpu.VMEM((gz, half, stripe), bf16), pltpu.SemaphoreType.DMA((gz,))]
+
+    def stripe_copy(start, lock, buf, sems, z):
+        rows = pl.ds(pl.multiple_of(start, half), half)
+        at = pl.ds(pl.multiple_of(z * stripe, stripe), stripe)
+        return pltpu.make_async_copy(lock.at[rows, at], buf.at[z], sems.at[z])
+
     def remove_own(gathered):
         def body(where_ref, *refs):
-            pieces, (lock, acc, held) = refs[:chips], refs[chips:]
+            pieces, (lock, acc, held, buf, sems) = refs[:chips], refs[chips:]
+            start = where_ref[0] * half
+            for z in range(gz):
+                stripe_copy(start, lock, buf, sems, z).start()
             collect(where_ref, pieces, held)
-            rows = pl.ds(pl.multiple_of(where_ref[0] * half, half), half)
 
             def step(z, carry):
                 at = pl.ds(pl.multiple_of(z * stripe, stripe), stripe)
-                acc[:, at] = dot_nn(held[...], lock[rows, at])
+                stripe_copy(start, lock, buf, sems, z).wait()
+                acc[:, at] = dot_nn(held[...], buf[z])
                 return carry
 
             lax.fori_loop(0, gz, step, 0)
 
         (acc,) = run(
             body,
-            [(where, "s")] + [(g, "v") for g in gathered] + [(locked_flat, "v")],
-            [((columns, cells), f32, True)],
-            scratch=[pltpu.VMEM((columns, half), bf16)],
-            limit=2,
+            [(where, "s")] + [(g, "v") for g in gathered] + [(locked_flat, "h")],
+            [((columns, cells), f32)],
+            scratch=[pltpu.VMEM((columns, half), bf16)] + stripe_scratch,
+            limit=22,
             name="remove_own",
         )
         return acc
@@ -385,15 +427,18 @@
             pieces = refs[:chips]
             lock, acc_ref, rhs_ref, field_ref, occ, scal = refs[chips : chips + 6]
             res, mid, low, high, dens, norm = refs[chips + 6 : chips + 12]
-            held, step_rows, lanes = refs[chips + 12 :]
+            held, step_rows, lanes, buf, sems = refs[chips + 12 :]
+            start = (1 - where_ref[0]) * half
+            for z in range(gz):
+                stripe_copy(start, lock, buf, sems, z).start()
             collect(where_ref, pieces, held)
             step_rows[...] = per_row(scal, 1, gy)
             lanes[...] = jnp.zeros_like(lanes)
-            rows = pl.ds(pl.multiple_of((1 - where_ref[0]) * half, half), half)
 
             def step(z, carry):
                 at = pl.ds(pl.multiple_of(z * stripe, stripe), stripe)
-                removed = acc_ref[:, at] + dot_nn(held[...], lock[rows, at])
+                stripe_copy(start, lock, buf, sems, z).wait()
+                removed = acc_ref[:, at] + dot_nn(held[...], buf[z])
                 value = rhs_ref[:, at] - removed
                 res[:, at] = value
                 lanes[...] += squares(value)
@@ -424,7 +469,7 @@
             [(where, "s")]
             + [(g, "v") for g in others]
             + [
-                (locked_flat, "v"),
+                (locked_flat, "h"),
                 (acc, "v"),
                 (rhs, "v"),
                 (field, "v"),
@@ -432,67 +477,62 @@
                 (scalars, "v"),
             ],
             [
-                ((columns, cells), f32, True),
-                ((columns, cells), f32, True),
-                ((columns, gz * 2 * gy), bf16, False),
-                ((columns, gz * 2 * gy), bf16, False),
-                ((perts, cells), bf16, False),
-                ((1, columns), f32, False),
+                ((columns, cells), f32),
+                ((columns, cells), f32),
+                ((columns, gz * 2 * gy), bf16),
+                ((columns, gz * 2 * gy), bf16),
+                ((perts, cells), bf16),
+                ((1, columns), f32),
             ],
             scratch=[
                 pltpu.VMEM((columns, half), bf16),
                 pltpu.VMEM((columns, gy), f32),
                 pltpu.VMEM((columns, gy), f32),
-            ],
+            ]
+            + stripe_scratch,
             aliases={chips + 3: 0, chips + 4: 1},
-            limit=5,
+            limit=26,
             name="first_finish",
         )
 
-    def second_finish(others, acc, rhs):
+    def second_finish(others, acc, rhs, before):
         def body(where_ref, *refs):
             pieces = refs[:chips]
-            lock, acc_ref, rhs_ref, res, norm, held, lanes = refs[chips:]
+            lock, acc_ref, rhs_ref, first, res, norm, held, lanes, buf, sems = refs[chips:]
+            start = (1 - where_ref[0]) * half
+            for z in range(gz):
+                stripe_copy(start, lock, buf, sems, z).start()
             collect(where_ref, pieces, held)
             lanes[...] = jnp.zeros_like(lanes)
-            rows = pl.ds(pl.multiple_of((1 - where_ref[0]) * half, half), half)
 
             def step(z, carry):
                 at = pl.ds(pl.multiple_of(z * stripe, stripe), stripe)
-                removed = acc_ref[:, at] + dot_nn(held[...], lock[rows, at])
+                stripe_copy(start, lock, buf, sems, z).wait()
+                removed = acc_ref[:, at] + dot_nn(held[...], buf[z])
                 value = rhs_ref[:, at] - removed
                 res[:, at] = value
                 lanes[...] += squares(value)
                 return carry
 
             lax.fori_loop(0, gz, step, 0)
-            norm[...] = line_of(lanes[...])
+            norm[0:1, :] = first[...]
+            norm[1:2, :] = line_of(lanes[...])
 
         return run(
             body,
             [(where, "s")]
             + [(g, "v") for g in others]
-            + [(locked_flat, "v"), (acc, "v"), (rhs, "v")],
-            [((columns, cells), f32, True), ((1, columns), f32, False)],
-            scratch=[pltpu.VMEM((columns, half), bf16), pltpu.VMEM((columns, gy), f32)],
+            + [(locked_flat, "h"), (acc, "v"), (rhs, "v"), (before, "v")],
+            [((columns, cells), f32), ((2, columns), f32)],
+            scratch=[pltpu.VMEM((columns, half), bf16), pltpu.VMEM((columns, gy), f32)]
+            + stripe_scratch,
             aliases={chips + 3: 0},
-            limit=2,
+            limit=22,
             name="second_finish",
         )
 
     def across(array, axis):
         return [array] + [swap(array, m, axis) for m in range(1, lax.axis_size(axis))]
-
-    def norm_terms(norm):
-        other = swap(norm, 1, "dom")
-
-        def body(one, two, out):
-            out[...] = one[...] + two[...]
-
-        (pair,) = run(
-            body, [(norm, "v"), (other, "v")], [((1, columns), f32, False)], limit=1, name="pair"
-        )
-        return [pair] + [swap(pair, 2 * m, "dom") for m in range(1, chips)]
 
     partial1 = stencil(flat_response)
     rhs1, gathered1 = margins(partial1, halos1, flat_perturbation)
@@ -503,12 +543,10 @@
     )
     halos2 = halos_of([low_edge, high_edge])
     densities = across(dens, "band")
-    norms1 = norm_terms(norm1)
 
     def potential_body(*refs):
-        parts, squares1 = refs[:bands], refs[bands : bands + chips]
-        pert, xc, flat, native, norm = refs[bands + chips :]
-        norm[...] = tree_sum([r[...] for r in squares1])
+        parts = refs[:bands]
+        pert, xc, flat, native = refs[bands:]
         density = tree_sum([r[...].astype(f32) for r in parts])
         for z in range(gz):
             for x in range(planes):
@@ -518,17 +556,15 @@
                     flat[p, 0:1, cut] = value
                     native[p, x, z : z + 1, :] = value
 
-    flat_rp, response_potential, first_norm = run(
+    flat_rp, response_potential = run(
         potential_body,
         [(d, "v") for d in densities]
-        + [(n, "v") for n in norms1]
         + [(flat_perturbation, "v"), (flat_xc, "v")],
         [
-            ((perts, 1, cells), f32, True),
-            ((perts, planes, gz, gy), f32, False),
-            ((1, columns), f32, True),
+            ((perts, 1, cells), f32),
+            ((perts, planes, gz, gy), f32),
         ],
-        limit=1,
+        limit=3,
         name="potential",
     )
 
@@ -536,13 +572,25 @@
     rhs2, gathered2 = margins(partial2, halos2, flat_rp)
     others2 = [swap(g, 1, "dom") for g in gathered2]
     acc2 = remove_own(gathered2)
-    second_res, norm2 = second_finish(others2, acc2, rhs2)
-    norms2 = norm_terms(norm2)
+    second_res, norms = second_finish(others2, acc2, rhs2, norm1)
+    other_norms = swap(norms, 1, "dom")
+
+    def norm_body(one, two, out):
+        out[...] = one[...] + two[...]
+
+    (pair_norms,) = run(
+        norm_body,
+        [(norms, "v"), (other_norms, "v")],
+        [((2, columns), f32)],
+        limit=1,
+        name="norm_pair",
+    )
+    all_norms = [pair_norms] + [swap(pair_norms, 2 * m, "dom") for m in range(1, chips)]
 
     def final_body(*refs):
-        twos = refs[:chips]
-        one, mid, res1, res2, scal, out, steps, blends = refs[chips:]
-        ratio = tree_sum([r[...] for r in twos]) / one[...]
+        sums = tree_sum([r[...] for r in refs[:chips]])
+        mid, res1, res2, scal, out, steps, blends = refs[chips:]
+        ratio = sums[1:2, :] / sums[0:1, :]
         blend = scal[2:3, :] * ratio
         steps[...] = per_row(scal, 2, gy)
         blends[...] = jnp.broadcast_to(blend, (gy, columns)).T
@@ -563,9 +611,9 @@
 
     (new_response,) = run(
         final_body,
-        [(n, "v") for n in norms2]
-        + [(first_norm, "v"), (middle, "v"), (first_res, "v"), (second_res, "v"), (scalars, "v")],
-        [((columns, planes, gz, gy), f32, False)],
+        [(n, "v") for n in all_norms]
+        + [(middle, "v"), (first_res, "v"), (second_res, "v"), (scalars, "v")],
+        [((columns, planes, gz, gy), f32)],
         scratch=[pltpu.VMEM((columns, gy), f32), pltpu.VMEM((columns, gy), f32)],
         limit=5,
         name="final",

time: 282 us -> 212 us (0.75)
  local copies, waits for them, and re-layouts: 89.3 us -> 15.5 us
  Pallas kernels: 85.7 us -> 104 us
  waiting for transfers between devices: 72.3 us -> 62 us
  starting transfers between devices: 33.2 us -> 29.8 us
    unnamed x26 -> x12, local copies, waits for them, and re-layouts: 87.1 us -> 13.3 us
    ppermute x33 -> x29, waiting for transfers between devices: 72.3 us -> 49.2 us  [swap(): return lax.ppermute(array, axis, [(i, i ^ mask) for i in range(count)])]
    pallas_call x19 -> x20, Pallas kernels: 85.7 us -> 104 us  [run(): pl.pallas_call(body, in_specs=[pl.BlockSpec(memory_space=kinds[kind]) for...]
    ppermute x2, waiting for transfers between devices: 0.01 us -> 12.8 us  [halos_of(): low = lax.ppermute(edges[2 * part + 1], 'dom', ahead)]
    ppermute x33 -> x29, starting transfers between devices: 27 us -> 23.6 us  [swap(): return lax.ppermute(array, axis, [(i, i ^ mask) for i in range(count)])]
  transfers between devices with their start and end apart: 37 -> 33, of which waited for: 17 -> 15; matrix products, arithmetic and copies ran while one was open for 0% -> 0% of each run, Pallas kernels for 14% -> 29%
where the time goes in v2:
time: 212 us
  Pallas kernels  104 us (49%)
  waiting for transfers between devices  62 us (29%)
  starting transfers between devices  29.8 us (14%)
  local copies, waits for them, and re-layouts  15.5 us (7%)
    pallas_call x20, Pallas kernels, run(): pl.pallas_call(body, in_specs=[pl.BlockSpec(memory_space=kinds[kind]) for...  104 us
    ppermute x29, waiting for transfers between devices, swap(): return lax.ppermute(array, axis, [(i, i ^ mask) for i in range(count)])  49.2 us
    ppermute x29, starting transfers between devices, swap(): return lax.ppermute(array, axis, [(i, i ^ mask) for i in range(count)])  23.6 us
    unnamed x12, local copies, waits for them, and re-layouts  13.3 us
    ppermute x2, waiting for transfers between devices, halos_of(): low = lax.ppermute(edges[2 * part + 1], 'dom', ahead)  12.8 us
    ppermute x2, starting transfers between devices, halos_of(): high = lax.ppermute(edges[2 * part], 'dom', behind)  5.61 us
  transfers between devices with their start and end apart: 33, of which 15 were waited for; matrix products, arithmetic and copies ran while one was open for 0% of the time, Pallas kernels for 29%

profile of v2, /device:TPU:0, one launch (start us, length us, event | category | flops | bytes accessed | tf_op | source)
XLA Modules:
  0.0 211.8 jit_solution(1912272119087296823)
XLA Ops:
  0.6 0.8 stack_reshape.6
  1.4 0.8 stack_reshape.7
  2.2 0.7 tile.2
  3.0 2.2 %copy-done.1 = f32[4,64,4,8,128]{4,3,2,1,0:T(8,128)S(1)} copy-done((f32[4,64,4,8,128]{4,3,2,1,0:T(8,128)S(1)}, f32[4,64,4,8,128]{4,3,2,1,0:T(8,128)}, u32[]{:S(2)}) %copy-start.1) | copy-done | bytes 4194328
  5.2 1.3 flatten.1
  7.0 3.0 %collective-permute-start.1 = (bf16[256,2048]{1,0:T(8,128)(2,1)S(1)}, bf16[256,2048]{1,0:T(8,128)(2,1)S(1)}, u32[]{:S(2)}, u32[]{:S(2)}) collective-permute-start(bf16[256,2048]{1,0:T(8,128)(2,1)S(1)} %get-tuple-element.36), channel_id=1, source_target_pairs={{1,0},{2,1},{3,2},{4,3},{5,4},{6,5},{7,6},{0,7},{9,8},{10,9},{11,1... | collective-permute-start | bytes 3145736 | tf_op jit(solution)/shard_map/ppermute | solution.py:127
  10.0 18.1 %relay.1.lock.refs_4_ = bf16[4096,4096]{1,0:T(8,128)(2,1)S(1)} custom-call(bf16[4096,4,8,128]{3,2,1,0:T(8,128)(2,1)} %source.1), custom_call_target="tpu_custom_call" | custom-call | tf_op jit(solution)/shard_map/relay/pallas_call | solution.py:19
  28.1 11.1 %copy-done = bf16[4096,4096]{1,0:T(8,128)(2,1)} copy-done((bf16[4096,4096]{1,0:T(8,128)(2,1)}, bf16[4096,4096]{1,0:T(8,128)(2,1)S(1)}, u32[]{:S(2)}) %copy-start) | copy-done | bytes 33554456
  39.5 5.0 %stencil.2.part_ref = f32[256,4096]{1,0:T(8,128)S(1)} custom-call(f32[256,4096]{1,0:T(8,128)S(1)} %get-tuple-element.33.field.refs_7_, f32[1,4096]{1,0:T(1,128)S(1)} %get-tuple-element.34.pot, f32[3,256]{1,0:T(4,128)S(1)} %pad_maximum_fusion.early.scal.refs_9_.refs_7_), custom_call_target="tpu_custom_call" | custom-call | tf_op jit(solution)/shard_map/stencil/pallas_call | solution.py:19
  44.5 7.9 %margin_other.2 = (f32[256,4096]{1,0:T(8,128)S(1)}, bf16[256,4096]{1,0:T(8,128)(2,1)S(1)}, bf16[256,2048]{1,0:T(8,128)(2,1)S(1)}) custom-call(s32[2]{0:T(128)S(1)} %pad_add_fusion.placed.where_ref, f32[256,4096]{1,0:T(8,128)S(1)} %stencil.2.part_ref, bf16[256,2048]{1,0:T(8,128)(2,1)S(1)} %collective-permute-done.low_ref, ...), custom_call_target="tpu_custom_call", output_to_operand_aliasing={{0}: (1, {})} | custom-call | tf_op jit(solution)/shard_map/margin_other/pallas_call | solution.py:19
  52.5 7.9 %margin_own.2.own_ref = f32[256,2048]{1,0:T(8,128)S(1)} custom-call(s32[2]{0:T(128)S(1)} %pad_add_fusion.placed.where_ref, bf16[256,4096]{1,0:T(8,128)(2,1)S(1)} %get-tuple-element.39.rounded_ref, bf16[4096,4096]{1,0:T(8,128)(2,1)} %copy-done), custom_call_target="tpu_custom_call" | custom-call | tf_op jit(solution)/shard_map/margin_own/pallas_call | solution.py:19
  60.6 1.4 collective-permute-start.3
  62.0 1.5 collective-permute-start.4
  63.5 0.9 collective-permute-start.5
  64.4 5.4 %collective-permute-done.3.refs_1_ = bf16[256,512]{1,0:T(8,128)(2,1)S(1)} collective-permute-done((bf16[256,512]{1,0:T(8,128)(2,1)S(1)}, bf16[256,512]{1,0:T(8,128)(2,1)S(1)}, u32[]{:S(2)}, u32[]{:S(2)}) %collective-permute-start.3) | collective-permute-done | bytes 262176 | tf_op jit(solution)/shard_map/ppermute | solution.py:86
  69.8 5.3 %collective-permute-done.4.refs_2_ = bf16[256,512]{1,0:T(8,128)(2,1)S(1)} collective-permute-done((bf16[256,512]{1,0:T(8,128)(2,1)S(1)}, bf16[256,512]{1,0:T(8,128)(2,1)S(1)}, u32[]{:S(2)}, u32[]{:S(2)}) %collective-permute-start.4) | collective-permute-done | bytes 262176 | tf_op jit(solution)/shard_map/ppermute | solution.py:86
  75.1 1.6 collective-permute-done.5.refs_3_
  76.8 1.8 collective-permute-start.11
  78.9 1.4 collective-permute-start.7
  80.4 6.7 %collective-permute-done.11.refs_3_ = bf16[256,512]{1,0:T(8,128)(2,1)S(1)} collective-permute-done((bf16[256,512]{1,0:T(8,128)(2,1)S(1)}, bf16[256,512]{1,0:T(8,128)(2,1)S(1)}, u32[]{:S(2)}, u32[]{:S(2)}) %collective-permute-start.11) | collective-permute-done | bytes 262176 | tf_op jit(solution)/shard_map/ppermute | solution.py:86
  87.0 4.3 %collective-permute-done.9.refs_2_ = bf16[256,512]{1,0:T(8,128)(2,1)S(1)} collective-permute-done((bf16[256,512]{1,0:T(8,128)(2,1)S(1)}, bf16[256,512]{1,0:T(8,128)(2,1)S(1)}, u32[]{:S(2)}, u32[]{:S(2)}) %collective-permute-start.9) | collective-permute-done | bytes 262176 | tf_op jit(solution)/shard_map/ppermute | solution.py:86
  91.9 7.9 %remove_own.2.refs_5_ = f32[256,4096]{1,0:T(8,128)S(1)} custom-call(s32[2]{0:T(128)S(1)} %pad_add_fusion.placed.where_ref, bf16[256,512]{1,0:T(8,128)(2,1)S(1)} %add_pieces.2.refs_0_, bf16[256,512]{1,0:T(8,128)(2,1)S(1)} %collective-permute-done.7.refs_1_, bf16[256,512]{1,0:T(8,128)(2,1)S(1)} %collective-permute-done.9.refs_2_, ...), custom_call_target="tpu_custom_call" | custom-call | tf_op jit(solution)/shard_map/remove_own/pallas_call | solution.py:19
  99.8 10.0 %first_finish.1 = (f32[256,4096]{1,0:T(8,128)S(1)}, f32[256,4096]{1,0:T(8,128)S(1)}, bf16[256,2048]{1,0:T(8,128)(2,1)S(1)}, bf16[256,2048]{1,0:T(8,128)(2,1)S(1)...) custom-call(s32[2]{0:T(128)S(1)} %pad_add_fusion.placed.where_ref, ...), custom_call_target="tpu_custom_call", output_to_operand_aliasing={{0}: (7, {}), {1}: (8, {})} | custom-call | tf_op jit(solution)/shard_map/first_finish/pallas_call | solution.py:19
  109.8 2.6 %collective-permute-start.14 = (bf16[256,2048]{1,0:T(8,128)(2,1)S(1)}, bf16[256,2048]{1,0:T(8,128)(2,1)S(1)}, u32[]{:S(2)}, u32[]{:S(2)}) collective-permute-start(bf16[256,2048]{1,0:T(8,128)(2,1)S(1)} %get-tuple-element.48), channel_id=1, source_target_pairs={{1,0},{2,1},{3,2},{4,3},{5,4},{6,5},{7,6},{0,7},{9,8},{10,9},{11,1... | collective-permute-start | bytes 3145736 | tf_op jit(solution)/shard_map/ppermute | solution.py:127
  112.4 3.6 %collective-permute-start.17 = (bf16[4,4096]{1,0:T(4,128)(2,1)S(1)}, bf16[4,4096]{1,0:T(4,128)(2,1)S(1)}, u32[]{:S(2)}, u32[]{:S(2)}) collective-permute-start(bf16[4,4096]{1,0:T(4,128)(2,1)S(1)} %get-tuple-element.49.refs_0_), channel_id=1, source_target_pairs={{0,24},{8,16},{16,8},{24,0},{1,25},{9,17},{17,9},{25,1},{2,26},{10... | collective-permute-start | bytes 98312 | tf_op jit(solution)/shard_map/ppermute | solution.py:86
  116.0 0.8 collective-permute-start.15
  116.8 5.0 %stencil.3.part_ref = f32[256,4096]{1,0:T(8,128)S(1)} custom-call(f32[256,4096]{1,0:T(8,128)S(1)} %get-tuple-element.46.field.refs_4_, f32[1,4096]{1,0:T(1,128)S(1)} %get-tuple-element.34.pot, f32[3,256]{1,0:T(4,128)S(1)} %pad_maximum_fusion.early.scal.refs_9_.refs_7_), custom_call_target="tpu_custom_call" | custom-call | tf_op jit(solution)/shard_map/stencil/pallas_call | solution.py:19
  121.9 0.7 potential.1
  122.6 12.8 %collective-permute-done.13.low_ref = bf16[256,2048]{1,0:T(8,128)(2,1)S(1)} collective-permute-done((bf16[256,2048]{1,0:T(8,128)(2,1)S(1)}, bf16[256,2048]{1,0:T(8,128)(2,1)S(1)}, u32[]{:S(2)}, u32[]{:S(2)}) %collective-permute-start.13) | collective-permute-done | bytes 1048608 | tf_op jit(solution)/shard_map/ppermute | solution.py:126
  135.3 7.9 %margin_other.3 = (f32[256,4096]{1,0:T(8,128)S(1)}, bf16[256,4096]{1,0:T(8,128)(2,1)S(1)}, bf16[256,2048]{1,0:T(8,128)(2,1)S(1)}) custom-call(s32[2]{0:T(128)S(1)} %pad_add_fusion.placed.where_ref, f32[256,4096]{1,0:T(8,128)S(1)} %stencil.3.part_ref, bf16[256,2048]{1,0:T(8,128)(2,1)S(1)} %collective-permute-done.13.low_ref, ...), custom_call_target="tpu_custom_call", output_to_operand_aliasing={{0}: (1, {})} | custom-call | tf_op jit(solution)/shard_map/margin_other/pallas_call | solution.py:19
  143.3 7.9 %margin_own.3.own_ref = f32[256,2048]{1,0:T(8,128)S(1)} custom-call(s32[2]{0:T(128)S(1)} %pad_add_fusion.placed.where_ref, bf16[256,4096]{1,0:T(8,128)(2,1)S(1)} %get-tuple-element.52.rounded_ref, bf16[4096,4096]{1,0:T(8,128)(2,1)} %copy-done), custom_call_target="tpu_custom_call" | custom-call | tf_op jit(solution)/shard_map/margin_own/pallas_call | solution.py:19
  151.5 1.2 collective-permute-start.19
  153.3 1.7 collective-permute-start.21
  155.1 5.6 %collective-permute-done.19.refs_1_ = bf16[256,512]{1,0:T(8,128)(2,1)S(1)} collective-permute-done((bf16[256,512]{1,0:T(8,128)(2,1)S(1)}, bf16[256,512]{1,0:T(8,128)(2,1)S(1)}, u32[]{:S(2)}, u32[]{:S(2)}) %collective-permute-start.19) | collective-permute-done | bytes 262176 | tf_op jit(solution)/shard_map/ppermute | solution.py:86
  160.7 5.6 %collective-permute-done.20.refs_2_ = bf16[256,512]{1,0:T(8,128)(2,1)S(1)} collective-permute-done((bf16[256,512]{1,0:T(8,128)(2,1)S(1)}, bf16[256,512]{1,0:T(8,128)(2,1)S(1)}, u32[]{:S(2)}, u32[]{:S(2)}) %collective-permute-start.20) | collective-permute-done | bytes 262176 | tf_op jit(solution)/shard_map/ppermute | solution.py:86
  166.4 1.5 collective-permute-start.27
  168.0 1.3 collective-permute-start.25
  169.3 0.7 collective-permute-start.23
  170.0 6.7 %collective-permute-done.27.refs_3_ = bf16[256,512]{1,0:T(8,128)(2,1)S(1)} collective-permute-done((bf16[256,512]{1,0:T(8,128)(2,1)S(1)}, bf16[256,512]{1,0:T(8,128)(2,1)S(1)}, u32[]{:S(2)}, u32[]{:S(2)}) %collective-permute-start.27) | collective-permute-done | bytes 262176 | tf_op jit(solution)/shard_map/ppermute | solution.py:86
  176.7 3.5 %collective-permute-done.25.refs_2_ = bf16[256,512]{1,0:T(8,128)(2,1)S(1)} collective-permute-done((bf16[256,512]{1,0:T(8,128)(2,1)S(1)}, bf16[256,512]{1,0:T(8,128)(2,1)S(1)}, u32[]{:S(2)}, u32[]{:S(2)}) %collective-permute-start.25) | collective-permute-done | bytes 262176 | tf_op jit(solution)/shard_map/ppermute | solution.py:86
  180.7 7.9 %remove_own.3.refs_5_ = f32[256,4096]{1,0:T(8,128)S(1)} custom-call(s32[2]{0:T(128)S(1)} %pad_add_fusion.placed.where_ref, bf16[256,512]{1,0:T(8,128)(2,1)S(1)} %add_pieces.3.refs_0_, bf16[256,512]{1,0:T(8,128)(2,1)S(1)} %collective-permute-done.23.refs_1_, bf16[256,512]{1,0:T(8,128)(2,1)S(1)} %collective-permute-done.25.refs_2_, ...), custom_call_target="tpu_custom_call" | custom-call | tf_op jit(solution)/shard_map/remove_own/pallas_call | solution.py:19
  188.6 8.2 %second_finish.1 = (f32[256,4096]{1,0:T(8,128)S(1)}, f32[2,256]{1,0:T(2,128)S(1)}) custom-call(s32[2]{0:T(128)S(1)} %pad_add_fusion.placed.where_ref, bf16[256,512]{1,0:T(8,128)(2,1)S(1)} %collective-permute-done.22.refs_0_, bf16[256,512]{1,0:T(8,128)(2,1)S(1)} %collective-permute-done.24.refs_1_, ...), custom_call_target="tpu_custom_call", output_to_operand_aliasing={{0}: (7, {})} | custom-call | tf_op jit(solution)/shard_map/second_finish/pallas_call | solution.py:19
  197.3 0.8 collective-permute-done.29.two
  198.1 1.4 collective-permute-start.32
  199.5 1.8 collective-permute-start.31
  201.6 1.0 collective-permute-done.32.refs_3_
  203.1 1.8 collective-permute-done.30.refs_1_
  204.9 6.9 %final.1 = f32[256,4,8,128]{3,2,1,0:T(8,128)} custom-call(f32[2,256]{1,0:T(2,128)S(1)} %norm_pair.1.refs_0_, f32[2,256]{1,0:T(2,128)S(1)} %collective-permute-done.30.refs_1_, f32[2,256]{1,0:T(2,128)S(1)} %collective-permute-done.31.refs_2_, f32[2,256]{1,0:T(2,128)S(1)} %collective-permute-done.32.refs_3_, f32[256,4096]{1,0:T(8,128)S(1)} %get-tuple-element.46.field.refs_4_, ...), custom_call_target="tpu_custom_call" | custom-call | tf_op jit(solution)/shard_map/final/pallas_call | solution.py:19
  (56 shorter events, 5.2 us)
Async XLA Ops:
  3.0 2.2 %copy-start.1 = (f32[4,64,4,8,128]{4,3,2,1,0:T(8,128)S(1)}, f32[4,64,4,8,128]{4,3,2,1,0:T(8,128)}, u32[]{:S(2)}) copy-start(f32[4,64,4,8,128]{4,3,2,1,0:T(8,128)} %param.9) | copy-start | bytes 12582916
  6.5 38.0 %collective-permute-start = (bf16[256,2048]{1,0:T(8,128)(2,1)S(1)}, bf16[256,2048]{1,0:T(8,128)(2,1)S(1)}, u32[]{:S(2)}, u32[]{:S(2)}) collective-permute-start(bf16[256,2048]{1,0:T(8,128)(2,1)S(1)} %get-tuple-element.35), channel_id=1, source_target_pairs={{0,1},{1,2},{2,3},{3,4},{4,5},{5,6},{6,7},{7,0},{8,9},{9,10},{10,1... | collective-permute-start | bytes 3145736 | tf_op jit(solution)/shard_map/ppermute | solution.py:126
  7.0 32.2 %copy-start.2 = (f32[64,4,8,128]{3,2,1,0:T(8,128)S(1)}, f32[64,4,8,128]{3,2,1,0:T(8,128)}, u32[]{:S(2)}) copy-start(f32[64,4,8,128]{3,2,1,0:T(8,128)} %occ.1) | copy-start | bytes 3145732
  7.0 32.2 %copy-start.3 = (f32[4,4,8,128]{3,2,1,0:T(8,128)S(1)}, f32[4,4,8,128]{3,2,1,0:T(8,128)}, u32[]{:S(2)}) copy-start(f32[4,4,8,128]{3,2,1,0:T(8,128)} %pert.1) | copy-start | bytes 196612
  7.0 32.2 %copy-start.4 = (f32[4,8,128]{2,1,0:T(8,128)S(1)}, f32[4,8,128]{2,1,0:T(8,128)}, u32[]{:S(2)}) copy-start(f32[4,8,128]{2,1,0:T(8,128)} %pot.1) | copy-start | bytes 49156
  7.0 32.2 %copy-start.5 = (f32[4,8,128]{2,1,0:T(8,128)S(1)}, f32[4,8,128]{2,1,0:T(8,128)}, u32[]{:S(2)}) copy-start(f32[4,8,128]{2,1,0:T(8,128)} %xc.1) | copy-start | bytes 49156
  7.0 37.5 %collective-permute-start.1 = (bf16[256,2048]{1,0:T(8,128)(2,1)S(1)}, bf16[256,2048]{1,0:T(8,128)(2,1)S(1)}, u32[]{:S(2)}, u32[]{:S(2)}) collective-permute-start(bf16[256,2048]{1,0:T(8,128)(2,1)S(1)} %get-tuple-element.36), channel_id=1, source_target_pairs={{1,0},{2,1},{3,2},{4,3},{5,4},{6,5},{7,6},{0,7},{9,8},{10,9},{11,1... | collective-permute-start | bytes 3145736 | tf_op jit(solution)/shard_map/ppermute | solution.py:127
  28.1 11.1 %copy-start = (bf16[4096,4096]{1,0:T(8,128)(2,1)}, bf16[4096,4096]{1,0:T(8,128)(2,1)S(1)}, u32[]{:S(2)}) copy-start(bf16[4096,4096]{1,0:T(8,128)(2,1)S(1)} %relay.1.lock.refs_4_) | copy-start | bytes 100663296
  52.4 8.0 %collective-permute-start.2 = (bf16[256,2048]{1,0:T(8,128)(2,1)S(1)}, bf16[256,2048]{1,0:T(8,128)(2,1)S(1)}, u32[]{:S(2)}, u32[]{:S(2)}) collective-permute-start(bf16[256,2048]{1,0:T(8,128)(2,1)S(1)} %get-tuple-element.40), channel_id=1, source_target_pairs={{0,1},{1,0},{2,3},{3,2},{4,5},{5,4},{6,7},{7,6},{8,9},{9,8},{10,11... | collective-permute-start | bytes 3145736 | tf_op jit(solution)/shard_map/ppermute | solution.py:86
  60.6 9.2 %collective-permute-start.3 = (bf16[256,512]{1,0:T(8,128)(2,1)S(1)}, bf16[256,512]{1,0:T(8,128)(2,1)S(1)}, u32[]{:S(2)}, u32[]{:S(2)}) collective-permute-start(bf16[256,512]{1,0:T(8,128)(2,1)S(1)} %get-tuple-element.42), channel_id=1, source_target_pairs={{0,2},{1,3},{2,0},{3,1},{4,6},{5,7},{6,4},{7,5},{8,10},{9,11},{10,... | collective-permute-start | bytes 786440 | tf_op jit(solution)/shard_map/ppermute | solution.py:86
  62.0 13.1 %collective-permute-start.4 = (bf16[256,512]{1,0:T(8,128)(2,1)S(1)}, bf16[256,512]{1,0:T(8,128)(2,1)S(1)}, u32[]{:S(2)}, u32[]{:S(2)}) collective-permute-start(bf16[256,512]{1,0:T(8,128)(2,1)S(1)} %get-tuple-element.43), channel_id=1, source_target_pairs={{0,4},{1,5},{2,6},{3,7},{4,0},{5,1},{6,2},{7,3},{8,12},{9,13},{10,... | collective-permute-start | bytes 786440 | tf_op jit(solution)/shard_map/ppermute | solution.py:86
  63.5 13.2 %collective-permute-start.5 = (bf16[256,512]{1,0:T(8,128)(2,1)S(1)}, bf16[256,512]{1,0:T(8,128)(2,1)S(1)}, u32[]{:S(2)}, u32[]{:S(2)}) collective-permute-start(bf16[256,512]{1,0:T(8,128)(2,1)S(1)} %get-tuple-element.44), channel_id=1, source_target_pairs={{0,6},{1,7},{2,4},{3,5},{4,2},{5,3},{6,0},{7,1},{8,14},{9,15},{10,... | collective-permute-start | bytes 786440 | tf_op jit(solution)/shard_map/ppermute | solution.py:86
  76.8 10.2 %collective-permute-start.11 = (bf16[256,512]{1,0:T(8,128)(2,1)S(1)}, bf16[256,512]{1,0:T(8,128)(2,1)S(1)}, u32[]{:S(2)}, u32[]{:S(2)}) collective-permute-start(bf16[256,512]{1,0:T(8,128)(2,1)S(1)} %add_pieces.2.refs_0_), channel_id=1, source_target_pairs={{0,6},{1,7},{2,4},{3,5},{4,2},{5,3},{6,0},{7,1},{8,14},{9,15},{10,... | collective-permute-start | bytes 786440 | tf_op jit(solution)/shard_map/ppermute | solution.py:86
  78.6 12.7 %collective-permute-start.9 = (bf16[256,512]{1,0:T(8,128)(2,1)S(1)}, bf16[256,512]{1,0:T(8,128)(2,1)S(1)}, u32[]{:S(2)}, u32[]{:S(2)}) collective-permute-start(bf16[256,512]{1,0:T(8,128)(2,1)S(1)} %add_pieces.2.refs_0_), channel_id=1, source_target_pairs={{0,4},{1,5},{2,6},{3,7},{4,0},{5,1},{6,2},{7,3},{8,12},{9,13},{10,... | collective-permute-start | bytes 786440 | tf_op jit(solution)/shard_map/ppermute | solution.py:86
  78.9 12.4 %collective-permute-start.7 = (bf16[256,512]{1,0:T(8,128)(2,1)S(1)}, bf16[256,512]{1,0:T(8,128)(2,1)S(1)}, u32[]{:S(2)}, u32[]{:S(2)}) collective-permute-start(bf16[256,512]{1,0:T(8,128)(2,1)S(1)} %add_pieces.2.refs_0_), channel_id=1, source_target_pairs={{0,2},{1,3},{2,0},{3,1},{4,6},{5,7},{6,4},{7,5},{8,10},{9,11},{10,... | collective-permute-start | bytes 786440 | tf_op jit(solution)/shard_map/ppermute | solution.py:86
  80.4 19.3 %collective-permute-start.6 = (bf16[256,512]{1,0:T(8,128)(2,1)S(1)}, bf16[256,512]{1,0:T(8,128)(2,1)S(1)}, u32[]{:S(2)}, u32[]{:S(2)}) collective-permute-start(bf16[256,512]{1,0:T(8,128)(2,1)S(1)} %add_pieces.2.refs_0_), channel_id=1, source_target_pairs={{0,1},{1,0},{2,3},{3,2},{4,5},{5,4},{6,7},{7,6},{8,9},{9,8},{10,11... | collective-permute-start | bytes 786440 | tf_op jit(solution)/shard_map/ppermute | solution.py:86
  87.0 12.7 %collective-permute-start.12 = (bf16[256,512]{1,0:T(8,128)(2,1)S(1)}, bf16[256,512]{1,0:T(8,128)(2,1)S(1)}, u32[]{:S(2)}, u32[]{:S(2)}) collective-permute-start(bf16[256,512]{1,0:T(8,128)(2,1)S(1)} %collective-permute-done.11.refs_3_), channel_id=1, source_target_pairs={{0,1},{1,0},{2,3},{3,2},{4,5},{5,4},{6,7},{7,6},{8,9},{9,8},{10,11... | collective-permute-start | bytes 786440 | tf_op jit(solution)/shard_map/ppermute | solution.py:86
  91.3 8.4 %collective-permute-start.10 = (bf16[256,512]{1,0:T(8,128)(2,1)S(1)}, bf16[256,512]{1,0:T(8,128)(2,1)S(1)}, u32[]{:S(2)}, u32[]{:S(2)}) collective-permute-start(bf16[256,512]{1,0:T(8,128)(2,1)S(1)} %collective-permute-done.9.refs_2_), channel_id=1, source_target_pairs={{0,1},{1,0},{2,3},{3,2},{4,5},{5,4},{6,7},{7,6},{8,9},{9,8},{10,11... | collective-permute-start | bytes 786440 | tf_op jit(solution)/shard_map/ppermute | solution.py:86
  91.4 8.4 %collective-permute-start.8 = (bf16[256,512]{1,0:T(8,128)(2,1)S(1)}, bf16[256,512]{1,0:T(8,128)(2,1)S(1)}, u32[]{:S(2)}, u32[]{:S(2)}) collective-permute-start(bf16[256,512]{1,0:T(8,128)(2,1)S(1)} %collective-permute-done.7.refs_1_), channel_id=1, source_target_pairs={{0,1},{1,0},{2,3},{3,2},{4,5},{5,4},{6,7},{7,6},{8,9},{9,8},{10,11... | collective-permute-start | bytes 786440 | tf_op jit(solution)/shard_map/ppermute | solution.py:86
  109.7 25.6 %collective-permute-start.13 = (bf16[256,2048]{1,0:T(8,128)(2,1)S(1)}, bf16[256,2048]{1,0:T(8,128)(2,1)S(1)}, u32[]{:S(2)}, u32[]{:S(2)}) collective-permute-start(bf16[256,2048]{1,0:T(8,128)(2,1)S(1)} %get-tuple-element.47), channel_id=1, source_target_pairs={{0,1},{1,2},{2,3},{3,4},{4,5},{5,6},{6,7},{7,0},{8,9},{9,10},{10,1... | collective-permute-start | bytes 3145736 | tf_op jit(solution)/shard_map/ppermute | solution.py:126
  109.8 25.5 %collective-permute-start.14 = (bf16[256,2048]{1,0:T(8,128)(2,1)S(1)}, bf16[256,2048]{1,0:T(8,128)(2,1)S(1)}, u32[]{:S(2)}, u32[]{:S(2)}) collective-permute-start(bf16[256,2048]{1,0:T(8,128)(2,1)S(1)} %get-tuple-element.48), channel_id=1, source_target_pairs={{1,0},{2,1},{3,2},{4,3},{5,4},{6,5},{7,6},{0,7},{9,8},{10,9},{11,1... | collective-permute-start | bytes 3145736 | tf_op jit(solution)/shard_map/ppermute | solution.py:127
  112.4 9.4 %collective-permute-start.17 = (bf16[4,4096]{1,0:T(4,128)(2,1)S(1)}, bf16[4,4096]{1,0:T(4,128)(2,1)S(1)}, u32[]{:S(2)}, u32[]{:S(2)}) collective-permute-start(bf16[4,4096]{1,0:T(4,128)(2,1)S(1)} %get-tuple-element.49.refs_0_), channel_id=1, source_target_pairs={{0,24},{8,16},{16,8},{24,0},{1,25},{9,17},{17,9},{25,1},{2,26},{10... | collective-permute-start | bytes 98312 | tf_op jit(solution)/shard_map/ppermute | solution.py:86
  116.0 5.8 %collective-permute-start.16 = (bf16[4,4096]{1,0:T(4,128)(2,1)S(1)}, bf16[4,4096]{1,0:T(4,128)(2,1)S(1)}, u32[]{:S(2)}, u32[]{:S(2)}) collective-permute-start(bf16[4,4096]{1,0:T(4,128)(2,1)S(1)} %get-tuple-element.49.refs_0_), channel_id=1, source_target_pairs={{0,16},{8,24},{16,0},{24,8},{1,17},{9,25},{17,1},{25,9},{2,18},{10... | collective-permute-start | bytes 98312 | tf_op jit(solution)/shard_map/ppermute | solution.py:86
  116.0 5.8 %collective-permute-start.15 = (bf16[4,4096]{1,0:T(4,128)(2,1)S(1)}, bf16[4,4096]{1,0:T(4,128)(2,1)S(1)}, u32[]{:S(2)}, u32[]{:S(2)}) collective-permute-start(bf16[4,4096]{1,0:T(4,128)(2,1)S(1)} %get-tuple-element.49.refs_0_), channel_id=1, source_target_pairs={{0,8},{8,0},{16,24},{24,16},{1,9},{9,1},{17,25},{25,17},{2,10},{10... | collective-permute-start | bytes 98312 | tf_op jit(solution)/shard_map/ppermute | solution.py:86
  143.3 8.0 %collective-permute-start.18 = (bf16[256,2048]{1,0:T(8,128)(2,1)S(1)}, bf16[256,2048]{1,0:T(8,128)(2,1)S(1)}, u32[]{:S(2)}, u32[]{:S(2)}) collective-permute-start(bf16[256,2048]{1,0:T(8,128)(2,1)S(1)} %get-tuple-element.53), channel_id=1, source_target_pairs={{0,1},{1,0},{2,3},{3,2},{4,5},{5,4},{6,7},{7,6},{8,9},{9,8},{10,11... | collective-permute-start | bytes 3145736 | tf_op jit(solution)/shard_map/ppermute | solution.py:86
  151.5 9.2 %collective-permute-start.19 = (bf16[256,512]{1,0:T(8,128)(2,1)S(1)}, bf16[256,512]{1,0:T(8,128)(2,1)S(1)}, u32[]{:S(2)}, u32[]{:S(2)}) collective-permute-start(bf16[256,512]{1,0:T(8,128)(2,1)S(1)} %get-tuple-element.55), channel_id=1, source_target_pairs={{0,2},{1,3},{2,0},{3,1},{4,6},{5,7},{6,4},{7,5},{8,10},{9,11},{10,... | collective-permute-start | bytes 786440 | tf_op jit(solution)/shard_map/ppermute | solution.py:86
  152.7 13.6 %collective-permute-start.20 = (bf16[256,512]{1,0:T(8,128)(2,1)S(1)}, bf16[256,512]{1,0:T(8,128)(2,1)S(1)}, u32[]{:S(2)}, u32[]{:S(2)}) collective-permute-start(bf16[256,512]{1,0:T(8,128)(2,1)S(1)} %get-tuple-element.56), channel_id=1, source_target_pairs={{0,4},{1,5},{2,6},{3,7},{4,0},{5,1},{6,2},{7,3},{8,12},{9,13},{10,... | collective-permute-start | bytes 786440 | tf_op jit(solution)/shard_map/ppermute | solution.py:86
  153.3 12.9 %collective-permute-start.21 = (bf16[256,512]{1,0:T(8,128)(2,1)S(1)}, bf16[256,512]{1,0:T(8,128)(2,1)S(1)}, u32[]{:S(2)}, u32[]{:S(2)}) collective-permute-start(bf16[256,512]{1,0:T(8,128)(2,1)S(1)} %get-tuple-element.57), channel_id=1, source_target_pairs={{0,6},{1,7},{2,4},{3,5},{4,2},{5,3},{6,0},{7,1},{8,14},{9,15},{10,... | collective-permute-start | bytes 786440 | tf_op jit(solution)/shard_map/ppermute | solution.py:86
  166.4 10.2 %collective-permute-start.27 = (bf16[256,512]{1,0:T(8,128)(2,1)S(1)}, bf16[256,512]{1,0:T(8,128)(2,1)S(1)}, u32[]{:S(2)}, u32[]{:S(2)}) collective-permute-start(bf16[256,512]{1,0:T(8,128)(2,1)S(1)} %add_pieces.3.refs_0_), channel_id=1, source_target_pairs={{0,6},{1,7},{2,4},{3,5},{4,2},{5,3},{6,0},{7,1},{8,14},{9,15},{10,... | collective-permute-start | bytes 786440 | tf_op jit(solution)/shard_map/ppermute | solution.py:86
  168.0 12.2 %collective-permute-start.25 = (bf16[256,512]{1,0:T(8,128)(2,1)S(1)}, bf16[256,512]{1,0:T(8,128)(2,1)S(1)}, u32[]{:S(2)}, u32[]{:S(2)}) collective-permute-start(bf16[256,512]{1,0:T(8,128)(2,1)S(1)} %add_pieces.3.refs_0_), channel_id=1, source_target_pairs={{0,4},{1,5},{2,6},{3,7},{4,0},{5,1},{6,2},{7,3},{8,12},{9,13},{10,... | collective-permute-start | bytes 786440 | tf_op jit(solution)/shard_map/ppermute | solution.py:86
  169.3 11.3 %collective-permute-start.23 = (bf16[256,512]{1,0:T(8,128)(2,1)S(1)}, bf16[256,512]{1,0:T(8,128)(2,1)S(1)}, u32[]{:S(2)}, u32[]{:S(2)}) collective-permute-start(bf16[256,512]{1,0:T(8,128)(2,1)S(1)} %add_pieces.3.refs_0_), channel_id=1, source_target_pairs={{0,2},{1,3},{2,0},{3,1},{4,6},{5,7},{6,4},{7,5},{8,10},{9,11},{10,... | collective-permute-start | bytes 786440 | tf_op jit(solution)/shard_map/ppermute | solution.py:86
  170.0 18.6 %collective-permute-start.22 = (bf16[256,512]{1,0:T(8,128)(2,1)S(1)}, bf16[256,512]{1,0:T(8,128)(2,1)S(1)}, u32[]{:S(2)}, u32[]{:S(2)}) collective-permute-start(bf16[256,512]{1,0:T(8,128)(2,1)S(1)} %add_pieces.3.refs_0_), channel_id=1, source_target_pairs={{0,1},{1,0},{2,3},{3,2},{4,5},{5,4},{6,7},{7,6},{8,9},{9,8},{10,11... | collective-permute-start | bytes 786440 | tf_op jit(solution)/shard_map/ppermute | solution.py:86
  176.7 11.9 %collective-permute-start.28 = (bf16[256,512]{1,0:T(8,128)(2,1)S(1)}, bf16[256,512]{1,0:T(8,128)(2,1)S(1)}, u32[]{:S(2)}, u32[]{:S(2)}) collective-permute-start(bf16[256,512]{1,0:T(8,128)(2,1)S(1)} %collective-permute-done.27.refs_3_), channel_id=1, source_target_pairs={{0,1},{1,0},{2,3},{3,2},{4,5},{5,4},{6,7},{7,6},{8,9},{9,8},{10,11... | collective-permute-start | bytes 786440 | tf_op jit(solution)/shard_map/ppermute | solution.py:86
  180.2 8.4 %collective-permute-start.26 = (bf16[256,512]{1,0:T(8,128)(2,1)S(1)}, bf16[256,512]{1,0:T(8,128)(2,1)S(1)}, u32[]{:S(2)}, u32[]{:S(2)}) collective-permute-start(bf16[256,512]{1,0:T(8,128)(2,1)S(1)} %collective-permute-done.25.refs_2_), channel_id=1, source_target_pairs={{0,1},{1,0},{2,3},{3,2},{4,5},{5,4},{6,7},{7,6},{8,9},{9,8},{10,11... | collective-permute-start | bytes 786440 | tf_op jit(solution)/shard_map/ppermute | solution.py:86
  180.6 8.0 %collective-permute-start.24 = (bf16[256,512]{1,0:T(8,128)(2,1)S(1)}, bf16[256,512]{1,0:T(8,128)(2,1)S(1)}, u32[]{:S(2)}, u32[]{:S(2)}) collective-permute-start(bf16[256,512]{1,0:T(8,128)(2,1)S(1)} %collective-permute-done.23.refs_1_), channel_id=1, source_target_pairs={{0,1},{1,0},{2,3},{3,2},{4,5},{5,4},{6,7},{7,6},{8,9},{9,8},{10,11... | collective-permute-start | bytes 786440 | tf_op jit(solution)/shard_map/ppermute | solution.py:86
  196.8 1.3 collective-permute-start.29
  198.1 4.5 %collective-permute-start.32 = (f32[2,256]{1,0:T(2,128)S(1)}, f32[2,256]{1,0:T(2,128)S(1)}, u32[]{:S(2)}, u32[]{:S(2)}) collective-permute-start(f32[2,256]{1,0:T(2,128)S(1)} %norm_pair.1.refs_0_), channel_id=1, source_target_pairs={{0,6},{1,7},{2,4},{3,5},{4,2},{5,3},{6,0},{7,1},{8,14},{9,15},{10,... | collective-permute-start | bytes 6152 | tf_op jit(solution)/shard_map/ppermute | solution.py:86
  199.5 3.6 %collective-permute-start.31 = (f32[2,256]{1,0:T(2,128)S(1)}, f32[2,256]{1,0:T(2,128)S(1)}, u32[]{:S(2)}, u32[]{:S(2)}) collective-permute-start(f32[2,256]{1,0:T(2,128)S(1)} %norm_pair.1.refs_0_), channel_id=1, source_target_pairs={{0,4},{1,5},{2,6},{3,7},{4,0},{5,1},{6,2},{7,3},{8,12},{9,13},{10,... | collective-permute-start | bytes 6152 | tf_op jit(solution)/shard_map/ppermute | solution.py:86
  201.3 3.6 %collective-permute-start.30 = (f32[2,256]{1,0:T(2,128)S(1)}, f32[2,256]{1,0:T(2,128)S(1)}, u32[]{:S(2)}, u32[]{:S(2)}) collective-permute-start(f32[2,256]{1,0:T(2,128)S(1)} %norm_pair.1.refs_0_), channel_id=1, source_target_pairs={{0,2},{1,3},{2,0},{3,1},{4,6},{5,7},{6,4},{7,5},{8,10},{9,11},{10,... | collective-permute-start | bytes 6152 | tf_op jit(solution)/shard_map/ppermute | solution.py:86

commit v3 on v2

--- a/solution.py
+++ b/solution.py
@@ -10,7 +10,6 @@
 near_half = 2.0 / 3.0
 far_half = -1.0 / 24.0
 centre_half = -3.75
-halo_parts = 1
 MIB = 1 << 20
 
 
@@ -20,7 +19,10 @@
         body,
         in_specs=[pl.BlockSpec(memory_space=kinds[kind]) for _, kind in args],
         out_specs=[pl.BlockSpec(memory_space=kinds[out[2] if len(out) > 2 else "v"]) for out in outs],
-        out_shape=[jax.ShapeDtypeStruct(out[0], out[1]) for out in outs],
+        out_shape=[
+            pltpu.HBM(out[0], out[1]) if out[2:] == ("h",) else jax.ShapeDtypeStruct(out[0], out[1])
+            for out in outs
+        ],
         scratch_shapes=list(scratch),
         input_output_aliases=aliases or {},
         compiler_params=pltpu.CompilerParams(vmem_limit_bytes=limit * MIB),
@@ -69,7 +71,7 @@
     chips = doms // 2
     half = locked // 2
     piece = half // chips
-    part_z = gz // halo_parts
+    part_z = gz // 2
     part_cells = part_z * stripe
     part_edge = part_z * 2 * gy
     position = lax.axis_index("dom")
@@ -100,13 +102,12 @@
                 for z in range(gz):
                     value = wide[:, z * gy : (z + 1) * gy]
                     flat[rows, col(z, x) : col(z, x) + gy] = value
-                    part, inner = divmod(z, part_z)
                     if x < 2:
-                        at = edge(inner, x)
-                        edges[2 * part][rows, at : at + gy] = value.astype(bf16)
+                        at = edge(z, x)
+                        edges[0][rows, at : at + gy] = value.astype(bf16)
                     if x >= planes - 2:
-                        at = edge(inner, x - planes + 2)
-                        edges[2 * part + 1][rows, at : at + gy] = value.astype(bf16)
+                        at = edge(z, x - planes + 2)
+                        edges[1][rows, at : at + gy] = value.astype(bf16)
             return carry
 
         lax.fori_loop(0, source.shape[0] // orbs, rows_step, 0)
@@ -115,20 +116,15 @@
         flatten_body,
         [(response.reshape(columns, planes, gz, gy), "v"), (scalars, "a"), (where, "a")],
         [((columns, cells), f32)]
-        + [((columns, part_edge), bf16)] * (2 * halo_parts),
+        + [((columns, gz * 2 * gy), bf16)] * 2,
         limit=8,
         name="flatten",
     )
 
-    def halos_of(edges):
-        received = []
-        for part in range(halo_parts):
-            low = lax.ppermute(edges[2 * part + 1], "dom", ahead)
-            high = lax.ppermute(edges[2 * part], "dom", behind)
-            received.append((low, high))
-        return received
-
-    halos1 = halos_of(edges1)
+    def halos_of(low_edge, high_edge):
+        return lax.ppermute(high_edge, "dom", ahead), lax.ppermute(low_edge, "dom", behind)
+
+    halos1 = halos_of(*edges1)
 
 
     def setup_body(occ, pot, pert, xc, occ_flat, pot_flat, pert_flat, xc_flat):
@@ -198,7 +194,7 @@
 
     (locked_flat,) = run(
         relay_body,
-        [(locked_set, "h")],
+        [(pltpu.with_memory_space_constraint(locked_set, pltpu.HBM), "h")],
         [((locked, cells), bf16, "h")],
         scratch=[
             pltpu.VMEM((3, chunk, planes, gz, gy), bf16),
@@ -209,6 +205,8 @@
         limit=12,
         name="relay",
     )
+
+    locked_flat = pltpu.with_memory_space_constraint(locked_flat, pltpu.HBM)
 
     def stencil_body(field, pot, scal, out, energy):
         energy[...] = per_row(scal, 0, gy)
@@ -254,15 +252,15 @@
         )
         return out
 
-    def finish_rhs(part, partial, low, high, occ, pot, rhs, rounded):
-        first = part * part_z
+    def finish_rhs(first, count, partial, low, high, occ, pot, rhs, rounded):
 
         def rows_step(p, carry):
             rows = pl.ds(pl.multiple_of(p * orbs, orbs), orbs)
-            for inner in range(part_z):
+            for inner in range(count):
                 for x in range(planes):
                     at = col(first + inner, x)
-                    value = partial[rows, at : at + gy] - pot[p, 0:1, at : at + gy] * occ[
+                    spot = col(inner, x)
+                    value = partial[rows, at : at + gy] - pot[p, 0:1, spot : spot + gy] * occ[
                         :, at : at + gy
                     ]
 
@@ -279,13 +277,148 @@
                     if x == planes - 1:
                         value = value + (near_half * halo(high, 0) + far_half * halo(high, 1))
                     rhs[rows, at : at + gy] = value
-                    rounded[rows, at : at + gy] = value.astype(bf16)
+                    rounded[rows, spot : spot + gy] = value.astype(bf16)
             return carry
 
         lax.fori_loop(0, perts, rows_step, 0)
 
+    def reduce_pieces(own, arrived):
+        def pair_body(own_ref, arrived_ref, kept, *sent):
+            for m in range(chips):
+                cut = slice(m * piece, (m + 1) * piece)
+                value = own_ref[:, cut] + arrived_ref[:, cut].astype(f32)
+                if m == 0:
+                    kept[...] = value
+                else:
+                    sent[m - 1][...] = value.astype(bf16)
+
+        kept, *sent = run(
+            pair_body,
+            [(own, "v"), (arrived, "v")],
+            [((columns, piece), f32)] + [((columns, piece), bf16)] * (chips - 1),
+            limit=6,
+            name="margin_pair",
+        )
+        arrivals = [swap(sent[m - 1], 2 * m, "dom") for m in range(1, chips)]
+
+        def add_body(*refs):
+            out = refs[-1]
+            out[...] = tree_sum([r[...].astype(f32) for r in refs[:-1]]).astype(bf16)
+
+        (mine,) = run(
+            add_body,
+            [(kept, "v")] + [(r, "v") for r in arrivals],
+            [((columns, piece), bf16)],
+            limit=2,
+            name="add_pieces",
+        )
+        gathered = [mine] + [swap(mine, 2 * m, "dom") for m in range(1, chips)]
+        return gathered
+
+    def margins_in_parts(partial, halos, pot):
+        def column_copies(where_ref, both, first, lock, buf, sems):
+            copies = []
+            for k in range(len(both)):
+                start = (where_ref[0] ^ both[k]) * half
+                for m in range(chips):
+                    rows = pl.ds(pl.multiple_of(start + (where_ref[1] ^ m) * piece, piece), piece)
+                    index = k * chips + m
+                    copies.append(
+                        pltpu.make_async_copy(
+                            lock.at[rows, first * part_cells : (first + 1) * part_cells],
+                            buf.at[index],
+                            sems.at[index],
+                        )
+                    )
+            return copies
+
+        def scratch_of(count):
+            return [
+                pltpu.VMEM((count, piece, part_cells), bf16),
+                pltpu.SemaphoreType.DMA((count,)),
+            ]
+
+        def early_body(where_ref, part_ref, low, high, occ, pot_ref, lock, rhs, out, rounded, buf, sems):
+            copies = column_copies(where_ref, (1, 0), 0, lock, buf, sems)
+            for copy in copies:
+                copy.start()
+            finish_rhs(0, part_z, part_ref, low, high, occ, pot_ref, rhs, rounded)
+            for m in range(2 * chips):
+                copies[m].wait()
+                out[:, m * piece : (m + 1) * piece] = dot_nt(rounded[...], buf[m])
+
+        rhs, early = run(
+            early_body,
+            [
+                (where, "s"),
+                (partial, "v"),
+                (halos[0][0], "v"),
+                (halos[0][1], "v"),
+                (flat_occupied, "v"),
+                (pot[0], "v"),
+                (locked_flat, "h"),
+            ],
+            [((columns, cells), f32), ((columns, locked), f32)],
+            scratch=[pltpu.VMEM((columns, part_cells), bf16)] + scratch_of(2 * chips),
+            aliases={1: 0},
+            limit=24,
+            name="margin_early",
+        )
+
+        def late_body(
+            where_ref, part_ref, low, high, occ, pot_ref, lock, early_ref, rhs, rounded, out, buf, sems
+        ):
+            copies = column_copies(where_ref, (1,), 1, lock, buf, sems)
+            for copy in copies:
+                copy.start()
+            finish_rhs(part_z, part_z, part_ref, low, high, occ, pot_ref, rhs, rounded)
+            for m in range(chips):
+                cut = slice(m * piece, (m + 1) * piece)
+                copies[m].wait()
+                out[:, cut] = (early_ref[:, cut] + dot_nt(rounded[...], buf[m])).astype(bf16)
+
+        rhs, rounded, other = run(
+            late_body,
+            [
+                (where, "s"),
+                (rhs, "v"),
+                (halos[1][0], "v"),
+                (halos[1][1], "v"),
+                (flat_occupied, "v"),
+                (pot[1], "v"),
+                (locked_flat, "h"),
+                (early, "v"),
+            ],
+            [((columns, cells), f32), ((columns, part_cells), bf16), ((columns, half), bf16)],
+            scratch=scratch_of(chips),
+            aliases={1: 0},
+            limit=14,
+            name="margin_late",
+        )
+        arrived = swap(other, 1, "dom")
+
+        def own_body(where_ref, rounded_ref, lock, early_ref, out, buf, sems):
+            copies = column_copies(where_ref, (0,), 1, lock, buf, sems)
+            for copy in copies:
+                copy.start()
+            for m in range(chips):
+                cut = slice(m * piece, (m + 1) * piece)
+                old = early_ref[:, half + m * piece : half + (m + 1) * piece]
+                copies[m].wait()
+                out[:, cut] = old + dot_nt(rounded_ref[...], buf[m])
+
+        (own,) = run(
+            own_body,
+            [(where, "s"), (rounded, "v"), (locked_flat, "h"), (early, "v")],
+            [((columns, half), f32)],
+            scratch=scratch_of(chips),
+            limit=14,
+            name="margin_late_own",
+        )
+        return rhs, reduce_pieces(own, arrived)
+
     def margins(partial, halos, pot):
-        low, high = halos[0]
+        low, high = halos
 
         def piece_copies(where_ref, start, lock, buf, sems):
             copies = []
@@ -302,7 +435,7 @@
             copies = piece_copies(where_ref, (1 - where_ref[0]) * half, lock, buf, sems)
             for copy in copies:
                 copy.start()
-            finish_rhs(0, part_ref, low_ref, high_ref, occ, pot_ref, rhs, rounded)
+            finish_rhs(0, gz, part_ref, low_ref, high_ref, occ, pot_ref, rhs, rounded)
             for m in range(chips):
                 copies[m].wait()
                 out[:, m * piece : (m + 1) * piece] = dot_nt(rounded[...], buf[m]).astype(bf16)
@@ -343,37 +476,7 @@
             name="margin_own",
         )
 
-        def pair_body(own_ref, arrived_ref, kept, *sent):
-            for m in range(chips):
-                cut = slice(m * piece, (m + 1) * piece)
-                value = own_ref[:, cut] + arrived_ref[:, cut].astype(f32)
-                if m == 0:
-                    kept[...] = value
-                else:
-                    sent[m - 1][...] = value.astype(bf16)
-
-        kept, *sent = run(
-            pair_body,
-            [(own, "v"), (arrived, "v")],
-            [((columns, piece), f32)] + [((columns, piece), bf16)] * (chips - 1),
-            limit=6,
-            name="margin_pair",
-        )
-        arrivals = [swap(sent[m - 1], 2 * m, "dom") for m in range(1, chips)]
-
-        def add_body(*refs):
-            out = refs[-1]
-            out[...] = tree_sum([r[...].astype(f32) for r in refs[:-1]]).astype(bf16)
-
-        (mine,) = run(
-            add_body,
-            [(kept, "v")] + [(r, "v") for r in arrivals],
-            [((columns, piece), bf16)],
-            limit=2,
-            name="add_pieces",
-        )
-        gathered = [mine] + [swap(mine, 2 * m, "dom") for m in range(1, chips)]
-        return rhs, gathered
+        return rhs, reduce_pieces(own, arrived)
 
     def collect(where_ref, pieces, held):
         for m, ref in enumerate(pieces):
@@ -422,14 +525,20 @@
             total = total + value[:, x * gy : (x + 1) * gy] * value[:, x * gy : (x + 1) * gy]
         return total
 
-    def first_finish(others, acc, rhs, field):
+    def first_finish(part, others, acc, rhs, field, before):
+        extra = [(array, "v") for array in before]
+        base = part * part_z
+        origin = 0 if part else base
+        width = part_cells * (part + 1)
+
         def body(where_ref, *refs):
             pieces = refs[:chips]
             lock, acc_ref, rhs_ref, field_ref, occ, scal = refs[chips : chips + 6]
-            res, mid, low, high, dens, norm = refs[chips + 6 : chips + 12]
-            held, step_rows, lanes, buf, sems = refs[chips + 12 :]
+            rest = refs[chips + 6 :]
+            old, rest = rest[: len(extra)], rest[len(extra) :]
+            res, mid, low, high, dens, norm, held, step_rows, lanes, buf, sems = rest
             start = (1 - where_ref[0]) * half
-            for z in range(gz):
+            for z in range(base, base + part_z):
                 stripe_copy(start, lock, buf, sems, z).start()
             collect(where_ref, pieces, held)
             step_rows[...] = per_row(scal, 1, gy)
@@ -452,17 +561,21 @@
                         jnp.sum(weight * new[p * orbs : (p + 1) * orbs], axis=0, keepdims=True)
                         for p in range(perts)
                     ]
-                    dens[:, spot] = jnp.concatenate(sums, axis=0).astype(bf16)
+                    kept = pl.ds(pl.multiple_of((z - origin) * stripe + x * gy, gy), gy)
+                    dens[:, kept] = jnp.concatenate(sums, axis=0).astype(bf16)
                     if x < 2:
-                        place = pl.ds(pl.multiple_of((z * 2 + x) * gy, gy), gy)
+                        place = pl.ds(pl.multiple_of(((z - base) * 2 + x) * gy, gy), gy)
                         low[:, place] = new.astype(bf16)
                     if x >= planes - 2:
-                        place = pl.ds(pl.multiple_of((z * 2 + x - planes + 2) * gy, gy), gy)
+                        place = pl.ds(pl.multiple_of(((z - base) * 2 + x - planes + 2) * gy, gy), gy)
                         high[:, place] = new.astype(bf16)
                 return carry
 
-            lax.fori_loop(0, gz, step, 0)
+            lax.fori_loop(base, base + part_z, step, 0)
             norm[...] = line_of(lanes[...])
+            if old:
+                norm[...] += old[1][...]
+                dens[:, :part_cells] = old[0][...]
 
         return run(
             body,
@@ -475,13 +588,14 @@
                 (field, "v"),
                 (flat_occupied, "v"),
                 (scalars, "v"),
-            ],
+            ]
+            + extra,
             [
                 ((columns, cells), f32),
                 ((columns, cells), f32),
-                ((columns, gz * 2 * gy), bf16),
-                ((columns, gz * 2 * gy), bf16),
-                ((perts, cells), bf16),
+                ((columns, part_edge), bf16),
+                ((columns, part_edge), bf16),
+                ((perts, width), bf16),
                 ((1, columns), f32),
             ],
             scratch=[
@@ -531,45 +645,58 @@
             name="second_finish",
         )
 
-    def across(array, axis):
-        return [array] + [swap(array, m, axis) for m in range(1, lax.axis_size(axis))]
-
     partial1 = stencil(flat_response)
     rhs1, gathered1 = margins(partial1, halos1, flat_perturbation)
     others1 = [swap(g, 1, "dom") for g in gathered1]
     acc1 = remove_own(gathered1)
-    first_res, middle, low_edge, high_edge, dens, norm1 = first_finish(
-        others1, acc1, rhs1, flat_response
-    )
-    halos2 = halos_of([low_edge, high_edge])
-    densities = across(dens, "band")
-
-    def potential_body(*refs):
-        parts = refs[:bands]
-        pert, xc, flat, native = refs[bands:]
-        density = tree_sum([r[...].astype(f32) for r in parts])
+    def add_body(one, two, out):
+        out[...] = (one[...].astype(f32) + two[...].astype(f32)).astype(bf16)
+
+    def potential_body(one, two, pert, xc, low, high, native):
+        density = one[...].astype(f32) + two[...].astype(f32)
         for z in range(gz):
             for x in range(planes):
                 cut = slice(col(z, x), col(z, x) + gy)
+                spot = slice(col(z % part_z, x), col(z % part_z, x) + gy)
+                flat = low if z < part_z else high
                 for p in range(perts):
                     value = pert[p, 0:1, cut] - xc[0:1, cut] * density[p : p + 1, cut]
-                    flat[p, 0:1, cut] = value
+                    flat[p, 0:1, spot] = value
                     native[p, x, z : z + 1, :] = value
 
-    flat_rp, response_potential = run(
+    halos2 = []
+    first_res, middle, before = rhs1, flat_response, []
+    for part in range(2):
+        first_res, middle, low_edge, high_edge, dens, norm1 = first_finish(
+            part, others1, acc1, first_res, middle, before
+        )
+        before = [dens, norm1]
+        halos2.append(halos_of(low_edge, high_edge))
+    mask = 1
+    while 2 * mask < bands:
+        (dens,) = run(
+            add_body,
+            [(dens, "v"), (swap(dens, mask, "band"), "v")],
+            [((perts, cells), bf16)],
+            limit=2,
+            name="add_density",
+        )
+        mask *= 2
+    rp_low, rp_high, response_potential = run(
         potential_body,
-        [(d, "v") for d in densities]
-        + [(flat_perturbation, "v"), (flat_xc, "v")],
         [
-            ((perts, 1, cells), f32),
-            ((perts, planes, gz, gy), f32),
+            (dens, "v"),
+            (swap(dens, mask, "band"), "v"),
+            (flat_perturbation, "v"),
+            (flat_xc, "v"),
         ],
+        [((perts, 1, part_cells), f32)] * 2 + [((perts, planes, gz, gy), f32)],
         limit=3,
         name="potential",
     )
 
     partial2 = stencil(middle)
-    rhs2, gathered2 = margins(partial2, halos2, flat_rp)
+    rhs2, gathered2 = margins_in_parts(partial2, halos2, [rp_low, rp_high])
     others2 = [swap(g, 1, "dom") for g in gathered2]
     acc2 = remove_own(gathered2)
     second_res, norms = second_finish(others2, acc2, rhs2, norm1)

time: 212 us -> 204 us (0.962)
  local copies, waits for them, and re-layouts: 15.5 us -> 4.46 us
  waiting for transfers between devices: 62 us -> 51.5 us
  Pallas kernels: 104 us -> 114 us
  starting transfers between devices: 29.8 us -> 32.7 us
    ppermute x4 -> x6, waiting for transfers between devices: 12.8 us -> 0.02 us  [the longest x3 0.01 us: halos_of(): lax.ppermute(low_edge, 'dom', behind)]
    unnamed x12 -> x10, local copies, waits for them, and re-layouts: 13.3 us -> 2.2 us
    pallas_call x20 -> x23, Pallas kernels: 104 us -> 114 us  [run(): pl.pallas_call(body, in_specs=[pl.BlockSpec(memory_space=kinds[kind]) for...]
    ppermute x4 -> x6, starting transfers between devices: 6.19 us -> 8.87 us  [the longest x3 8.24 us: halos_of(): lax.ppermute(low_edge, 'dom', behind)]
    ppermute x29 -> x28, waiting for transfers between devices: 49.2 us -> 51.4 us  [swap(): return lax.ppermute(array, axis, [(i, i ^ mask) for i in range(count)])]
    ppermute x29 -> x28, starting transfers between devices: 23.6 us -> 23.8 us  [swap(): return lax.ppermute(array, axis, [(i, i ^ mask) for i in range(count)])]
  transfers between devices with their start and end apart: 33 -> 34, of which waited for: 15 -> 15; matrix products, arithmetic and copies ran while one was open for 0% -> 0% of each run, Pallas kernels for 29% -> 38%
where the time goes in v3:
time: 204 us
  Pallas kernels  114 us (56%)
  waiting for transfers between devices  51.5 us (25%)
  starting transfers between devices  32.7 us (16%)
  local copies, waits for them, and re-layouts  4.46 us (2%)
    pallas_call x23, Pallas kernels, run(): pl.pallas_call(body, in_specs=[pl.BlockSpec(memory_space=kinds[kind]) for...  114 us
    ppermute x28, waiting for transfers between devices, swap(): return lax.ppermute(array, axis, [(i, i ^ mask) for i in range(count)])  51.4 us
    ppermute x28, starting transfers between devices, swap(): return lax.ppermute(array, axis, [(i, i ^ mask) for i in range(count)])  23.8 us
    ppermute x3, starting transfers between devices, halos_of(): lax.ppermute(low_edge, 'dom', behind)  8.24 us
  transfers between devices with their start and end apart: 34, of which 15 were waited for; matrix products, arithmetic and copies ran while one was open for 0% of the time, Pallas kernels for 38%

profile of v3, /device:TPU:0, one launch (start us, length us, event | category | flops | bytes accessed | tf_op | source)
XLA Modules:
  0.0 204.2 jit_solution(10619089038184880203)
XLA Ops:
  0.6 0.8 stack_reshape.6
  1.4 0.8 stack_reshape.7
  2.2 0.7 tile.2
  3.0 2.2 %copy-done = f32[4,64,4,8,128]{4,3,2,1,0:T(8,128)S(1)} copy-done((f32[4,64,4,8,128]{4,3,2,1,0:T(8,128)S(1)}, f32[4,64,4,8,128]{4,3,2,1,0:T(8,128)}, u32[]{:S(2)}) %copy-start) | copy-done | bytes 4194328
  5.2 1.3 flatten.1
  7.0 3.0 %collective-permute-start.1 = (bf16[256,2048]{1,0:T(8,128)(2,1)S(1)}, bf16[256,2048]{1,0:T(8,128)(2,1)S(1)}, u32[]{:S(2)}, u32[]{:S(2)}) collective-permute-start(bf16[256,2048]{1,0:T(8,128)(2,1)S(1)} %get-tuple-element.45), channel_id=1, source_target_pairs={{1,0},{2,1},{3,2},{4,3},{5,4},{6,5},{7,6},{0,7},{9,8},{10,9},{11,1... | collective-permute-start | bytes 3145736 | tf_op jit(solution)/shard_map/ppermute | solution.py:125
  9.9 24.0 %relay.1.lock.refs_4_ = bf16[4096,4096]{1,0:T(8,128)(2,1)} custom-call(bf16[4096,4,8,128]{3,2,1,0:T(8,128)(2,1)} %source.1), custom_call_target="tpu_custom_call" | custom-call | tf_op jit(solution)/shard_map/relay/pallas_call | solution.py:18
  34.3 5.0 %stencil.2.part_ref = f32[256,4096]{1,0:T(8,128)S(1)} custom-call(f32[256,4096]{1,0:T(8,128)S(1)} %get-tuple-element.42.field.refs_7_, f32[1,4096]{1,0:T(1,128)S(1)} %get-tuple-element.43.pot, f32[3,256]{1,0:T(4,128)S(1)} %pad_maximum_fusion.early.scal.refs_9_.refs_7_), custom_call_target="tpu_custom_call" | custom-call | tf_op jit(solution)/shard_map/stencil/pallas_call | solution.py:18
  39.3 7.9 %margin_other.1 = (f32[256,4096]{1,0:T(8,128)S(1)}, bf16[256,4096]{1,0:T(8,128)(2,1)S(1)}, bf16[256,2048]{1,0:T(8,128)(2,1)S(1)}) custom-call(s32[2]{0:T(128)S(1)} %pad_add_fusion.placed.where_ref, f32[256,4096]{1,0:T(8,128)S(1)} %stencil.2.part_ref, bf16[256,2048]{1,0:T(8,128)(2,1)S(1)} %collective-permute-done.low_ref, ...), custom_call_target="tpu_custom_call", output_to_operand_aliasing={{0}: (1, {})} | custom-call | tf_op jit(solution)/shard_map/margin_other/pallas_call | solution.py:18
  47.3 7.9 %margin_own.1.own_ref = f32[256,2048]{1,0:T(8,128)S(1)} custom-call(s32[2]{0:T(128)S(1)} %pad_add_fusion.placed.where_ref, bf16[256,4096]{1,0:T(8,128)(2,1)S(1)} %get-tuple-element.48.rounded_ref, bf16[4096,4096]{1,0:T(8,128)(2,1)} %relay.1.lock.refs_4_), custom_call_target="tpu_custom_call" | custom-call | tf_op jit(solution)/shard_map/margin_own/pallas_call | solution.py:18
  55.4 1.4 collective-permute-start.3
  56.8 1.5 collective-permute-start.4
  58.3 0.9 collective-permute-start.5
  59.2 5.4 %collective-permute-done.3.refs_1_ = bf16[256,512]{1,0:T(8,128)(2,1)S(1)} collective-permute-done((bf16[256,512]{1,0:T(8,128)(2,1)S(1)}, bf16[256,512]{1,0:T(8,128)(2,1)S(1)}, u32[]{:S(2)}, u32[]{:S(2)}) %collective-permute-start.3) | collective-permute-done | bytes 262176 | tf_op jit(solution)/shard_map/ppermute | solution.py:88
  64.6 5.3 %collective-permute-done.4.refs_2_ = bf16[256,512]{1,0:T(8,128)(2,1)S(1)} collective-permute-done((bf16[256,512]{1,0:T(8,128)(2,1)S(1)}, bf16[256,512]{1,0:T(8,128)(2,1)S(1)}, u32[]{:S(2)}, u32[]{:S(2)}) %collective-permute-start.4) | collective-permute-done | bytes 262176 | tf_op jit(solution)/shard_map/ppermute | solution.py:88
  69.9 1.6 collective-permute-done.5.refs_3_
  71.6 1.8 collective-permute-start.11
  73.8 1.4 collective-permute-start.7
  75.2 6.7 %collective-permute-done.11.refs_3_ = bf16[256,512]{1,0:T(8,128)(2,1)S(1)} collective-permute-done((bf16[256,512]{1,0:T(8,128)(2,1)S(1)}, bf16[256,512]{1,0:T(8,128)(2,1)S(1)}, u32[]{:S(2)}, u32[]{:S(2)}) %collective-permute-start.11) | collective-permute-done | bytes 262176 | tf_op jit(solution)/shard_map/ppermute | solution.py:88
  81.8 4.3 %collective-permute-done.9.refs_2_ = bf16[256,512]{1,0:T(8,128)(2,1)S(1)} collective-permute-done((bf16[256,512]{1,0:T(8,128)(2,1)S(1)}, bf16[256,512]{1,0:T(8,128)(2,1)S(1)}, u32[]{:S(2)}, u32[]{:S(2)}) %collective-permute-start.9) | collective-permute-done | bytes 262176 | tf_op jit(solution)/shard_map/ppermute | solution.py:88
  86.6 7.9 %remove_own.2.refs_5_ = f32[256,4096]{1,0:T(8,128)S(1)} custom-call(s32[2]{0:T(128)S(1)} %pad_add_fusion.placed.where_ref, bf16[256,512]{1,0:T(8,128)(2,1)S(1)} %add_pieces.2.refs_0_, bf16[256,512]{1,0:T(8,128)(2,1)S(1)} %collective-permute-done.7.refs_1_, bf16[256,512]{1,0:T(8,128)(2,1)S(1)} %collective-permute-done.9.refs_2_, ...), custom_call_target="tpu_custom_call" | custom-call | tf_op jit(solution)/shard_map/remove_own/pallas_call | solution.py:18
  94.5 6.1 %first_finish.2 = (f32[256,4096]{1,0:T(8,128)S(1)}, f32[256,4096]{1,0:T(8,128)S(1)}, bf16[256,1024]{1,0:T(8,128)(2,1)S(1)}, bf16[256,1024]{1,0:T(8,128)(2,1)S(1)...) custom-call(s32[2]{0:T(128)S(1)} %pad_add_fusion.placed.where_ref, ...), custom_call_target="tpu_custom_call", output_to_operand_aliasing={{0}: (7, {}), {1}: (8, {})} | custom-call | tf_op jit(solution)/shard_map/first_finish/pallas_call | solution.py:18
  100.8 2.6 %collective-permute-start.14 = (bf16[256,1024]{1,0:T(8,128)(2,1)S(1)}, bf16[256,1024]{1,0:T(8,128)(2,1)S(1)}, u32[]{:S(2)}, u32[]{:S(2)}) collective-permute-start(bf16[256,1024]{1,0:T(8,128)(2,1)S(1)} %get-tuple-element.61), channel_id=1, source_target_pairs={{1,0},{2,1},{3,2},{4,3},{5,4},{6,5},{7,6},{0,7},{9,8},{10,9},{11,1... | collective-permute-start | bytes 1572872 | tf_op jit(solution)/shard_map/ppermute | solution.py:125
  103.4 6.1 %first_finish.3 = (f32[256,4096]{1,0:T(8,128)S(1)}, f32[256,4096]{1,0:T(8,128)S(1)}, bf16[256,1024]{1,0:T(8,128)(2,1)S(1)}, bf16[256,1024]{1,0:T(8,128)(2,1)S(1)...) custom-call(s32[2]{0:T(128)S(1)} %pad_add_fusion.placed.where_ref, ...), custom_call_target="tpu_custom_call", output_to_operand_aliasing={{0}: (7, {}), {1}: (8, {})} | custom-call | tf_op jit(solution)/shard_map/first_finish/pallas_call | solution.py:18
  109.6 2.6 %collective-permute-start.18 = (bf16[256,1024]{1,0:T(8,128)(2,1)S(1)}, bf16[256,1024]{1,0:T(8,128)(2,1)S(1)}, u32[]{:S(2)}, u32[]{:S(2)}) collective-permute-start(bf16[256,1024]{1,0:T(8,128)(2,1)S(1)} %get-tuple-element.67), channel_id=1, source_target_pairs={{1,0},{2,1},{3,2},{4,3},{5,4},{6,5},{7,6},{0,7},{9,8},{10,9},{11,1... | collective-permute-start | bytes 1572872 | tf_op jit(solution)/shard_map/ppermute | solution.py:125
  112.2 1.6 collective-permute-start.15
  113.8 2.3 %collective-permute-done.15.two = bf16[4,4096]{1,0:T(4,128)(2,1)S(1)} collective-permute-done((bf16[4,4096]{1,0:T(4,128)(2,1)S(1)}, bf16[4,4096]{1,0:T(4,128)(2,1)S(1)}, u32[]{:S(2)}, u32[]{:S(2)}) %collective-permute-start.15) | collective-permute-done | bytes 32800 | tf_op jit(solution)/shard_map/ppermute | solution.py:88
  116.2 3.0 %collective-permute-start.16 = (bf16[4,4096]{1,0:T(4,128)(2,1)S(1)}, bf16[4,4096]{1,0:T(4,128)(2,1)S(1)}, u32[]{:S(2)}, u32[]{:S(2)}) collective-permute-start(bf16[4,4096]{1,0:T(4,128)(2,1)S(1)} %add_density.1.one), channel_id=1, source_target_pairs={{0,16},{8,24},{16,0},{24,8},{1,17},{9,25},{17,1},{25,9},{2,18},{10... | collective-permute-start | bytes 98312 | tf_op jit(solution)/shard_map/ppermute | solution.py:88
  119.2 5.2 %stencil.3.part_ref = f32[256,4096]{1,0:T(8,128)S(1)} custom-call(f32[256,4096]{1,0:T(8,128)S(1)} %get-tuple-element.59.field.refs_4_, f32[1,4096]{1,0:T(1,128)S(1)} %get-tuple-element.43.pot, f32[3,256]{1,0:T(4,128)S(1)} %pad_maximum_fusion.early.scal.refs_9_.refs_7_), custom_call_target="tpu_custom_call" | custom-call | tf_op jit(solution)/shard_map/stencil/pallas_call | solution.py:18
  124.4 0.7 potential.1
  125.1 8.1 %margin_early.1 = (f32[256,4096]{1,0:T(8,128)S(1)}, f32[256,4096]{1,0:T(8,128)S(1)}) custom-call(s32[2]{0:T(128)S(1)} %pad_add_fusion.placed.where_ref, f32[256,4096]{1,0:T(8,128)S(1)} %stencil.3.part_ref, bf16[256,1024]{1,0:T(8,128)(2,1)S(1)} %collective-permute-done.13.low, ...), custom_call_target="tpu_custom_call", output_to_operand_aliasing={{0}: (1, {})} | custom-call | tf_op jit(solution)/shard_map/margin_early/pallas_call | solution.py:18
  133.2 5.2 %margin_late.1 = (f32[256,4096]{1,0:T(8,128)S(1)}, bf16[256,2048]{1,0:T(8,128)(2,1)S(1)}, bf16[256,2048]{1,0:T(8,128)(2,1)S(1)}) custom-call(s32[2]{0:T(128)S(1)} %pad_add_fusion.placed.where_ref, f32[256,4096]{1,0:T(8,128)S(1)} %get-tuple-element.65.part_ref, bf16[256,1024]{1,0:T(8,128)(2,1)S(1)} %collective-permute-done.17.low, ...), custom_call_target="tpu_custom_call", output_to_operand_aliasing={{0}: (1, {})} | custom-call | tf_op jit(solution)/shard_map/margin_late/pallas_call | solution.py:18
  138.5 5.3 %margin_late_own.1.own_ref = f32[256,2048]{1,0:T(8,128)S(1)} custom-call(s32[2]{0:T(128)S(1)} %pad_add_fusion.placed.where_ref, bf16[256,2048]{1,0:T(8,128)(2,1)S(1)} %get-tuple-element.70.rounded_ref, bf16[4096,4096]{1,0:T(8,128)(2,1)} %relay.1.lock.refs_4_, f32[256,4096]{1,0:T(8,128)S(1)} %get-tuple-element.69.early_ref), custom_call_target="tpu_custom_call" | custom-call | tf_op jit(solution)/shard_map/margin_late_own/pallas_call | solution.py:18
  144.6 3.0 %collective-permute-start.22 = (bf16[256,512]{1,0:T(8,128)(2,1)S(1)}, bf16[256,512]{1,0:T(8,128)(2,1)S(1)}, u32[]{:S(2)}, u32[]{:S(2)}) collective-permute-start(bf16[256,512]{1,0:T(8,128)(2,1)S(1)} %get-tuple-element.75), channel_id=1, source_target_pairs={{0,6},{1,7},{2,4},{3,5},{4,2},{5,3},{6,0},{7,1},{8,14},{9,15},{10,... | collective-permute-start | bytes 786440 | tf_op jit(solution)/shard_map/ppermute | solution.py:88
  147.5 5.6 %collective-permute-done.20.refs_1_ = bf16[256,512]{1,0:T(8,128)(2,1)S(1)} collective-permute-done((bf16[256,512]{1,0:T(8,128)(2,1)S(1)}, bf16[256,512]{1,0:T(8,128)(2,1)S(1)}, u32[]{:S(2)}, u32[]{:S(2)}) %collective-permute-start.20) | collective-permute-done | bytes 262176 | tf_op jit(solution)/shard_map/ppermute | solution.py:88
  153.1 5.3 %collective-permute-done.21.refs_2_ = bf16[256,512]{1,0:T(8,128)(2,1)S(1)} collective-permute-done((bf16[256,512]{1,0:T(8,128)(2,1)S(1)}, bf16[256,512]{1,0:T(8,128)(2,1)S(1)}, u32[]{:S(2)}, u32[]{:S(2)}) %collective-permute-start.21) | collective-permute-done | bytes 262176 | tf_op jit(solution)/shard_map/ppermute | solution.py:88
  158.6 1.6 collective-permute-start.28
  160.2 1.6 collective-permute-start.26
  162.1 6.7 %collective-permute-done.28.refs_3_ = bf16[256,512]{1,0:T(8,128)(2,1)S(1)} collective-permute-done((bf16[256,512]{1,0:T(8,128)(2,1)S(1)}, bf16[256,512]{1,0:T(8,128)(2,1)S(1)}, u32[]{:S(2)}, u32[]{:S(2)}) %collective-permute-start.28) | collective-permute-done | bytes 262176 | tf_op jit(solution)/shard_map/ppermute | solution.py:88
  168.8 4.1 %collective-permute-done.26.refs_2_ = bf16[256,512]{1,0:T(8,128)(2,1)S(1)} collective-permute-done((bf16[256,512]{1,0:T(8,128)(2,1)S(1)}, bf16[256,512]{1,0:T(8,128)(2,1)S(1)}, u32[]{:S(2)}, u32[]{:S(2)}) %collective-permute-start.26) | collective-permute-done | bytes 262176 | tf_op jit(solution)/shard_map/ppermute | solution.py:88
  173.5 7.9 %remove_own.3.refs_5_ = f32[256,4096]{1,0:T(8,128)S(1)} custom-call(s32[2]{0:T(128)S(1)} %pad_add_fusion.placed.where_ref, bf16[256,512]{1,0:T(8,128)(2,1)S(1)} %add_pieces.3.refs_0_, bf16[256,512]{1,0:T(8,128)(2,1)S(1)} %collective-permute-done.24.refs_1_, bf16[256,512]{1,0:T(8,128)(2,1)S(1)} %collective-permute-done.26.refs_2_, ...), custom_call_target="tpu_custom_call" | custom-call | tf_op jit(solution)/shard_map/remove_own/pallas_call | solution.py:18
  181.4 8.2 %second_finish.1 = (f32[256,4096]{1,0:T(8,128)S(1)}, f32[2,256]{1,0:T(2,128)S(1)}) custom-call(s32[2]{0:T(128)S(1)} %pad_add_fusion.placed.where_ref, bf16[256,512]{1,0:T(8,128)(2,1)S(1)} %collective-permute-done.23.refs_0_, bf16[256,512]{1,0:T(8,128)(2,1)S(1)} %collective-permute-done.25.refs_1_, ...), custom_call_target="tpu_custom_call", output_to_operand_aliasing={{0}: (7, {})} | custom-call | tf_op jit(solution)/shard_map/second_finish/pallas_call | solution.py:18
  189.7 1.1 collective-permute-done.30.two
  190.8 1.5 collective-permute-start.33
  192.2 1.5 collective-permute-start.32
  194.3 1.0 collective-permute-done.33.refs_3_
  195.8 1.5 collective-permute-done.31.refs_1_
  197.3 6.9 %final.1 = f32[256,4,8,128]{3,2,1,0:T(8,128)} custom-call(f32[2,256]{1,0:T(2,128)S(1)} %norm_pair.1.refs_0_, f32[2,256]{1,0:T(2,128)S(1)} %collective-permute-done.31.refs_1_, f32[2,256]{1,0:T(2,128)S(1)} %collective-permute-done.32.refs_2_, f32[2,256]{1,0:T(2,128)S(1)} %collective-permute-done.33.refs_3_, f32[256,4096]{1,0:T(8,128)S(1)} %get-tuple-element.59.field.refs_4_, ...), custom_call_target="tpu_custom_call" | custom-call | tf_op jit(solution)/shard_map/final/pallas_call | solution.py:18
  (59 shorter events, 5.5 us)
Async XLA Ops:
  3.0 2.2 %copy-start = (f32[4,64,4,8,128]{4,3,2,1,0:T(8,128)S(1)}, f32[4,64,4,8,128]{4,3,2,1,0:T(8,128)}, u32[]{:S(2)}) copy-start(f32[4,64,4,8,128]{4,3,2,1,0:T(8,128)} %param.9) | copy-start | bytes 12582916
  6.4 32.9 %collective-permute-start = (bf16[256,2048]{1,0:T(8,128)(2,1)S(1)}, bf16[256,2048]{1,0:T(8,128)(2,1)S(1)}, u32[]{:S(2)}, u32[]{:S(2)}) collective-permute-start(bf16[256,2048]{1,0:T(8,128)(2,1)S(1)} %get-tuple-element.44), channel_id=1, source_target_pairs={{0,1},{1,2},{2,3},{3,4},{4,5},{5,6},{6,7},{7,0},{8,9},{9,10},{10,1... | collective-permute-start | bytes 3145736 | tf_op jit(solution)/shard_map/ppermute | solution.py:125
  6.9 27.0 %copy-start.1 = (f32[64,4,8,128]{3,2,1,0:T(8,128)S(1)}, f32[64,4,8,128]{3,2,1,0:T(8,128)}, u32[]{:S(2)}) copy-start(f32[64,4,8,128]{3,2,1,0:T(8,128)} %occ.1) | copy-start | bytes 3145732
  6.9 27.0 %copy-start.2 = (f32[4,4,8,128]{3,2,1,0:T(8,128)S(1)}, f32[4,4,8,128]{3,2,1,0:T(8,128)}, u32[]{:S(2)}) copy-start(f32[4,4,8,128]{3,2,1,0:T(8,128)} %pert.1) | copy-start | bytes 196612
  6.9 27.0 %copy-start.3 = (f32[4,8,128]{2,1,0:T(8,128)S(1)}, f32[4,8,128]{2,1,0:T(8,128)}, u32[]{:S(2)}) copy-start(f32[4,8,128]{2,1,0:T(8,128)} %pot.1) | copy-start | bytes 49156
  6.9 27.0 %copy-start.4 = (f32[4,8,128]{2,1,0:T(8,128)S(1)}, f32[4,8,128]{2,1,0:T(8,128)}, u32[]{:S(2)}) copy-start(f32[4,8,128]{2,1,0:T(8,128)} %xc.1) | copy-start | bytes 49156
  7.0 32.4 %collective-permute-start.1 = (bf16[256,2048]{1,0:T(8,128)(2,1)S(1)}, bf16[256,2048]{1,0:T(8,128)(2,1)S(1)}, u32[]{:S(2)}, u32[]{:S(2)}) collective-permute-start(bf16[256,2048]{1,0:T(8,128)(2,1)S(1)} %get-tuple-element.45), channel_id=1, source_target_pairs={{1,0},{2,1},{3,2},{4,3},{5,4},{6,5},{7,6},{0,7},{9,8},{10,9},{11,1... | collective-permute-start | bytes 3145736 | tf_op jit(solution)/shard_map/ppermute | solution.py:125
  47.3 8.0 %collective-permute-start.2 = (bf16[256,2048]{1,0:T(8,128)(2,1)S(1)}, bf16[256,2048]{1,0:T(8,128)(2,1)S(1)}, u32[]{:S(2)}, u32[]{:S(2)}) collective-permute-start(bf16[256,2048]{1,0:T(8,128)(2,1)S(1)} %get-tuple-element.49), channel_id=1, source_target_pairs={{0,1},{1,0},{2,3},{3,2},{4,5},{5,4},{6,7},{7,6},{8,9},{9,8},{10,11... | collective-permute-start | bytes 3145736 | tf_op jit(solution)/shard_map/ppermute | solution.py:88
  55.4 9.2 %collective-permute-start.3 = (bf16[256,512]{1,0:T(8,128)(2,1)S(1)}, bf16[256,512]{1,0:T(8,128)(2,1)S(1)}, u32[]{:S(2)}, u32[]{:S(2)}) collective-permute-start(bf16[256,512]{1,0:T(8,128)(2,1)S(1)} %get-tuple-element.51), channel_id=1, source_target_pairs={{0,2},{1,3},{2,0},{3,1},{4,6},{5,7},{6,4},{7,5},{8,10},{9,11},{10,... | collective-permute-start | bytes 786440 | tf_op jit(solution)/shard_map/ppermute | solution.py:88
  56.8 13.1 %collective-permute-start.4 = (bf16[256,512]{1,0:T(8,128)(2,1)S(1)}, bf16[256,512]{1,0:T(8,128)(2,1)S(1)}, u32[]{:S(2)}, u32[]{:S(2)}) collective-permute-start(bf16[256,512]{1,0:T(8,128)(2,1)S(1)} %get-tuple-element.52), channel_id=1, source_target_pairs={{0,4},{1,5},{2,6},{3,7},{4,0},{5,1},{6,2},{7,3},{8,12},{9,13},{10,... | collective-permute-start | bytes 786440 | tf_op jit(solution)/shard_map/ppermute | solution.py:88
  58.3 13.2 %collective-permute-start.5 = (bf16[256,512]{1,0:T(8,128)(2,1)S(1)}, bf16[256,512]{1,0:T(8,128)(2,1)S(1)}, u32[]{:S(2)}, u32[]{:S(2)}) collective-permute-start(bf16[256,512]{1,0:T(8,128)(2,1)S(1)} %get-tuple-element.53), channel_id=1, source_target_pairs={{0,6},{1,7},{2,4},{3,5},{4,2},{5,3},{6,0},{7,1},{8,14},{9,15},{10,... | collective-permute-start | bytes 786440 | tf_op jit(solution)/shard_map/ppermute | solution.py:88
  71.6 10.2 %collective-permute-start.11 = (bf16[256,512]{1,0:T(8,128)(2,1)S(1)}, bf16[256,512]{1,0:T(8,128)(2,1)S(1)}, u32[]{:S(2)}, u32[]{:S(2)}) collective-permute-start(bf16[256,512]{1,0:T(8,128)(2,1)S(1)} %add_pieces.2.refs_0_), channel_id=1, source_target_pairs={{0,6},{1,7},{2,4},{3,5},{4,2},{5,3},{6,0},{7,1},{8,14},{9,15},{10,... | collective-permute-start | bytes 786440 | tf_op jit(solution)/shard_map/ppermute | solution.py:88
  73.4 12.7 %collective-permute-start.9 = (bf16[256,512]{1,0:T(8,128)(2,1)S(1)}, bf16[256,512]{1,0:T(8,128)(2,1)S(1)}, u32[]{:S(2)}, u32[]{:S(2)}) collective-permute-start(bf16[256,512]{1,0:T(8,128)(2,1)S(1)} %add_pieces.2.refs_0_), channel_id=1, source_target_pairs={{0,4},{1,5},{2,6},{3,7},{4,0},{5,1},{6,2},{7,3},{8,12},{9,13},{10,... | collective-permute-start | bytes 786440 | tf_op jit(solution)/shard_map/ppermute | solution.py:88
  73.8 12.4 %collective-permute-start.7 = (bf16[256,512]{1,0:T(8,128)(2,1)S(1)}, bf16[256,512]{1,0:T(8,128)(2,1)S(1)}, u32[]{:S(2)}, u32[]{:S(2)}) collective-permute-start(bf16[256,512]{1,0:T(8,128)(2,1)S(1)} %add_pieces.2.refs_0_), channel_id=1, source_target_pairs={{0,2},{1,3},{2,0},{3,1},{4,6},{5,7},{6,4},{7,5},{8,10},{9,11},{10,... | collective-permute-start | bytes 786440 | tf_op jit(solution)/shard_map/ppermute | solution.py:88
  75.2 19.3 %collective-permute-start.6 = (bf16[256,512]{1,0:T(8,128)(2,1)S(1)}, bf16[256,512]{1,0:T(8,128)(2,1)S(1)}, u32[]{:S(2)}, u32[]{:S(2)}) collective-permute-start(bf16[256,512]{1,0:T(8,128)(2,1)S(1)} %add_pieces.2.refs_0_), channel_id=1, source_target_pairs={{0,1},{1,0},{2,3},{3,2},{4,5},{5,4},{6,7},{7,6},{8,9},{9,8},{10,11... | collective-permute-start | bytes 786440 | tf_op jit(solution)/shard_map/ppermute | solution.py:88
  81.8 12.7 %collective-permute-start.12 = (bf16[256,512]{1,0:T(8,128)(2,1)S(1)}, bf16[256,512]{1,0:T(8,128)(2,1)S(1)}, u32[]{:S(2)}, u32[]{:S(2)}) collective-permute-start(bf16[256,512]{1,0:T(8,128)(2,1)S(1)} %collective-permute-done.11.refs_3_), channel_id=1, source_target_pairs={{0,1},{1,0},{2,3},{3,2},{4,5},{5,4},{6,7},{7,6},{8,9},{9,8},{10,11... | collective-permute-start | bytes 786440 | tf_op jit(solution)/shard_map/ppermute | solution.py:88
  86.1 8.4 %collective-permute-start.10 = (bf16[256,512]{1,0:T(8,128)(2,1)S(1)}, bf16[256,512]{1,0:T(8,128)(2,1)S(1)}, u32[]{:S(2)}, u32[]{:S(2)}) collective-permute-start(bf16[256,512]{1,0:T(8,128)(2,1)S(1)} %collective-permute-done.9.refs_2_), channel_id=1, source_target_pairs={{0,1},{1,0},{2,3},{3,2},{4,5},{5,4},{6,7},{7,6},{8,9},{9,8},{10,11... | collective-permute-start | bytes 786440 | tf_op jit(solution)/shard_map/ppermute | solution.py:88
  86.1 8.4 %collective-permute-start.8 = (bf16[256,512]{1,0:T(8,128)(2,1)S(1)}, bf16[256,512]{1,0:T(8,128)(2,1)S(1)}, u32[]{:S(2)}, u32[]{:S(2)}) collective-permute-start(bf16[256,512]{1,0:T(8,128)(2,1)S(1)} %collective-permute-done.7.refs_1_), channel_id=1, source_target_pairs={{0,1},{1,0},{2,3},{3,2},{4,5},{5,4},{6,7},{7,6},{8,9},{9,8},{10,11... | collective-permute-start | bytes 786440 | tf_op jit(solution)/shard_map/ppermute | solution.py:88
  100.7 24.4 %collective-permute-start.13 = (bf16[256,1024]{1,0:T(8,128)(2,1)S(1)}, bf16[256,1024]{1,0:T(8,128)(2,1)S(1)}, u32[]{:S(2)}, u32[]{:S(2)}) collective-permute-start(bf16[256,1024]{1,0:T(8,128)(2,1)S(1)} %get-tuple-element.60), channel_id=1, source_target_pairs={{0,1},{1,2},{2,3},{3,4},{4,5},{5,6},{6,7},{7,0},{8,9},{9,10},{10,1... | collective-permute-start | bytes 1572872 | tf_op jit(solution)/shard_map/ppermute | solution.py:125
  100.8 24.3 %collective-permute-start.14 = (bf16[256,1024]{1,0:T(8,128)(2,1)S(1)}, bf16[256,1024]{1,0:T(8,128)(2,1)S(1)}, u32[]{:S(2)}, u32[]{:S(2)}) collective-permute-start(bf16[256,1024]{1,0:T(8,128)(2,1)S(1)} %get-tuple-element.61), channel_id=1, source_target_pairs={{1,0},{2,1},{3,2},{4,3},{5,4},{6,5},{7,6},{0,7},{9,8},{10,9},{11,1... | collective-permute-start | bytes 1572872 | tf_op jit(solution)/shard_map/ppermute | solution.py:125
  109.5 23.7 %collective-permute-start.17 = (bf16[256,1024]{1,0:T(8,128)(2,1)S(1)}, bf16[256,1024]{1,0:T(8,128)(2,1)S(1)}, u32[]{:S(2)}, u32[]{:S(2)}) collective-permute-start(bf16[256,1024]{1,0:T(8,128)(2,1)S(1)} %get-tuple-element.66), channel_id=1, source_target_pairs={{0,1},{1,2},{2,3},{3,4},{4,5},{5,6},{6,7},{7,0},{8,9},{9,10},{10,1... | collective-permute-start | bytes 1572872 | tf_op jit(solution)/shard_map/ppermute | solution.py:125
  109.6 23.7 %collective-permute-start.18 = (bf16[256,1024]{1,0:T(8,128)(2,1)S(1)}, bf16[256,1024]{1,0:T(8,128)(2,1)S(1)}, u32[]{:S(2)}, u32[]{:S(2)}) collective-permute-start(bf16[256,1024]{1,0:T(8,128)(2,1)S(1)} %get-tuple-element.67), channel_id=1, source_target_pairs={{1,0},{2,1},{3,2},{4,3},{5,4},{6,5},{7,6},{0,7},{9,8},{10,9},{11,1... | collective-permute-start | bytes 1572872 | tf_op jit(solution)/shard_map/ppermute | solution.py:125
  112.2 3.9 %collective-permute-start.15 = (bf16[4,4096]{1,0:T(4,128)(2,1)S(1)}, bf16[4,4096]{1,0:T(4,128)(2,1)S(1)}, u32[]{:S(2)}, u32[]{:S(2)}) collective-permute-start(bf16[4,4096]{1,0:T(4,128)(2,1)S(1)} %get-tuple-element.62.one), channel_id=1, source_target_pairs={{0,8},{8,0},{16,24},{24,16},{1,9},{9,1},{17,25},{25,17},{2,10},{10... | collective-permute-start | bytes 98312 | tf_op jit(solution)/shard_map/ppermute | solution.py:88
  116.2 8.2 %collective-permute-start.16 = (bf16[4,4096]{1,0:T(4,128)(2,1)S(1)}, bf16[4,4096]{1,0:T(4,128)(2,1)S(1)}, u32[]{:S(2)}, u32[]{:S(2)}) collective-permute-start(bf16[4,4096]{1,0:T(4,128)(2,1)S(1)} %add_density.1.one), channel_id=1, source_target_pairs={{0,16},{8,24},{16,0},{24,8},{1,17},{9,25},{17,1},{25,9},{2,18},{10... | collective-permute-start | bytes 98312 | tf_op jit(solution)/shard_map/ppermute | solution.py:88
  138.4 5.3 %collective-permute-start.19 = (bf16[256,2048]{1,0:T(8,128)(2,1)S(1)}, bf16[256,2048]{1,0:T(8,128)(2,1)S(1)}, u32[]{:S(2)}, u32[]{:S(2)}) collective-permute-start(bf16[256,2048]{1,0:T(8,128)(2,1)S(1)} %get-tuple-element.71), channel_id=1, source_target_pairs={{0,1},{1,0},{2,3},{3,2},{4,5},{5,4},{6,7},{7,6},{8,9},{9,8},{10,11... | collective-permute-start | bytes 3145736 | tf_op jit(solution)/shard_map/ppermute | solution.py:88
  144.0 9.2 %collective-permute-start.20 = (bf16[256,512]{1,0:T(8,128)(2,1)S(1)}, bf16[256,512]{1,0:T(8,128)(2,1)S(1)}, u32[]{:S(2)}, u32[]{:S(2)}) collective-permute-start(bf16[256,512]{1,0:T(8,128)(2,1)S(1)} %get-tuple-element.73), channel_id=1, source_target_pairs={{0,2},{1,3},{2,0},{3,1},{4,6},{5,7},{6,4},{7,5},{8,10},{9,11},{10,... | collective-permute-start | bytes 786440 | tf_op jit(solution)/shard_map/ppermute | solution.py:88
  144.0 14.4 %collective-permute-start.21 = (bf16[256,512]{1,0:T(8,128)(2,1)S(1)}, bf16[256,512]{1,0:T(8,128)(2,1)S(1)}, u32[]{:S(2)}, u32[]{:S(2)}) collective-permute-start(bf16[256,512]{1,0:T(8,128)(2,1)S(1)} %get-tuple-element.74), channel_id=1, source_target_pairs={{0,4},{1,5},{2,6},{3,7},{4,0},{5,1},{6,2},{7,3},{8,12},{9,13},{10,... | collective-permute-start | bytes 786440 | tf_op jit(solution)/shard_map/ppermute | solution.py:88
  144.6 13.9 %collective-permute-start.22 = (bf16[256,512]{1,0:T(8,128)(2,1)S(1)}, bf16[256,512]{1,0:T(8,128)(2,1)S(1)}, u32[]{:S(2)}, u32[]{:S(2)}) collective-permute-start(bf16[256,512]{1,0:T(8,128)(2,1)S(1)} %get-tuple-element.75), channel_id=1, source_target_pairs={{0,6},{1,7},{2,4},{3,5},{4,2},{5,3},{6,0},{7,1},{8,14},{9,15},{10,... | collective-permute-start | bytes 786440 | tf_op jit(solution)/shard_map/ppermute | solution.py:88
  158.6 10.2 %collective-permute-start.28 = (bf16[256,512]{1,0:T(8,128)(2,1)S(1)}, bf16[256,512]{1,0:T(8,128)(2,1)S(1)}, u32[]{:S(2)}, u32[]{:S(2)}) collective-permute-start(bf16[256,512]{1,0:T(8,128)(2,1)S(1)} %add_pieces.3.refs_0_), channel_id=1, source_target_pairs={{0,6},{1,7},{2,4},{3,5},{4,2},{5,3},{6,0},{7,1},{8,14},{9,15},{10,... | collective-permute-start | bytes 786440 | tf_op jit(solution)/shard_map/ppermute | solution.py:88
  160.2 12.7 %collective-permute-start.26 = (bf16[256,512]{1,0:T(8,128)(2,1)S(1)}, bf16[256,512]{1,0:T(8,128)(2,1)S(1)}, u32[]{:S(2)}, u32[]{:S(2)}) collective-permute-start(bf16[256,512]{1,0:T(8,128)(2,1)S(1)} %add_pieces.3.refs_0_), channel_id=1, source_target_pairs={{0,4},{1,5},{2,6},{3,7},{4,0},{5,1},{6,2},{7,3},{8,12},{9,13},{10,... | collective-permute-start | bytes 786440 | tf_op jit(solution)/shard_map/ppermute | solution.py:88
  161.7 11.3 %collective-permute-start.24 = (bf16[256,512]{1,0:T(8,128)(2,1)S(1)}, bf16[256,512]{1,0:T(8,128)(2,1)S(1)}, u32[]{:S(2)}, u32[]{:S(2)}) collective-permute-start(bf16[256,512]{1,0:T(8,128)(2,1)S(1)} %add_pieces.3.refs_0_), channel_id=1, source_target_pairs={{0,2},{1,3},{2,0},{3,1},{4,6},{5,7},{6,4},{7,5},{8,10},{9,11},{10,... | collective-permute-start | bytes 786440 | tf_op jit(solution)/shard_map/ppermute | solution.py:88
  162.1 19.2 %collective-permute-start.23 = (bf16[256,512]{1,0:T(8,128)(2,1)S(1)}, bf16[256,512]{1,0:T(8,128)(2,1)S(1)}, u32[]{:S(2)}, u32[]{:S(2)}) collective-permute-start(bf16[256,512]{1,0:T(8,128)(2,1)S(1)} %add_pieces.3.refs_0_), channel_id=1, source_target_pairs={{0,1},{1,0},{2,3},{3,2},{4,5},{5,4},{6,7},{7,6},{8,9},{9,8},{10,11... | collective-permute-start | bytes 786440 | tf_op jit(solution)/shard_map/ppermute | solution.py:88
  168.8 12.6 %collective-permute-start.29 = (bf16[256,512]{1,0:T(8,128)(2,1)S(1)}, bf16[256,512]{1,0:T(8,128)(2,1)S(1)}, u32[]{:S(2)}, u32[]{:S(2)}) collective-permute-start(bf16[256,512]{1,0:T(8,128)(2,1)S(1)} %collective-permute-done.28.refs_3_), channel_id=1, source_target_pairs={{0,1},{1,0},{2,3},{3,2},{4,5},{5,4},{6,7},{7,6},{8,9},{9,8},{10,11... | collective-permute-start | bytes 786440 | tf_op jit(solution)/shard_map/ppermute | solution.py:88
  172.9 8.4 %collective-permute-start.27 = (bf16[256,512]{1,0:T(8,128)(2,1)S(1)}, bf16[256,512]{1,0:T(8,128)(2,1)S(1)}, u32[]{:S(2)}, u32[]{:S(2)}) collective-permute-start(bf16[256,512]{1,0:T(8,128)(2,1)S(1)} %collective-permute-done.26.refs_2_), channel_id=1, source_target_pairs={{0,1},{1,0},{2,3},{3,2},{4,5},{5,4},{6,7},{7,6},{8,9},{9,8},{10,11... | collective-permute-start | bytes 786440 | tf_op jit(solution)/shard_map/ppermute | solution.py:88
  173.0 8.3 %collective-permute-start.25 = (bf16[256,512]{1,0:T(8,128)(2,1)S(1)}, bf16[256,512]{1,0:T(8,128)(2,1)S(1)}, u32[]{:S(2)}, u32[]{:S(2)}) collective-permute-start(bf16[256,512]{1,0:T(8,128)(2,1)S(1)} %collective-permute-done.24.refs_1_), channel_id=1, source_target_pairs={{0,1},{1,0},{2,3},{3,2},{4,5},{5,4},{6,7},{7,6},{8,9},{9,8},{10,11... | collective-permute-start | bytes 786440 | tf_op jit(solution)/shard_map/ppermute | solution.py:88
  189.5 1.2 collective-permute-start.30
  190.8 4.5 %collective-permute-start.33 = (f32[2,256]{1,0:T(2,128)S(1)}, f32[2,256]{1,0:T(2,128)S(1)}, u32[]{:S(2)}, u32[]{:S(2)}) collective-permute-start(f32[2,256]{1,0:T(2,128)S(1)} %norm_pair.1.refs_0_), channel_id=1, source_target_pairs={{0,6},{1,7},{2,4},{3,5},{4,2},{5,3},{6,0},{7,1},{8,14},{9,15},{10,... | collective-permute-start | bytes 6152 | tf_op jit(solution)/shard_map/ppermute | solution.py:88
  192.2 3.6 %collective-permute-start.32 = (f32[2,256]{1,0:T(2,128)S(1)}, f32[2,256]{1,0:T(2,128)S(1)}, u32[]{:S(2)}, u32[]{:S(2)}) collective-permute-start(f32[2,256]{1,0:T(2,128)S(1)} %norm_pair.1.refs_0_), channel_id=1, source_target_pairs={{0,4},{1,5},{2,6},{3,7},{4,0},{5,1},{6,2},{7,3},{8,12},{9,13},{10,... | collective-permute-start | bytes 6152 | tf_op jit(solution)/shard_map/ppermute | solution.py:88
  193.7 3.6 %collective-permute-start.31 = (f32[2,256]{1,0:T(2,128)S(1)}, f32[2,256]{1,0:T(2,128)S(1)}, u32[]{:S(2)}, u32[]{:S(2)}) collective-permute-start(f32[2,256]{1,0:T(2,128)S(1)} %norm_pair.1.refs_0_), channel_id=1, source_target_pairs={{0,2},{1,3},{2,0},{3,1},{4,6},{5,7},{6,4},{7,5},{8,10},{9,11},{10,... | collective-permute-start | bytes 6152 | tf_op jit(solution)/shard_map/ppermute | solution.py:88

commit v4 on v3

--- a/solution.py
+++ b/solution.py
@@ -37,8 +37,7 @@
     return terms[0]
 
 
-def per_row(scalars, row, width):
-    line = scalars[row : row + 1, :]
+def per_row(line, width):
     return jnp.broadcast_to(line, (width, line.shape[1])).T
 
 
@@ -90,11 +89,9 @@
     ahead = [(i, (i + 1) % doms) for i in range(doms)]
     behind = [((i + 1) % doms, i) for i in range(doms)]
 
-    scalars = jnp.stack(
-        [jnp.tile(energies, perts), first_step.reshape(columns), second_step.reshape(columns)]
-    )
-
-    def flatten_body(source, early, placed, flat, *edges):
+    lines = (energies.reshape(1, orbs), first_step, second_step)
+
+    def flatten_body(source, placed, flat, *edges):
         def rows_step(p, carry):
             rows = pl.ds(pl.multiple_of(p * orbs, orbs), orbs)
             for x in range(planes):
@@ -114,7 +111,7 @@
 
     flat_response, *edges1 = run(
         flatten_body,
-        [(response.reshape(columns, planes, gz, gy), "v"), (scalars, "a"), (where, "a")],
+        [(response.reshape(columns, planes, gz, gy), "v"), (where, "a")],
         [((columns, cells), f32)]
         + [((columns, gz * 2 * gy), bf16)] * 2,
         limit=8,
@@ -209,7 +206,8 @@
     locked_flat = pltpu.with_memory_space_constraint(locked_flat, pltpu.HBM)
 
     def stencil_body(field, pot, scal, out, energy):
-        energy[...] = per_row(scal, 0, gy)
+        for p in range(perts):
+            energy[p * orbs : (p + 1) * orbs, :] = per_row(scal[...], gy)
         block = 32
 
         def rows_step(i, carry):
@@ -244,7 +242,7 @@
     def stencil(field):
         (out,) = run(
             stencil_body,
-            [(field, "v"), (flat_potential, "v"), (scalars, "v")],
+            [(field, "v"), (flat_potential, "v"), (lines[0], "v")],
             [((columns, cells), f32)],
             scratch=[pltpu.VMEM((columns, gy), f32)],
             limit=1,
@@ -541,7 +539,8 @@
             for z in range(base, base + part_z):
                 stripe_copy(start, lock, buf, sems, z).start()
             collect(where_ref, pieces, held)
-            step_rows[...] = per_row(scal, 1, gy)
+            for p in range(perts):
+                step_rows[p * orbs : (p + 1) * orbs, :] = per_row(scal[p : p + 1, :], gy)
             lanes[...] = jnp.zeros_like(lanes)
 
             def step(z, carry):
@@ -587,7 +586,7 @@
                 (rhs, "v"),
                 (field, "v"),
                 (flat_occupied, "v"),
-                (scalars, "v"),
+                (lines[1], "v"),
             ]
             + extra,
             [
@@ -716,33 +715,44 @@
 
     def final_body(*refs):
         sums = tree_sum([r[...] for r in refs[:chips]])
-        mid, res1, res2, scal, out, steps, blends = refs[chips:]
+        mid, res1, res2, scal, out, steps, blends, ready, sems = refs[chips:]
         ratio = sums[1:2, :] / sums[0:1, :]
-        blend = scal[2:3, :] * ratio
-        steps[...] = per_row(scal, 2, gy)
-        blends[...] = jnp.broadcast_to(blend, (gy, columns)).T
-        block = 64 if columns % 64 == 0 else columns
+        blends[...] = jnp.broadcast_to(ratio, (gy, columns)).T
+        for p in range(perts):
+            steps[p * orbs : (p + 1) * orbs, :] = per_row(scal[p : p + 1, :], gy)
+
+        def flush(i):
+            rows = pl.ds(pl.multiple_of(i * orbs, orbs), orbs)
+            return pltpu.make_async_copy(ready.at[i], out.at[rows], sems.at[i])
 
         def rows_step(i, carry):
-            rows = pl.ds(pl.multiple_of(i * block, block), block)
+            rows = pl.ds(pl.multiple_of(i * orbs, orbs), orbs)
             step, mix = steps[rows, :], blends[rows, :]
             for x in range(planes):
                 values = []
                 for z in range(gz):
                     cut = slice(col(z, x), col(z, x) + gy)
-                    values.append(mid[rows, cut] + step * res2[rows, cut] + mix * res1[rows, cut])
-                out[rows, x] = jnp.concatenate(values, axis=1).reshape(block, gz, gy)
+                    values.append(mid[rows, cut] + step * (res2[rows, cut] + mix * res1[rows, cut]))
+                ready[i, :, x] = jnp.concatenate(values, axis=1).reshape(orbs, gz, gy)
+            flush(i).start()
             return carry
 
-        lax.fori_loop(0, columns // block, rows_step, 0)
+        lax.fori_loop(0, perts, rows_step, 0)
+        for p in range(perts):
+            flush(p).wait()
 
     (new_response,) = run(
         final_body,
         [(n, "v") for n in all_norms]
-        + [(middle, "v"), (first_res, "v"), (second_res, "v"), (scalars, "v")],
-        [((columns, planes, gz, gy), f32)],
-        scratch=[pltpu.VMEM((columns, gy), f32), pltpu.VMEM((columns, gy), f32)],
-        limit=5,
+        + [(middle, "v"), (first_res, "v"), (second_res, "v"), (lines[2], "v")],
+        [((columns, planes, gz, gy), f32, "h")],
+        scratch=[
+            pltpu.VMEM((columns, gy), f32),
+            pltpu.VMEM((columns, gy), f32),
+            pltpu.VMEM((perts, orbs, planes, gz, gy), f32),
+            pltpu.SemaphoreType.DMA((perts,)),
+        ],
+        limit=8,
         name="final",
     )
     return new_response.reshape(response.shape), response_potential

time: 204 us -> 201 us (0.985)
  local copies, waits for them, and re-layouts: 4.46 us -> 2.22 us
    another operation x4 -> x0, local copies, waits for them, and re-layouts: 2.26 us -> none  [the longest x3 1.61 us: local(): jnp.stack([jnp.tile(energies, perts), first_step.reshape(columns), second...]
  transfers between devices with their start and end apart: 34 -> 34, of which waited for: 15 -> 14; matrix products, arithmetic and copies ran while one was open for 0% -> 0% of each run, Pallas kernels for 38% -> 39%
where the time goes in v4:
time: 201 us
  Pallas kernels  113 us (56%)
  waiting for transfers between devices  51.6 us (26%)
  starting transfers between devices  32.5 us (16%)
  local copies, waits for them, and re-layouts  2.22 us (1%)
    pallas_call x23, Pallas kernels, run(): pl.pallas_call(body, in_specs=[pl.BlockSpec(memory_space=kinds[kind]) for...  113 us
    ppermute x28, waiting for transfers between devices, swap(): return lax.ppermute(array, axis, [(i, i ^ mask) for i in range(count)])  51.6 us
    ppermute x28, starting transfers between devices, swap(): return lax.ppermute(array, axis, [(i, i ^ mask) for i in range(count)])  23.7 us
    ppermute x3, starting transfers between devices, halos_of(): lax.ppermute(low_edge, 'dom', behind)  8.25 us
  transfers between devices with their start and end apart: 34, of which 14 were waited for; matrix products, arithmetic and copies ran while one was open for 0% of the time, Pallas kernels for 39%

profile of v4, /device:TPU:0, one launch (start us, length us, event | category | flops | bytes accessed | tf_op | source)
XLA Modules:
  0.0 201.1 jit_solution(2963039862395868587)
XLA Ops:
  0.7 2.2 %copy-done = f32[4,64,4,8,128]{4,3,2,1,0:T(8,128)S(1)} copy-done((f32[4,64,4,8,128]{4,3,2,1,0:T(8,128)S(1)}, f32[4,64,4,8,128]{4,3,2,1,0:T(8,128)}, u32[]{:S(2)}) %copy-start) | copy-done | bytes 4194328
  2.9 1.3 flatten.1
  4.7 3.0 %collective-permute-start.1 = (bf16[256,2048]{1,0:T(8,128)(2,1)S(1)}, bf16[256,2048]{1,0:T(8,128)(2,1)S(1)}, u32[]{:S(2)}, u32[]{:S(2)}) collective-permute-start(bf16[256,2048]{1,0:T(8,128)(2,1)S(1)} %get-tuple-element.45), channel_id=1, source_target_pairs={{1,0},{2,1},{3,2},{4,3},{5,4},{6,5},{7,6},{0,7},{9,8},{10,9},{11,1... | collective-permute-start | bytes 3145736 | tf_op jit(solution)/shard_map/ppermute | solution.py:122
  7.7 24.0 %relay.1.lock.refs_4_ = bf16[4096,4096]{1,0:T(8,128)(2,1)} custom-call(bf16[4096,4,8,128]{3,2,1,0:T(8,128)(2,1)} %source.1), custom_call_target="tpu_custom_call" | custom-call | tf_op jit(solution)/shard_map/relay/pallas_call | solution.py:18
  32.1 5.0 %stencil.2.part_ref = f32[256,4096]{1,0:T(8,128)S(1)} custom-call(f32[256,4096]{1,0:T(8,128)S(1)} %get-tuple-element.42.field.refs_7_, f32[1,4096]{1,0:T(1,128)S(1)} %get-tuple-element.43.pot, f32[1,64]{1,0:T(1,128)S(1)} %bitcast.6), custom_call_target="tpu_custom_call" | custom-call | tf_op jit(solution)/shard_map/stencil/pallas_call | solution.py:18
  37.1 7.9 %margin_other.1 = (f32[256,4096]{1,0:T(8,128)S(1)}, bf16[256,4096]{1,0:T(8,128)(2,1)S(1)}, bf16[256,2048]{1,0:T(8,128)(2,1)S(1)}) custom-call(s32[2]{0:T(128)S(1)} %pad_add_fusion.placed.where_ref, f32[256,4096]{1,0:T(8,128)S(1)} %stencil.2.part_ref, bf16[256,2048]{1,0:T(8,128)(2,1)S(1)} %collective-permute-done.low_ref, ...), custom_call_target="tpu_custom_call", output_to_operand_aliasing={{0}: (1, {})} | custom-call | tf_op jit(solution)/shard_map/margin_other/pallas_call | solution.py:18
  45.1 7.9 %margin_own.1.own_ref = f32[256,2048]{1,0:T(8,128)S(1)} custom-call(s32[2]{0:T(128)S(1)} %pad_add_fusion.placed.where_ref, bf16[256,4096]{1,0:T(8,128)(2,1)S(1)} %get-tuple-element.48.rounded_ref, bf16[4096,4096]{1,0:T(8,128)(2,1)} %relay.1.lock.refs_4_), custom_call_target="tpu_custom_call" | custom-call | tf_op jit(solution)/shard_map/margin_own/pallas_call | solution.py:18
  53.2 1.4 collective-permute-start.3
  54.6 1.5 collective-permute-start.4
  56.1 0.9 collective-permute-start.5
  57.0 5.4 %collective-permute-done.3.refs_1_ = bf16[256,512]{1,0:T(8,128)(2,1)S(1)} collective-permute-done((bf16[256,512]{1,0:T(8,128)(2,1)S(1)}, bf16[256,512]{1,0:T(8,128)(2,1)S(1)}, u32[]{:S(2)}, u32[]{:S(2)}) %collective-permute-start.3) | collective-permute-done | bytes 262176 | tf_op jit(solution)/shard_map/ppermute | solution.py:87
  62.4 5.3 %collective-permute-done.4.refs_2_ = bf16[256,512]{1,0:T(8,128)(2,1)S(1)} collective-permute-done((bf16[256,512]{1,0:T(8,128)(2,1)S(1)}, bf16[256,512]{1,0:T(8,128)(2,1)S(1)}, u32[]{:S(2)}, u32[]{:S(2)}) %collective-permute-start.4) | collective-permute-done | bytes 262176 | tf_op jit(solution)/shard_map/ppermute | solution.py:87
  67.7 1.6 collective-permute-done.5.refs_3_
  69.4 1.8 collective-permute-start.11
  71.5 1.4 collective-permute-start.7
  73.0 6.7 %collective-permute-done.11.refs_3_ = bf16[256,512]{1,0:T(8,128)(2,1)S(1)} collective-permute-done((bf16[256,512]{1,0:T(8,128)(2,1)S(1)}, bf16[256,512]{1,0:T(8,128)(2,1)S(1)}, u32[]{:S(2)}, u32[]{:S(2)}) %collective-permute-start.11) | collective-permute-done | bytes 262176 | tf_op jit(solution)/shard_map/ppermute | solution.py:87
  79.7 4.3 %collective-permute-done.9.refs_2_ = bf16[256,512]{1,0:T(8,128)(2,1)S(1)} collective-permute-done((bf16[256,512]{1,0:T(8,128)(2,1)S(1)}, bf16[256,512]{1,0:T(8,128)(2,1)S(1)}, u32[]{:S(2)}, u32[]{:S(2)}) %collective-permute-start.9) | collective-permute-done | bytes 262176 | tf_op jit(solution)/shard_map/ppermute | solution.py:87
  84.5 7.9 %remove_own.2.refs_5_ = f32[256,4096]{1,0:T(8,128)S(1)} custom-call(s32[2]{0:T(128)S(1)} %pad_add_fusion.placed.where_ref, bf16[256,512]{1,0:T(8,128)(2,1)S(1)} %add_pieces.2.refs_0_, bf16[256,512]{1,0:T(8,128)(2,1)S(1)} %collective-permute-done.7.refs_1_, bf16[256,512]{1,0:T(8,128)(2,1)S(1)} %collective-permute-done.9.refs_2_, ...), custom_call_target="tpu_custom_call" | custom-call | tf_op jit(solution)/shard_map/remove_own/pallas_call | solution.py:18
  92.4 6.1 %first_finish.2 = (f32[256,4096]{1,0:T(8,128)S(1)}, f32[256,4096]{1,0:T(8,128)S(1)}, bf16[256,1024]{1,0:T(8,128)(2,1)S(1)}, bf16[256,1024]{1,0:T(8,128)(2,1)S(1)...) custom-call(s32[2]{0:T(128)S(1)} %pad_add_fusion.placed.where_ref, ...), custom_call_target="tpu_custom_call", output_to_operand_aliasing={{0}: (7, {}), {1}: (8, {})} | custom-call | tf_op jit(solution)/shard_map/first_finish/pallas_call | solution.py:18
  98.6 2.6 %collective-permute-start.14 = (bf16[256,1024]{1,0:T(8,128)(2,1)S(1)}, bf16[256,1024]{1,0:T(8,128)(2,1)S(1)}, u32[]{:S(2)}, u32[]{:S(2)}) collective-permute-start(bf16[256,1024]{1,0:T(8,128)(2,1)S(1)} %get-tuple-element.61), channel_id=1, source_target_pairs={{1,0},{2,1},{3,2},{4,3},{5,4},{6,5},{7,6},{0,7},{9,8},{10,9},{11,1... | collective-permute-start | bytes 1572872 | tf_op jit(solution)/shard_map/ppermute | solution.py:122
  101.2 6.1 %first_finish.3 = (f32[256,4096]{1,0:T(8,128)S(1)}, f32[256,4096]{1,0:T(8,128)S(1)}, bf16[256,1024]{1,0:T(8,128)(2,1)S(1)}, bf16[256,1024]{1,0:T(8,128)(2,1)S(1)...) custom-call(s32[2]{0:T(128)S(1)} %pad_add_fusion.placed.where_ref, ...), custom_call_target="tpu_custom_call", output_to_operand_aliasing={{0}: (7, {}), {1}: (8, {})} | custom-call | tf_op jit(solution)/shard_map/first_finish/pallas_call | solution.py:18
  107.4 2.6 %collective-permute-start.18 = (bf16[256,1024]{1,0:T(8,128)(2,1)S(1)}, bf16[256,1024]{1,0:T(8,128)(2,1)S(1)}, u32[]{:S(2)}, u32[]{:S(2)}) collective-permute-start(bf16[256,1024]{1,0:T(8,128)(2,1)S(1)} %get-tuple-element.67), channel_id=1, source_target_pairs={{1,0},{2,1},{3,2},{4,3},{5,4},{6,5},{7,6},{0,7},{9,8},{10,9},{11,1... | collective-permute-start | bytes 1572872 | tf_op jit(solution)/shard_map/ppermute | solution.py:122
  110.0 1.5 collective-permute-start.15
  111.6 2.4 %collective-permute-done.15.two = bf16[4,4096]{1,0:T(4,128)(2,1)S(1)} collective-permute-done((bf16[4,4096]{1,0:T(4,128)(2,1)S(1)}, bf16[4,4096]{1,0:T(4,128)(2,1)S(1)}, u32[]{:S(2)}, u32[]{:S(2)}) %collective-permute-start.15) | collective-permute-done | bytes 32800 | tf_op jit(solution)/shard_map/ppermute | solution.py:87
  114.0 3.0 %collective-permute-start.16 = (bf16[4,4096]{1,0:T(4,128)(2,1)S(1)}, bf16[4,4096]{1,0:T(4,128)(2,1)S(1)}, u32[]{:S(2)}, u32[]{:S(2)}) collective-permute-start(bf16[4,4096]{1,0:T(4,128)(2,1)S(1)} %add_density.1.one), channel_id=1, source_target_pairs={{0,16},{8,24},{16,0},{24,8},{1,17},{9,25},{17,1},{25,9},{2,18},{10... | collective-permute-start | bytes 98312 | tf_op jit(solution)/shard_map/ppermute | solution.py:87
  116.9 5.2 %stencil.3.part_ref = f32[256,4096]{1,0:T(8,128)S(1)} custom-call(f32[256,4096]{1,0:T(8,128)S(1)} %get-tuple-element.59.field.refs_4_, f32[1,4096]{1,0:T(1,128)S(1)} %get-tuple-element.43.pot, f32[1,64]{1,0:T(1,128)S(1)} %bitcast.7), custom_call_target="tpu_custom_call" | custom-call | tf_op jit(solution)/shard_map/stencil/pallas_call | solution.py:18
  122.1 0.7 potential.1
  122.8 8.1 %margin_early.1 = (f32[256,4096]{1,0:T(8,128)S(1)}, f32[256,4096]{1,0:T(8,128)S(1)}) custom-call(s32[2]{0:T(128)S(1)} %pad_add_fusion.placed.where_ref, f32[256,4096]{1,0:T(8,128)S(1)} %stencil.3.part_ref, bf16[256,1024]{1,0:T(8,128)(2,1)S(1)} %collective-permute-done.13.low, ...), custom_call_target="tpu_custom_call", output_to_operand_aliasing={{0}: (1, {})} | custom-call | tf_op jit(solution)/shard_map/margin_early/pallas_call | solution.py:18
  131.0 5.2 %margin_late.1 = (f32[256,4096]{1,0:T(8,128)S(1)}, bf16[256,2048]{1,0:T(8,128)(2,1)S(1)}, bf16[256,2048]{1,0:T(8,128)(2,1)S(1)}) custom-call(s32[2]{0:T(128)S(1)} %pad_add_fusion.placed.where_ref, f32[256,4096]{1,0:T(8,128)S(1)} %get-tuple-element.65.part_ref, bf16[256,1024]{1,0:T(8,128)(2,1)S(1)} %collective-permute-done.17.low, ...), custom_call_target="tpu_custom_call", output_to_operand_aliasing={{0}: (1, {})} | custom-call | tf_op jit(solution)/shard_map/margin_late/pallas_call | solution.py:18
  136.3 5.3 %margin_late_own.1.own_ref = f32[256,2048]{1,0:T(8,128)S(1)} custom-call(s32[2]{0:T(128)S(1)} %pad_add_fusion.placed.where_ref, bf16[256,2048]{1,0:T(8,128)(2,1)S(1)} %get-tuple-element.70.rounded_ref, bf16[4096,4096]{1,0:T(8,128)(2,1)} %relay.1.lock.refs_4_, f32[256,4096]{1,0:T(8,128)S(1)} %get-tuple-element.69.early_ref), custom_call_target="tpu_custom_call" | custom-call | tf_op jit(solution)/shard_map/margin_late_own/pallas_call | solution.py:18
  141.8 0.6 collective-permute-start.21
  142.4 2.9 %collective-permute-start.22 = (bf16[256,512]{1,0:T(8,128)(2,1)S(1)}, bf16[256,512]{1,0:T(8,128)(2,1)S(1)}, u32[]{:S(2)}, u32[]{:S(2)}) collective-permute-start(bf16[256,512]{1,0:T(8,128)(2,1)S(1)} %get-tuple-element.75), channel_id=1, source_target_pairs={{0,6},{1,7},{2,4},{3,5},{4,2},{5,3},{6,0},{7,1},{8,14},{9,15},{10,... | collective-permute-start | bytes 786440 | tf_op jit(solution)/shard_map/ppermute | solution.py:87
  145.3 5.6 %collective-permute-done.20.refs_1_ = bf16[256,512]{1,0:T(8,128)(2,1)S(1)} collective-permute-done((bf16[256,512]{1,0:T(8,128)(2,1)S(1)}, bf16[256,512]{1,0:T(8,128)(2,1)S(1)}, u32[]{:S(2)}, u32[]{:S(2)}) %collective-permute-start.20) | collective-permute-done | bytes 262176 | tf_op jit(solution)/shard_map/ppermute | solution.py:87
  150.9 5.3 %collective-permute-done.21.refs_2_ = bf16[256,512]{1,0:T(8,128)(2,1)S(1)} collective-permute-done((bf16[256,512]{1,0:T(8,128)(2,1)S(1)}, bf16[256,512]{1,0:T(8,128)(2,1)S(1)}, u32[]{:S(2)}, u32[]{:S(2)}) %collective-permute-start.21) | collective-permute-done | bytes 262176 | tf_op jit(solution)/shard_map/ppermute | solution.py:87
  156.3 1.7 collective-permute-start.28
  158.0 1.5 collective-permute-start.26
  159.9 6.7 %collective-permute-done.28.refs_3_ = bf16[256,512]{1,0:T(8,128)(2,1)S(1)} collective-permute-done((bf16[256,512]{1,0:T(8,128)(2,1)S(1)}, bf16[256,512]{1,0:T(8,128)(2,1)S(1)}, u32[]{:S(2)}, u32[]{:S(2)}) %collective-permute-start.28) | collective-permute-done | bytes 262176 | tf_op jit(solution)/shard_map/ppermute | solution.py:87
  166.5 4.2 %collective-permute-done.26.refs_2_ = bf16[256,512]{1,0:T(8,128)(2,1)S(1)} collective-permute-done((bf16[256,512]{1,0:T(8,128)(2,1)S(1)}, bf16[256,512]{1,0:T(8,128)(2,1)S(1)}, u32[]{:S(2)}, u32[]{:S(2)}) %collective-permute-start.26) | collective-permute-done | bytes 262176 | tf_op jit(solution)/shard_map/ppermute | solution.py:87
  171.3 7.9 %remove_own.3.refs_5_ = f32[256,4096]{1,0:T(8,128)S(1)} custom-call(s32[2]{0:T(128)S(1)} %pad_add_fusion.placed.where_ref, bf16[256,512]{1,0:T(8,128)(2,1)S(1)} %add_pieces.3.refs_0_, bf16[256,512]{1,0:T(8,128)(2,1)S(1)} %collective-permute-done.24.refs_1_, bf16[256,512]{1,0:T(8,128)(2,1)S(1)} %collective-permute-done.26.refs_2_, ...), custom_call_target="tpu_custom_call" | custom-call | tf_op jit(solution)/shard_map/remove_own/pallas_call | solution.py:18
  179.2 8.2 %second_finish.1 = (f32[256,4096]{1,0:T(8,128)S(1)}, f32[2,256]{1,0:T(2,128)S(1)}) custom-call(s32[2]{0:T(128)S(1)} %pad_add_fusion.placed.where_ref, bf16[256,512]{1,0:T(8,128)(2,1)S(1)} %collective-permute-done.23.refs_0_, bf16[256,512]{1,0:T(8,128)(2,1)S(1)} %collective-permute-done.25.refs_1_, ...), custom_call_target="tpu_custom_call", output_to_operand_aliasing={{0}: (7, {})} | custom-call | tf_op jit(solution)/shard_map/second_finish/pallas_call | solution.py:18
  187.4 1.1 collective-permute-done.30.two
  188.6 1.4 collective-permute-start.33
  190.0 1.5 collective-permute-start.32
  191.5 0.6 collective-permute-start.31
  192.1 1.0 collective-permute-done.33.refs_3_
  193.1 0.5 collective-permute-done.32.refs_2_
  193.6 1.5 collective-permute-done.31.refs_1_
  195.1 5.8 %final.1 = f32[256,4,8,128]{3,2,1,0:T(8,128)} custom-call(f32[2,256]{1,0:T(2,128)S(1)} %norm_pair.1.refs_0_, f32[2,256]{1,0:T(2,128)S(1)} %collective-permute-done.31.refs_1_, f32[2,256]{1,0:T(2,128)S(1)} %collective-permute-done.32.refs_2_, f32[2,256]{1,0:T(2,128)S(1)} %collective-permute-done.33.refs_3_, f32[256,4096]{1,0:T(8,128)S(1)} %get-tuple-element.59.field.refs_4_, ...), custom_call_target="tpu_custom_call" | custom-call | tf_op jit(solution)/shard_map/final/pallas_call | solution.py:18
  (60 shorter events, 3.7 us)
Async XLA Ops:
  0.7 2.2 %copy-start = (f32[4,64,4,8,128]{4,3,2,1,0:T(8,128)S(1)}, f32[4,64,4,8,128]{4,3,2,1,0:T(8,128)}, u32[]{:S(2)}) copy-start(f32[4,64,4,8,128]{4,3,2,1,0:T(8,128)} %param.9) | copy-start | bytes 12582916
  4.2 32.9 %collective-permute-start = (bf16[256,2048]{1,0:T(8,128)(2,1)S(1)}, bf16[256,2048]{1,0:T(8,128)(2,1)S(1)}, u32[]{:S(2)}, u32[]{:S(2)}) collective-permute-start(bf16[256,2048]{1,0:T(8,128)(2,1)S(1)} %get-tuple-element.44), channel_id=1, source_target_pairs={{0,1},{1,2},{2,3},{3,4},{4,5},{5,6},{6,7},{7,0},{8,9},{9,10},{10,1... | collective-permute-start | bytes 3145736 | tf_op jit(solution)/shard_map/ppermute | solution.py:122
  4.7 27.0 %copy-start.1 = (f32[64,4,8,128]{3,2,1,0:T(8,128)S(1)}, f32[64,4,8,128]{3,2,1,0:T(8,128)}, u32[]{:S(2)}) copy-start(f32[64,4,8,128]{3,2,1,0:T(8,128)} %occ.1) | copy-start | bytes 3145732
  4.7 27.0 %copy-start.2 = (f32[4,4,8,128]{3,2,1,0:T(8,128)S(1)}, f32[4,4,8,128]{3,2,1,0:T(8,128)}, u32[]{:S(2)}) copy-start(f32[4,4,8,128]{3,2,1,0:T(8,128)} %pert.1) | copy-start | bytes 196612
  4.7 27.0 %copy-start.3 = (f32[4,8,128]{2,1,0:T(8,128)S(1)}, f32[4,8,128]{2,1,0:T(8,128)}, u32[]{:S(2)}) copy-start(f32[4,8,128]{2,1,0:T(8,128)} %pot.1) | copy-start | bytes 49156
  4.7 27.1 %copy-start.4 = (f32[4,8,128]{2,1,0:T(8,128)S(1)}, f32[4,8,128]{2,1,0:T(8,128)}, u32[]{:S(2)}) copy-start(f32[4,8,128]{2,1,0:T(8,128)} %xc.1) | copy-start | bytes 49156
  4.7 27.4 %copy-start.7 = (f32[64]{0:T(128)S(1)}, f32[64]{0:T(128)}, u32[]{:S(2)}) copy-start(f32[64]{0:T(128)} %param.15) | copy-start | bytes 772
  4.7 32.4 %collective-permute-start.1 = (bf16[256,2048]{1,0:T(8,128)(2,1)S(1)}, bf16[256,2048]{1,0:T(8,128)(2,1)S(1)}, u32[]{:S(2)}, u32[]{:S(2)}) collective-permute-start(bf16[256,2048]{1,0:T(8,128)(2,1)S(1)} %get-tuple-element.45), channel_id=1, source_target_pairs={{1,0},{2,1},{3,2},{4,3},{5,4},{6,5},{7,6},{0,7},{9,8},{10,9},{11,1... | collective-permute-start | bytes 3145736 | tf_op jit(solution)/shard_map/ppermute | solution.py:122
  45.0 8.0 %collective-permute-start.2 = (bf16[256,2048]{1,0:T(8,128)(2,1)S(1)}, bf16[256,2048]{1,0:T(8,128)(2,1)S(1)}, u32[]{:S(2)}, u32[]{:S(2)}) collective-permute-start(bf16[256,2048]{1,0:T(8,128)(2,1)S(1)} %get-tuple-element.49), channel_id=1, source_target_pairs={{0,1},{1,0},{2,3},{3,2},{4,5},{5,4},{6,7},{7,6},{8,9},{9,8},{10,11... | collective-permute-start | bytes 3145736 | tf_op jit(solution)/shard_map/ppermute | solution.py:87
  53.2 9.2 %collective-permute-start.3 = (bf16[256,512]{1,0:T(8,128)(2,1)S(1)}, bf16[256,512]{1,0:T(8,128)(2,1)S(1)}, u32[]{:S(2)}, u32[]{:S(2)}) collective-permute-start(bf16[256,512]{1,0:T(8,128)(2,1)S(1)} %get-tuple-element.51), channel_id=1, source_target_pairs={{0,2},{1,3},{2,0},{3,1},{4,6},{5,7},{6,4},{7,5},{8,10},{9,11},{10,... | collective-permute-start | bytes 786440 | tf_op jit(solution)/shard_map/ppermute | solution.py:87
  54.6 13.1 %collective-permute-start.4 = (bf16[256,512]{1,0:T(8,128)(2,1)S(1)}, bf16[256,512]{1,0:T(8,128)(2,1)S(1)}, u32[]{:S(2)}, u32[]{:S(2)}) collective-permute-start(bf16[256,512]{1,0:T(8,128)(2,1)S(1)} %get-tuple-element.52), channel_id=1, source_target_pairs={{0,4},{1,5},{2,6},{3,7},{4,0},{5,1},{6,2},{7,3},{8,12},{9,13},{10,... | collective-permute-start | bytes 786440 | tf_op jit(solution)/shard_map/ppermute | solution.py:87
  56.1 13.2 %collective-permute-start.5 = (bf16[256,512]{1,0:T(8,128)(2,1)S(1)}, bf16[256,512]{1,0:T(8,128)(2,1)S(1)}, u32[]{:S(2)}, u32[]{:S(2)}) collective-permute-start(bf16[256,512]{1,0:T(8,128)(2,1)S(1)} %get-tuple-element.53), channel_id=1, source_target_pairs={{0,6},{1,7},{2,4},{3,5},{4,2},{5,3},{6,0},{7,1},{8,14},{9,15},{10,... | collective-permute-start | bytes 786440 | tf_op jit(solution)/shard_map/ppermute | solution.py:87
  69.4 23.0 %copy-start.5 = (f32[4,64]{1,0:T(4,128)S(1)}, f32[4,64]{1,0:T(4,128)}, u32[]{:S(2)}) copy-start(f32[4,64]{1,0:T(4,128)} %refs_9_.3) | copy-start | bytes 3076
  69.4 10.2 %collective-permute-start.11 = (bf16[256,512]{1,0:T(8,128)(2,1)S(1)}, bf16[256,512]{1,0:T(8,128)(2,1)S(1)}, u32[]{:S(2)}, u32[]{:S(2)}) collective-permute-start(bf16[256,512]{1,0:T(8,128)(2,1)S(1)} %add_pieces.2.refs_0_), channel_id=1, source_target_pairs={{0,6},{1,7},{2,4},{3,5},{4,2},{5,3},{6,0},{7,1},{8,14},{9,15},{10,... | collective-permute-start | bytes 786440 | tf_op jit(solution)/shard_map/ppermute | solution.py:87
  71.2 12.7 %collective-permute-start.9 = (bf16[256,512]{1,0:T(8,128)(2,1)S(1)}, bf16[256,512]{1,0:T(8,128)(2,1)S(1)}, u32[]{:S(2)}, u32[]{:S(2)}) collective-permute-start(bf16[256,512]{1,0:T(8,128)(2,1)S(1)} %add_pieces.2.refs_0_), channel_id=1, source_target_pairs={{0,4},{1,5},{2,6},{3,7},{4,0},{5,1},{6,2},{7,3},{8,12},{9,13},{10,... | collective-permute-start | bytes 786440 | tf_op jit(solution)/shard_map/ppermute | solution.py:87
  71.5 12.4 %collective-permute-start.7 = (bf16[256,512]{1,0:T(8,128)(2,1)S(1)}, bf16[256,512]{1,0:T(8,128)(2,1)S(1)}, u32[]{:S(2)}, u32[]{:S(2)}) collective-permute-start(bf16[256,512]{1,0:T(8,128)(2,1)S(1)} %add_pieces.2.refs_0_), channel_id=1, source_target_pairs={{0,2},{1,3},{2,0},{3,1},{4,6},{5,7},{6,4},{7,5},{8,10},{9,11},{10,... | collective-permute-start | bytes 786440 | tf_op jit(solution)/shard_map/ppermute | solution.py:87
  73.0 19.3 %collective-permute-start.6 = (bf16[256,512]{1,0:T(8,128)(2,1)S(1)}, bf16[256,512]{1,0:T(8,128)(2,1)S(1)}, u32[]{:S(2)}, u32[]{:S(2)}) collective-permute-start(bf16[256,512]{1,0:T(8,128)(2,1)S(1)} %add_pieces.2.refs_0_), channel_id=1, source_target_pairs={{0,1},{1,0},{2,3},{3,2},{4,5},{5,4},{6,7},{7,6},{8,9},{9,8},{10,11... | collective-permute-start | bytes 786440 | tf_op jit(solution)/shard_map/ppermute | solution.py:87
  79.6 12.7 %collective-permute-start.12 = (bf16[256,512]{1,0:T(8,128)(2,1)S(1)}, bf16[256,512]{1,0:T(8,128)(2,1)S(1)}, u32[]{:S(2)}, u32[]{:S(2)}) collective-permute-start(bf16[256,512]{1,0:T(8,128)(2,1)S(1)} %collective-permute-done.11.refs_3_), channel_id=1, source_target_pairs={{0,1},{1,0},{2,3},{3,2},{4,5},{5,4},{6,7},{7,6},{8,9},{9,8},{10,11... | collective-permute-start | bytes 786440 | tf_op jit(solution)/shard_map/ppermute | solution.py:87
  83.9 8.4 %collective-permute-start.10 = (bf16[256,512]{1,0:T(8,128)(2,1)S(1)}, bf16[256,512]{1,0:T(8,128)(2,1)S(1)}, u32[]{:S(2)}, u32[]{:S(2)}) collective-permute-start(bf16[256,512]{1,0:T(8,128)(2,1)S(1)} %collective-permute-done.9.refs_2_), channel_id=1, source_target_pairs={{0,1},{1,0},{2,3},{3,2},{4,5},{5,4},{6,7},{7,6},{8,9},{9,8},{10,11... | collective-permute-start | bytes 786440 | tf_op jit(solution)/shard_map/ppermute | solution.py:87
  84.0 8.4 %collective-permute-start.8 = (bf16[256,512]{1,0:T(8,128)(2,1)S(1)}, bf16[256,512]{1,0:T(8,128)(2,1)S(1)}, u32[]{:S(2)}, u32[]{:S(2)}) collective-permute-start(bf16[256,512]{1,0:T(8,128)(2,1)S(1)} %collective-permute-done.7.refs_1_), channel_id=1, source_target_pairs={{0,1},{1,0},{2,3},{3,2},{4,5},{5,4},{6,7},{7,6},{8,9},{9,8},{10,11... | collective-permute-start | bytes 786440 | tf_op jit(solution)/shard_map/ppermute | solution.py:87
  98.5 24.3 %collective-permute-start.13 = (bf16[256,1024]{1,0:T(8,128)(2,1)S(1)}, bf16[256,1024]{1,0:T(8,128)(2,1)S(1)}, u32[]{:S(2)}, u32[]{:S(2)}) collective-permute-start(bf16[256,1024]{1,0:T(8,128)(2,1)S(1)} %get-tuple-element.60), channel_id=1, source_target_pairs={{0,1},{1,2},{2,3},{3,4},{4,5},{5,6},{6,7},{7,0},{8,9},{9,10},{10,1... | collective-permute-start | bytes 1572872 | tf_op jit(solution)/shard_map/ppermute | solution.py:122
  98.6 24.3 %collective-permute-start.14 = (bf16[256,1024]{1,0:T(8,128)(2,1)S(1)}, bf16[256,1024]{1,0:T(8,128)(2,1)S(1)}, u32[]{:S(2)}, u32[]{:S(2)}) collective-permute-start(bf16[256,1024]{1,0:T(8,128)(2,1)S(1)} %get-tuple-element.61), channel_id=1, source_target_pairs={{1,0},{2,1},{3,2},{4,3},{5,4},{6,5},{7,6},{0,7},{9,8},{10,9},{11,1... | collective-permute-start | bytes 1572872 | tf_op jit(solution)/shard_map/ppermute | solution.py:122
  107.3 23.7 %collective-permute-start.17 = (bf16[256,1024]{1,0:T(8,128)(2,1)S(1)}, bf16[256,1024]{1,0:T(8,128)(2,1)S(1)}, u32[]{:S(2)}, u32[]{:S(2)}) collective-permute-start(bf16[256,1024]{1,0:T(8,128)(2,1)S(1)} %get-tuple-element.66), channel_id=1, source_target_pairs={{0,1},{1,2},{2,3},{3,4},{4,5},{5,6},{6,7},{7,0},{8,9},{9,10},{10,1... | collective-permute-start | bytes 1572872 | tf_op jit(solution)/shard_map/ppermute | solution.py:122
  107.4 23.6 %collective-permute-start.18 = (bf16[256,1024]{1,0:T(8,128)(2,1)S(1)}, bf16[256,1024]{1,0:T(8,128)(2,1)S(1)}, u32[]{:S(2)}, u32[]{:S(2)}) collective-permute-start(bf16[256,1024]{1,0:T(8,128)(2,1)S(1)} %get-tuple-element.67), channel_id=1, source_target_pairs={{1,0},{2,1},{3,2},{4,3},{5,4},{6,5},{7,6},{0,7},{9,8},{10,9},{11,1... | collective-permute-start | bytes 1572872 | tf_op jit(solution)/shard_map/ppermute | solution.py:122
  110.0 3.9 %collective-permute-start.15 = (bf16[4,4096]{1,0:T(4,128)(2,1)S(1)}, bf16[4,4096]{1,0:T(4,128)(2,1)S(1)}, u32[]{:S(2)}, u32[]{:S(2)}) collective-permute-start(bf16[4,4096]{1,0:T(4,128)(2,1)S(1)} %get-tuple-element.62.one), channel_id=1, source_target_pairs={{0,8},{8,0},{16,24},{24,16},{1,9},{9,1},{17,25},{25,17},{2,10},{10... | collective-permute-start | bytes 98312 | tf_op jit(solution)/shard_map/ppermute | solution.py:87
  114.0 8.1 %collective-permute-start.16 = (bf16[4,4096]{1,0:T(4,128)(2,1)S(1)}, bf16[4,4096]{1,0:T(4,128)(2,1)S(1)}, u32[]{:S(2)}, u32[]{:S(2)}) collective-permute-start(bf16[4,4096]{1,0:T(4,128)(2,1)S(1)} %add_density.1.one), channel_id=1, source_target_pairs={{0,16},{8,24},{16,0},{24,8},{1,17},{9,25},{17,1},{25,9},{2,18},{10... | collective-permute-start | bytes 98312 | tf_op jit(solution)/shard_map/ppermute | solution.py:87
  136.2 5.3 %collective-permute-start.19 = (bf16[256,2048]{1,0:T(8,128)(2,1)S(1)}, bf16[256,2048]{1,0:T(8,128)(2,1)S(1)}, u32[]{:S(2)}, u32[]{:S(2)}) collective-permute-start(bf16[256,2048]{1,0:T(8,128)(2,1)S(1)} %get-tuple-element.71), channel_id=1, source_target_pairs={{0,1},{1,0},{2,3},{3,2},{4,5},{5,4},{6,7},{7,6},{8,9},{9,8},{10,11... | collective-permute-start | bytes 3145736 | tf_op jit(solution)/shard_map/ppermute | solution.py:87
  141.7 9.2 %collective-permute-start.20 = (bf16[256,512]{1,0:T(8,128)(2,1)S(1)}, bf16[256,512]{1,0:T(8,128)(2,1)S(1)}, u32[]{:S(2)}, u32[]{:S(2)}) collective-permute-start(bf16[256,512]{1,0:T(8,128)(2,1)S(1)} %get-tuple-element.73), channel_id=1, source_target_pairs={{0,2},{1,3},{2,0},{3,1},{4,6},{5,7},{6,4},{7,5},{8,10},{9,11},{10,... | collective-permute-start | bytes 786440 | tf_op jit(solution)/shard_map/ppermute | solution.py:87
  141.8 14.4 %collective-permute-start.21 = (bf16[256,512]{1,0:T(8,128)(2,1)S(1)}, bf16[256,512]{1,0:T(8,128)(2,1)S(1)}, u32[]{:S(2)}, u32[]{:S(2)}) collective-permute-start(bf16[256,512]{1,0:T(8,128)(2,1)S(1)} %get-tuple-element.74), channel_id=1, source_target_pairs={{0,4},{1,5},{2,6},{3,7},{4,0},{5,1},{6,2},{7,3},{8,12},{9,13},{10,... | collective-permute-start | bytes 786440 | tf_op jit(solution)/shard_map/ppermute | solution.py:87
  142.4 13.8 %collective-permute-start.22 = (bf16[256,512]{1,0:T(8,128)(2,1)S(1)}, bf16[256,512]{1,0:T(8,128)(2,1)S(1)}, u32[]{:S(2)}, u32[]{:S(2)}) collective-permute-start(bf16[256,512]{1,0:T(8,128)(2,1)S(1)} %get-tuple-element.75), channel_id=1, source_target_pairs={{0,6},{1,7},{2,4},{3,5},{4,2},{5,3},{6,0},{7,1},{8,14},{9,15},{10,... | collective-permute-start | bytes 786440 | tf_op jit(solution)/shard_map/ppermute | solution.py:87
  156.3 10.2 %collective-permute-start.28 = (bf16[256,512]{1,0:T(8,128)(2,1)S(1)}, bf16[256,512]{1,0:T(8,128)(2,1)S(1)}, u32[]{:S(2)}, u32[]{:S(2)}) collective-permute-start(bf16[256,512]{1,0:T(8,128)(2,1)S(1)} %add_pieces.3.refs_0_), channel_id=1, source_target_pairs={{0,6},{1,7},{2,4},{3,5},{4,2},{5,3},{6,0},{7,1},{8,14},{9,15},{10,... | collective-permute-start | bytes 786440 | tf_op jit(solution)/shard_map/ppermute | solution.py:87
  158.0 12.7 %collective-permute-start.26 = (bf16[256,512]{1,0:T(8,128)(2,1)S(1)}, bf16[256,512]{1,0:T(8,128)(2,1)S(1)}, u32[]{:S(2)}, u32[]{:S(2)}) collective-permute-start(bf16[256,512]{1,0:T(8,128)(2,1)S(1)} %add_pieces.3.refs_0_), channel_id=1, source_target_pairs={{0,4},{1,5},{2,6},{3,7},{4,0},{5,1},{6,2},{7,3},{8,12},{9,13},{10,... | collective-permute-start | bytes 786440 | tf_op jit(solution)/shard_map/ppermute | solution.py:87
  159.5 11.3 %collective-permute-start.24 = (bf16[256,512]{1,0:T(8,128)(2,1)S(1)}, bf16[256,512]{1,0:T(8,128)(2,1)S(1)}, u32[]{:S(2)}, u32[]{:S(2)}) collective-permute-start(bf16[256,512]{1,0:T(8,128)(2,1)S(1)} %add_pieces.3.refs_0_), channel_id=1, source_target_pairs={{0,2},{1,3},{2,0},{3,1},{4,6},{5,7},{6,4},{7,5},{8,10},{9,11},{10,... | collective-permute-start | bytes 786440 | tf_op jit(solution)/shard_map/ppermute | solution.py:87
  159.9 19.3 %collective-permute-start.23 = (bf16[256,512]{1,0:T(8,128)(2,1)S(1)}, bf16[256,512]{1,0:T(8,128)(2,1)S(1)}, u32[]{:S(2)}, u32[]{:S(2)}) collective-permute-start(bf16[256,512]{1,0:T(8,128)(2,1)S(1)} %add_pieces.3.refs_0_), channel_id=1, source_target_pairs={{0,1},{1,0},{2,3},{3,2},{4,5},{5,4},{6,7},{7,6},{8,9},{9,8},{10,11... | collective-permute-start | bytes 786440 | tf_op jit(solution)/shard_map/ppermute | solution.py:87
  166.5 12.6 %collective-permute-start.29 = (bf16[256,512]{1,0:T(8,128)(2,1)S(1)}, bf16[256,512]{1,0:T(8,128)(2,1)S(1)}, u32[]{:S(2)}, u32[]{:S(2)}) collective-permute-start(bf16[256,512]{1,0:T(8,128)(2,1)S(1)} %collective-permute-done.28.refs_3_), channel_id=1, source_target_pairs={{0,1},{1,0},{2,3},{3,2},{4,5},{5,4},{6,7},{7,6},{8,9},{9,8},{10,11... | collective-permute-start | bytes 786440 | tf_op jit(solution)/shard_map/ppermute | solution.py:87
  170.7 8.4 %collective-permute-start.27 = (bf16[256,512]{1,0:T(8,128)(2,1)S(1)}, bf16[256,512]{1,0:T(8,128)(2,1)S(1)}, u32[]{:S(2)}, u32[]{:S(2)}) collective-permute-start(bf16[256,512]{1,0:T(8,128)(2,1)S(1)} %collective-permute-done.26.refs_2_), channel_id=1, source_target_pairs={{0,1},{1,0},{2,3},{3,2},{4,5},{5,4},{6,7},{7,6},{8,9},{9,8},{10,11... | collective-permute-start | bytes 786440 | tf_op jit(solution)/shard_map/ppermute | solution.py:87
  170.8 8.4 %collective-permute-start.25 = (bf16[256,512]{1,0:T(8,128)(2,1)S(1)}, bf16[256,512]{1,0:T(8,128)(2,1)S(1)}, u32[]{:S(2)}, u32[]{:S(2)}) collective-permute-start(bf16[256,512]{1,0:T(8,128)(2,1)S(1)} %collective-permute-done.24.refs_1_), channel_id=1, source_target_pairs={{0,1},{1,0},{2,3},{3,2},{4,5},{5,4},{6,7},{7,6},{8,9},{9,8},{10,11... | collective-permute-start | bytes 786440 | tf_op jit(solution)/shard_map/ppermute | solution.py:87
  179.2 15.9 %copy-start.6 = (f32[4,64]{1,0:T(4,128)S(1)}, f32[4,64]{1,0:T(4,128)}, u32[]{:S(2)}) copy-start(f32[4,64]{1,0:T(4,128)} %refs_7_.1) | copy-start | bytes 3076
  187.4 1.2 collective-permute-start.30
  188.6 4.5 %collective-permute-start.33 = (f32[2,256]{1,0:T(2,128)S(1)}, f32[2,256]{1,0:T(2,128)S(1)}, u32[]{:S(2)}, u32[]{:S(2)}) collective-permute-start(f32[2,256]{1,0:T(2,128)S(1)} %norm_pair.1.refs_0_), channel_id=1, source_target_pairs={{0,6},{1,7},{2,4},{3,5},{4,2},{5,3},{6,0},{7,1},{8,14},{9,15},{10,... | collective-permute-start | bytes 6152 | tf_op jit(solution)/shard_map/ppermute | solution.py:87
  190.0 3.6 %collective-permute-start.32 = (f32[2,256]{1,0:T(2,128)S(1)}, f32[2,256]{1,0:T(2,128)S(1)}, u32[]{:S(2)}, u32[]{:S(2)}) collective-permute-start(f32[2,256]{1,0:T(2,128)S(1)} %norm_pair.1.refs_0_), channel_id=1, source_target_pairs={{0,4},{1,5},{2,6},{3,7},{4,0},{5,1},{6,2},{7,3},{8,12},{9,13},{10,... | collective-permute-start | bytes 6152 | tf_op jit(solution)/shard_map/ppermute | solution.py:87
  191.5 3.6 %collective-permute-start.31 = (f32[2,256]{1,0:T(2,128)S(1)}, f32[2,256]{1,0:T(2,128)S(1)}, u32[]{:S(2)}, u32[]{:S(2)}) collective-permute-start(f32[2,256]{1,0:T(2,128)S(1)} %norm_pair.1.refs_0_), channel_id=1, source_target_pairs={{0,2},{1,3},{2,0},{3,1},{4,6},{5,7},{6,4},{7,5},{8,10},{9,11},{10,... | collective-permute-start | bytes 6152 | tf_op jit(solution)/shard_map/ppermute | solution.py:87

commit v5 on v4

--- a/solution.py
+++ b/solution.py
@@ -208,14 +208,20 @@
     def stencil_body(field, pot, scal, out, energy):
         for p in range(perts):
             energy[p * orbs : (p + 1) * orbs, :] = per_row(scal[...], gy)
-        block = 32
+        block = 8
 
         def rows_step(i, carry):
             rows = pl.ds(pl.multiple_of(i * block, block), block)
             base = energy[rows, :] + centre_half
 
+            loaded = {
+                (z, x): field[rows, col(z, x) : col(z, x) + gy]
+                for z in range(gz)
+                for x in range(planes)
+            }
+
             def at(z, x):
-                return field[rows, col(z, x) : col(z, x) + gy]
+                return loaded[z, x]
 
             for z in range(gz):
                 for x in range(planes):

time: 201 us -> 205 us (1.020)
  Pallas kernels: 113 us -> 117 us
    pallas_call x23, Pallas kernels: 113 us -> 117 us  [run(): pl.pallas_call(body, in_specs=[pl.BlockSpec(memory_space=kinds[kind]) for...]
  transfers between devices with their start and end apart: 34 -> 34, of which waited for: 14 -> 15; matrix products, arithmetic and copies ran while one was open for 0% -> 0% of each run, Pallas kernels for 39% -> 40%
where the time goes in v5:
time: 205 us
  Pallas kernels  117 us (57%)
  waiting for transfers between devices  51.5 us (25%)
  starting transfers between devices  32.8 us (16%)
  local copies, waits for them, and re-layouts  2.22 us (1%)
    pallas_call x23, Pallas kernels, run(): pl.pallas_call(body, in_specs=[pl.BlockSpec(memory_space=kinds[kind]) for...  117 us
    ppermute x28, waiting for transfers between devices, swap(): return lax.ppermute(array, axis, [(i, i ^ mask) for i in range(count)])  51.5 us
    ppermute x28, starting transfers between devices, swap(): return lax.ppermute(array, axis, [(i, i ^ mask) for i in range(count)])  23.8 us
    ppermute x3, starting transfers between devices, halos_of(): lax.ppermute(low_edge, 'dom', behind)  8.25 us
  transfers between devices with their start and end apart: 34, of which 15 were waited for; matrix products, arithmetic and copies ran while one was open for 0% of the time, Pallas kernels for 40%

profile of v5, /device:TPU:0, one launch (start us, length us, event | category | flops | bytes accessed | tf_op | source)
XLA Modules:
  0.0 204.6 jit_solution(17483334809503615819)
XLA Ops:
  0.7 2.2 %copy-done = f32[4,64,4,8,128]{4,3,2,1,0:T(8,128)S(1)} copy-done((f32[4,64,4,8,128]{4,3,2,1,0:T(8,128)S(1)}, f32[4,64,4,8,128]{4,3,2,1,0:T(8,128)}, u32[]{:S(2)}) %copy-start) | copy-done | bytes 4194328
  2.9 1.3 flatten.1
  4.7 3.0 %collective-permute-start.1 = (bf16[256,2048]{1,0:T(8,128)(2,1)S(1)}, bf16[256,2048]{1,0:T(8,128)(2,1)S(1)}, u32[]{:S(2)}, u32[]{:S(2)}) collective-permute-start(bf16[256,2048]{1,0:T(8,128)(2,1)S(1)} %get-tuple-element.45), channel_id=1, source_target_pairs={{1,0},{2,1},{3,2},{4,3},{5,4},{6,5},{7,6},{0,7},{9,8},{10,9},{11,1... | collective-permute-start | bytes 3145736 | tf_op jit(solution)/shard_map/ppermute | solution.py:122
  7.7 24.0 %relay.1.lock.refs_4_ = bf16[4096,4096]{1,0:T(8,128)(2,1)} custom-call(bf16[4096,4,8,128]{3,2,1,0:T(8,128)(2,1)} %source.1), custom_call_target="tpu_custom_call" | custom-call | tf_op jit(solution)/shard_map/relay/pallas_call | solution.py:18
  32.1 6.8 %stencil.2.part_ref = f32[256,4096]{1,0:T(8,128)S(1)} custom-call(f32[256,4096]{1,0:T(8,128)S(1)} %get-tuple-element.42.field.refs_7_, f32[1,4096]{1,0:T(1,128)S(1)} %get-tuple-element.43.pot, f32[1,64]{1,0:T(1,128)S(1)} %bitcast.6), custom_call_target="tpu_custom_call" | custom-call | tf_op jit(solution)/shard_map/stencil/pallas_call | solution.py:18
  38.9 7.9 %margin_other.1 = (f32[256,4096]{1,0:T(8,128)S(1)}, bf16[256,4096]{1,0:T(8,128)(2,1)S(1)}, bf16[256,2048]{1,0:T(8,128)(2,1)S(1)}) custom-call(s32[2]{0:T(128)S(1)} %pad_add_fusion.placed.where_ref, f32[256,4096]{1,0:T(8,128)S(1)} %stencil.2.part_ref, bf16[256,2048]{1,0:T(8,128)(2,1)S(1)} %collective-permute-done.low_ref, ...), custom_call_target="tpu_custom_call", output_to_operand_aliasing={{0}: (1, {})} | custom-call | tf_op jit(solution)/shard_map/margin_other/pallas_call | solution.py:18
  46.9 7.9 %margin_own.1.own_ref = f32[256,2048]{1,0:T(8,128)S(1)} custom-call(s32[2]{0:T(128)S(1)} %pad_add_fusion.placed.where_ref, bf16[256,4096]{1,0:T(8,128)(2,1)S(1)} %get-tuple-element.48.rounded_ref, bf16[4096,4096]{1,0:T(8,128)(2,1)} %relay.1.lock.refs_4_), custom_call_target="tpu_custom_call" | custom-call | tf_op jit(solution)/shard_map/margin_own/pallas_call | solution.py:18
  55.0 1.4 collective-permute-start.3
  56.4 1.5 collective-permute-start.4
  57.9 0.9 collective-permute-start.5
  58.8 5.4 %collective-permute-done.3.refs_1_ = bf16[256,512]{1,0:T(8,128)(2,1)S(1)} collective-permute-done((bf16[256,512]{1,0:T(8,128)(2,1)S(1)}, bf16[256,512]{1,0:T(8,128)(2,1)S(1)}, u32[]{:S(2)}, u32[]{:S(2)}) %collective-permute-start.3) | collective-permute-done | bytes 262176 | tf_op jit(solution)/shard_map/ppermute | solution.py:87
  64.2 5.3 %collective-permute-done.4.refs_2_ = bf16[256,512]{1,0:T(8,128)(2,1)S(1)} collective-permute-done((bf16[256,512]{1,0:T(8,128)(2,1)S(1)}, bf16[256,512]{1,0:T(8,128)(2,1)S(1)}, u32[]{:S(2)}, u32[]{:S(2)}) %collective-permute-start.4) | collective-permute-done | bytes 262176 | tf_op jit(solution)/shard_map/ppermute | solution.py:87
  69.4 1.6 collective-permute-done.5.refs_3_
  71.2 1.8 collective-permute-start.11
  73.3 1.4 collective-permute-start.7
  74.7 6.7 %collective-permute-done.11.refs_3_ = bf16[256,512]{1,0:T(8,128)(2,1)S(1)} collective-permute-done((bf16[256,512]{1,0:T(8,128)(2,1)S(1)}, bf16[256,512]{1,0:T(8,128)(2,1)S(1)}, u32[]{:S(2)}, u32[]{:S(2)}) %collective-permute-start.11) | collective-permute-done | bytes 262176 | tf_op jit(solution)/shard_map/ppermute | solution.py:87
  81.4 4.3 %collective-permute-done.9.refs_2_ = bf16[256,512]{1,0:T(8,128)(2,1)S(1)} collective-permute-done((bf16[256,512]{1,0:T(8,128)(2,1)S(1)}, bf16[256,512]{1,0:T(8,128)(2,1)S(1)}, u32[]{:S(2)}, u32[]{:S(2)}) %collective-permute-start.9) | collective-permute-done | bytes 262176 | tf_op jit(solution)/shard_map/ppermute | solution.py:87
  86.2 7.9 %remove_own.2.refs_5_ = f32[256,4096]{1,0:T(8,128)S(1)} custom-call(s32[2]{0:T(128)S(1)} %pad_add_fusion.placed.where_ref, bf16[256,512]{1,0:T(8,128)(2,1)S(1)} %add_pieces.2.refs_0_, bf16[256,512]{1,0:T(8,128)(2,1)S(1)} %collective-permute-done.7.refs_1_, bf16[256,512]{1,0:T(8,128)(2,1)S(1)} %collective-permute-done.9.refs_2_, ...), custom_call_target="tpu_custom_call" | custom-call | tf_op jit(solution)/shard_map/remove_own/pallas_call | solution.py:18
  94.1 6.1 %first_finish.2 = (f32[256,4096]{1,0:T(8,128)S(1)}, f32[256,4096]{1,0:T(8,128)S(1)}, bf16[256,1024]{1,0:T(8,128)(2,1)S(1)}, bf16[256,1024]{1,0:T(8,128)(2,1)S(1)...) custom-call(s32[2]{0:T(128)S(1)} %pad_add_fusion.placed.where_ref, ...), custom_call_target="tpu_custom_call", output_to_operand_aliasing={{0}: (7, {}), {1}: (8, {})} | custom-call | tf_op jit(solution)/shard_map/first_finish/pallas_call | solution.py:18
  100.5 2.6 %collective-permute-start.14 = (bf16[256,1024]{1,0:T(8,128)(2,1)S(1)}, bf16[256,1024]{1,0:T(8,128)(2,1)S(1)}, u32[]{:S(2)}, u32[]{:S(2)}) collective-permute-start(bf16[256,1024]{1,0:T(8,128)(2,1)S(1)} %get-tuple-element.61), channel_id=1, source_target_pairs={{1,0},{2,1},{3,2},{4,3},{5,4},{6,5},{7,6},{0,7},{9,8},{10,9},{11,1... | collective-permute-start | bytes 1572872 | tf_op jit(solution)/shard_map/ppermute | solution.py:122
  103.1 6.1 %first_finish.3 = (f32[256,4096]{1,0:T(8,128)S(1)}, f32[256,4096]{1,0:T(8,128)S(1)}, bf16[256,1024]{1,0:T(8,128)(2,1)S(1)}, bf16[256,1024]{1,0:T(8,128)(2,1)S(1)...) custom-call(s32[2]{0:T(128)S(1)} %pad_add_fusion.placed.where_ref, ...), custom_call_target="tpu_custom_call", output_to_operand_aliasing={{0}: (7, {}), {1}: (8, {})} | custom-call | tf_op jit(solution)/shard_map/first_finish/pallas_call | solution.py:18
  109.3 2.6 %collective-permute-start.18 = (bf16[256,1024]{1,0:T(8,128)(2,1)S(1)}, bf16[256,1024]{1,0:T(8,128)(2,1)S(1)}, u32[]{:S(2)}, u32[]{:S(2)}) collective-permute-start(bf16[256,1024]{1,0:T(8,128)(2,1)S(1)} %get-tuple-element.67), channel_id=1, source_target_pairs={{1,0},{2,1},{3,2},{4,3},{5,4},{6,5},{7,6},{0,7},{9,8},{10,9},{11,1... | collective-permute-start | bytes 1572872 | tf_op jit(solution)/shard_map/ppermute | solution.py:122
  111.9 1.6 collective-permute-start.15
  113.5 2.3 %collective-permute-done.15.two = bf16[4,4096]{1,0:T(4,128)(2,1)S(1)} collective-permute-done((bf16[4,4096]{1,0:T(4,128)(2,1)S(1)}, bf16[4,4096]{1,0:T(4,128)(2,1)S(1)}, u32[]{:S(2)}, u32[]{:S(2)}) %collective-permute-start.15) | collective-permute-done | bytes 32800 | tf_op jit(solution)/shard_map/ppermute | solution.py:87
  115.9 3.0 %collective-permute-start.16 = (bf16[4,4096]{1,0:T(4,128)(2,1)S(1)}, bf16[4,4096]{1,0:T(4,128)(2,1)S(1)}, u32[]{:S(2)}, u32[]{:S(2)}) collective-permute-start(bf16[4,4096]{1,0:T(4,128)(2,1)S(1)} %add_density.1.one), channel_id=1, source_target_pairs={{0,16},{8,24},{16,0},{24,8},{1,17},{9,25},{17,1},{25,9},{2,18},{10... | collective-permute-start | bytes 98312 | tf_op jit(solution)/shard_map/ppermute | solution.py:87
  118.9 6.8 %stencil.3.part_ref = f32[256,4096]{1,0:T(8,128)S(1)} custom-call(f32[256,4096]{1,0:T(8,128)S(1)} %get-tuple-element.59.field.refs_4_, f32[1,4096]{1,0:T(1,128)S(1)} %get-tuple-element.43.pot, f32[1,64]{1,0:T(1,128)S(1)} %bitcast.7), custom_call_target="tpu_custom_call" | custom-call | tf_op jit(solution)/shard_map/stencil/pallas_call | solution.py:18
  125.7 0.7 potential.1
  126.4 8.1 %margin_early.1 = (f32[256,4096]{1,0:T(8,128)S(1)}, f32[256,4096]{1,0:T(8,128)S(1)}) custom-call(s32[2]{0:T(128)S(1)} %pad_add_fusion.placed.where_ref, f32[256,4096]{1,0:T(8,128)S(1)} %stencil.3.part_ref, bf16[256,1024]{1,0:T(8,128)(2,1)S(1)} %collective-permute-done.13.low, ...), custom_call_target="tpu_custom_call", output_to_operand_aliasing={{0}: (1, {})} | custom-call | tf_op jit(solution)/shard_map/margin_early/pallas_call | solution.py:18
  134.6 5.2 %margin_late.1 = (f32[256,4096]{1,0:T(8,128)S(1)}, bf16[256,2048]{1,0:T(8,128)(2,1)S(1)}, bf16[256,2048]{1,0:T(8,128)(2,1)S(1)}) custom-call(s32[2]{0:T(128)S(1)} %pad_add_fusion.placed.where_ref, f32[256,4096]{1,0:T(8,128)S(1)} %get-tuple-element.65.part_ref, bf16[256,1024]{1,0:T(8,128)(2,1)S(1)} %collective-permute-done.17.low, ...), custom_call_target="tpu_custom_call", output_to_operand_aliasing={{0}: (1, {})} | custom-call | tf_op jit(solution)/shard_map/margin_late/pallas_call | solution.py:18
  139.8 5.3 %margin_late_own.1.own_ref = f32[256,2048]{1,0:T(8,128)S(1)} custom-call(s32[2]{0:T(128)S(1)} %pad_add_fusion.placed.where_ref, bf16[256,2048]{1,0:T(8,128)(2,1)S(1)} %get-tuple-element.70.rounded_ref, bf16[4096,4096]{1,0:T(8,128)(2,1)} %relay.1.lock.refs_4_, f32[256,4096]{1,0:T(8,128)S(1)} %get-tuple-element.69.early_ref), custom_call_target="tpu_custom_call" | custom-call | tf_op jit(solution)/shard_map/margin_late_own/pallas_call | solution.py:18
  145.4 0.5 collective-permute-start.21
  145.9 2.9 %collective-permute-start.22 = (bf16[256,512]{1,0:T(8,128)(2,1)S(1)}, bf16[256,512]{1,0:T(8,128)(2,1)S(1)}, u32[]{:S(2)}, u32[]{:S(2)}) collective-permute-start(bf16[256,512]{1,0:T(8,128)(2,1)S(1)} %get-tuple-element.75), channel_id=1, source_target_pairs={{0,6},{1,7},{2,4},{3,5},{4,2},{5,3},{6,0},{7,1},{8,14},{9,15},{10,... | collective-permute-start | bytes 786440 | tf_op jit(solution)/shard_map/ppermute | solution.py:87
  148.8 5.6 %collective-permute-done.20.refs_1_ = bf16[256,512]{1,0:T(8,128)(2,1)S(1)} collective-permute-done((bf16[256,512]{1,0:T(8,128)(2,1)S(1)}, bf16[256,512]{1,0:T(8,128)(2,1)S(1)}, u32[]{:S(2)}, u32[]{:S(2)}) %collective-permute-start.20) | collective-permute-done | bytes 262176 | tf_op jit(solution)/shard_map/ppermute | solution.py:87
  154.5 5.3 %collective-permute-done.21.refs_2_ = bf16[256,512]{1,0:T(8,128)(2,1)S(1)} collective-permute-done((bf16[256,512]{1,0:T(8,128)(2,1)S(1)}, bf16[256,512]{1,0:T(8,128)(2,1)S(1)}, u32[]{:S(2)}, u32[]{:S(2)}) %collective-permute-start.21) | collective-permute-done | bytes 262176 | tf_op jit(solution)/shard_map/ppermute | solution.py:87
  159.9 1.7 collective-permute-start.28
  161.5 1.5 collective-permute-start.26
  163.4 6.7 %collective-permute-done.28.refs_3_ = bf16[256,512]{1,0:T(8,128)(2,1)S(1)} collective-permute-done((bf16[256,512]{1,0:T(8,128)(2,1)S(1)}, bf16[256,512]{1,0:T(8,128)(2,1)S(1)}, u32[]{:S(2)}, u32[]{:S(2)}) %collective-permute-start.28) | collective-permute-done | bytes 262176 | tf_op jit(solution)/shard_map/ppermute | solution.py:87
  170.1 4.2 %collective-permute-done.26.refs_2_ = bf16[256,512]{1,0:T(8,128)(2,1)S(1)} collective-permute-done((bf16[256,512]{1,0:T(8,128)(2,1)S(1)}, bf16[256,512]{1,0:T(8,128)(2,1)S(1)}, u32[]{:S(2)}, u32[]{:S(2)}) %collective-permute-start.26) | collective-permute-done | bytes 262176 | tf_op jit(solution)/shard_map/ppermute | solution.py:87
  174.8 7.9 %remove_own.3.refs_5_ = f32[256,4096]{1,0:T(8,128)S(1)} custom-call(s32[2]{0:T(128)S(1)} %pad_add_fusion.placed.where_ref, bf16[256,512]{1,0:T(8,128)(2,1)S(1)} %add_pieces.3.refs_0_, bf16[256,512]{1,0:T(8,128)(2,1)S(1)} %collective-permute-done.24.refs_1_, bf16[256,512]{1,0:T(8,128)(2,1)S(1)} %collective-permute-done.26.refs_2_, ...), custom_call_target="tpu_custom_call" | custom-call | tf_op jit(solution)/shard_map/remove_own/pallas_call | solution.py:18
  182.7 8.2 %second_finish.1 = (f32[256,4096]{1,0:T(8,128)S(1)}, f32[2,256]{1,0:T(2,128)S(1)}) custom-call(s32[2]{0:T(128)S(1)} %pad_add_fusion.placed.where_ref, bf16[256,512]{1,0:T(8,128)(2,1)S(1)} %collective-permute-done.23.refs_0_, bf16[256,512]{1,0:T(8,128)(2,1)S(1)} %collective-permute-done.25.refs_1_, ...), custom_call_target="tpu_custom_call", output_to_operand_aliasing={{0}: (7, {})} | custom-call | tf_op jit(solution)/shard_map/second_finish/pallas_call | solution.py:18
  191.0 1.1 collective-permute-done.30.two
  192.1 1.5 collective-permute-start.33
  193.6 1.5 collective-permute-start.32
  195.0 0.6 collective-permute-start.31
  195.6 1.0 collective-permute-done.33.refs_3_
  196.6 0.6 collective-permute-done.32.refs_2_
  197.2 1.5 collective-permute-done.31.refs_1_
  198.6 5.8 %final.1 = f32[256,4,8,128]{3,2,1,0:T(8,128)} custom-call(f32[2,256]{1,0:T(2,128)S(1)} %norm_pair.1.refs_0_, f32[2,256]{1,0:T(2,128)S(1)} %collective-permute-done.31.refs_1_, f32[2,256]{1,0:T(2,128)S(1)} %collective-permute-done.32.refs_2_, f32[2,256]{1,0:T(2,128)S(1)} %collective-permute-done.33.refs_3_, f32[256,4096]{1,0:T(8,128)S(1)} %get-tuple-element.59.field.refs_4_, ...), custom_call_target="tpu_custom_call" | custom-call | tf_op jit(solution)/shard_map/final/pallas_call | solution.py:18
  (60 shorter events, 3.9 us)
Async XLA Ops:
  0.7 2.2 %copy-start = (f32[4,64,4,8,128]{4,3,2,1,0:T(8,128)S(1)}, f32[4,64,4,8,128]{4,3,2,1,0:T(8,128)}, u32[]{:S(2)}) copy-start(f32[4,64,4,8,128]{4,3,2,1,0:T(8,128)} %param.9) | copy-start | bytes 12582916
  4.2 34.7 %collective-permute-start = (bf16[256,2048]{1,0:T(8,128)(2,1)S(1)}, bf16[256,2048]{1,0:T(8,128)(2,1)S(1)}, u32[]{:S(2)}, u32[]{:S(2)}) collective-permute-start(bf16[256,2048]{1,0:T(8,128)(2,1)S(1)} %get-tuple-element.44), channel_id=1, source_target_pairs={{0,1},{1,2},{2,3},{3,4},{4,5},{5,6},{6,7},{7,0},{8,9},{9,10},{10,1... | collective-permute-start | bytes 3145736 | tf_op jit(solution)/shard_map/ppermute | solution.py:122
  4.7 27.0 %copy-start.1 = (f32[64,4,8,128]{3,2,1,0:T(8,128)S(1)}, f32[64,4,8,128]{3,2,1,0:T(8,128)}, u32[]{:S(2)}) copy-start(f32[64,4,8,128]{3,2,1,0:T(8,128)} %occ.1) | copy-start | bytes 3145732
  4.7 27.0 %copy-start.2 = (f32[4,4,8,128]{3,2,1,0:T(8,128)S(1)}, f32[4,4,8,128]{3,2,1,0:T(8,128)}, u32[]{:S(2)}) copy-start(f32[4,4,8,128]{3,2,1,0:T(8,128)} %pert.1) | copy-start | bytes 196612
  4.7 27.0 %copy-start.3 = (f32[4,8,128]{2,1,0:T(8,128)S(1)}, f32[4,8,128]{2,1,0:T(8,128)}, u32[]{:S(2)}) copy-start(f32[4,8,128]{2,1,0:T(8,128)} %pot.1) | copy-start | bytes 49156
  4.7 27.1 %copy-start.4 = (f32[4,8,128]{2,1,0:T(8,128)S(1)}, f32[4,8,128]{2,1,0:T(8,128)}, u32[]{:S(2)}) copy-start(f32[4,8,128]{2,1,0:T(8,128)} %xc.1) | copy-start | bytes 49156
  4.7 27.4 %copy-start.7 = (f32[64]{0:T(128)S(1)}, f32[64]{0:T(128)}, u32[]{:S(2)}) copy-start(f32[64]{0:T(128)} %param.15) | copy-start | bytes 772
  4.7 34.2 %collective-permute-start.1 = (bf16[256,2048]{1,0:T(8,128)(2,1)S(1)}, bf16[256,2048]{1,0:T(8,128)(2,1)S(1)}, u32[]{:S(2)}, u32[]{:S(2)}) collective-permute-start(bf16[256,2048]{1,0:T(8,128)(2,1)S(1)} %get-tuple-element.45), channel_id=1, source_target_pairs={{1,0},{2,1},{3,2},{4,3},{5,4},{6,5},{7,6},{0,7},{9,8},{10,9},{11,1... | collective-permute-start | bytes 3145736 | tf_op jit(solution)/shard_map/ppermute | solution.py:122
  46.8 8.0 %collective-permute-start.2 = (bf16[256,2048]{1,0:T(8,128)(2,1)S(1)}, bf16[256,2048]{1,0:T(8,128)(2,1)S(1)}, u32[]{:S(2)}, u32[]{:S(2)}) collective-permute-start(bf16[256,2048]{1,0:T(8,128)(2,1)S(1)} %get-tuple-element.49), channel_id=1, source_target_pairs={{0,1},{1,0},{2,3},{3,2},{4,5},{5,4},{6,7},{7,6},{8,9},{9,8},{10,11... | collective-permute-start | bytes 3145736 | tf_op jit(solution)/shard_map/ppermute | solution.py:87
  55.0 9.2 %collective-permute-start.3 = (bf16[256,512]{1,0:T(8,128)(2,1)S(1)}, bf16[256,512]{1,0:T(8,128)(2,1)S(1)}, u32[]{:S(2)}, u32[]{:S(2)}) collective-permute-start(bf16[256,512]{1,0:T(8,128)(2,1)S(1)} %get-tuple-element.51), channel_id=1, source_target_pairs={{0,2},{1,3},{2,0},{3,1},{4,6},{5,7},{6,4},{7,5},{8,10},{9,11},{10,... | collective-permute-start | bytes 786440 | tf_op jit(solution)/shard_map/ppermute | solution.py:87
  56.4 13.1 %collective-permute-start.4 = (bf16[256,512]{1,0:T(8,128)(2,1)S(1)}, bf16[256,512]{1,0:T(8,128)(2,1)S(1)}, u32[]{:S(2)}, u32[]{:S(2)}) collective-permute-start(bf16[256,512]{1,0:T(8,128)(2,1)S(1)} %get-tuple-element.52), channel_id=1, source_target_pairs={{0,4},{1,5},{2,6},{3,7},{4,0},{5,1},{6,2},{7,3},{8,12},{9,13},{10,... | collective-permute-start | bytes 786440 | tf_op jit(solution)/shard_map/ppermute | solution.py:87
  57.9 13.2 %collective-permute-start.5 = (bf16[256,512]{1,0:T(8,128)(2,1)S(1)}, bf16[256,512]{1,0:T(8,128)(2,1)S(1)}, u32[]{:S(2)}, u32[]{:S(2)}) collective-permute-start(bf16[256,512]{1,0:T(8,128)(2,1)S(1)} %get-tuple-element.53), channel_id=1, source_target_pairs={{0,6},{1,7},{2,4},{3,5},{4,2},{5,3},{6,0},{7,1},{8,14},{9,15},{10,... | collective-permute-start | bytes 786440 | tf_op jit(solution)/shard_map/ppermute | solution.py:87
  71.2 22.9 %copy-start.5 = (f32[4,64]{1,0:T(4,128)S(1)}, f32[4,64]{1,0:T(4,128)}, u32[]{:S(2)}) copy-start(f32[4,64]{1,0:T(4,128)} %refs_9_.3) | copy-start | bytes 3076
  71.2 10.2 %collective-permute-start.11 = (bf16[256,512]{1,0:T(8,128)(2,1)S(1)}, bf16[256,512]{1,0:T(8,128)(2,1)S(1)}, u32[]{:S(2)}, u32[]{:S(2)}) collective-permute-start(bf16[256,512]{1,0:T(8,128)(2,1)S(1)} %add_pieces.2.refs_0_), channel_id=1, source_target_pairs={{0,6},{1,7},{2,4},{3,5},{4,2},{5,3},{6,0},{7,1},{8,14},{9,15},{10,... | collective-permute-start | bytes 786440 | tf_op jit(solution)/shard_map/ppermute | solution.py:87
  73.0 12.7 %collective-permute-start.9 = (bf16[256,512]{1,0:T(8,128)(2,1)S(1)}, bf16[256,512]{1,0:T(8,128)(2,1)S(1)}, u32[]{:S(2)}, u32[]{:S(2)}) collective-permute-start(bf16[256,512]{1,0:T(8,128)(2,1)S(1)} %add_pieces.2.refs_0_), channel_id=1, source_target_pairs={{0,4},{1,5},{2,6},{3,7},{4,0},{5,1},{6,2},{7,3},{8,12},{9,13},{10,... | collective-permute-start | bytes 786440 | tf_op jit(solution)/shard_map/ppermute | solution.py:87
  73.3 12.4 %collective-permute-start.7 = (bf16[256,512]{1,0:T(8,128)(2,1)S(1)}, bf16[256,512]{1,0:T(8,128)(2,1)S(1)}, u32[]{:S(2)}, u32[]{:S(2)}) collective-permute-start(bf16[256,512]{1,0:T(8,128)(2,1)S(1)} %add_pieces.2.refs_0_), channel_id=1, source_target_pairs={{0,2},{1,3},{2,0},{3,1},{4,6},{5,7},{6,4},{7,5},{8,10},{9,11},{10,... | collective-permute-start | bytes 786440 | tf_op jit(solution)/shard_map/ppermute | solution.py:87
  74.7 19.3 %collective-permute-start.6 = (bf16[256,512]{1,0:T(8,128)(2,1)S(1)}, bf16[256,512]{1,0:T(8,128)(2,1)S(1)}, u32[]{:S(2)}, u32[]{:S(2)}) collective-permute-start(bf16[256,512]{1,0:T(8,128)(2,1)S(1)} %add_pieces.2.refs_0_), channel_id=1, source_target_pairs={{0,1},{1,0},{2,3},{3,2},{4,5},{5,4},{6,7},{7,6},{8,9},{9,8},{10,11... | collective-permute-start | bytes 786440 | tf_op jit(solution)/shard_map/ppermute | solution.py:87
  81.4 12.7 %collective-permute-start.12 = (bf16[256,512]{1,0:T(8,128)(2,1)S(1)}, bf16[256,512]{1,0:T(8,128)(2,1)S(1)}, u32[]{:S(2)}, u32[]{:S(2)}) collective-permute-start(bf16[256,512]{1,0:T(8,128)(2,1)S(1)} %collective-permute-done.11.refs_3_), channel_id=1, source_target_pairs={{0,1},{1,0},{2,3},{3,2},{4,5},{5,4},{6,7},{7,6},{8,9},{9,8},{10,11... | collective-permute-start | bytes 786440 | tf_op jit(solution)/shard_map/ppermute | solution.py:87
  85.7 8.4 %collective-permute-start.10 = (bf16[256,512]{1,0:T(8,128)(2,1)S(1)}, bf16[256,512]{1,0:T(8,128)(2,1)S(1)}, u32[]{:S(2)}, u32[]{:S(2)}) collective-permute-start(bf16[256,512]{1,0:T(8,128)(2,1)S(1)} %collective-permute-done.9.refs_2_), channel_id=1, source_target_pairs={{0,1},{1,0},{2,3},{3,2},{4,5},{5,4},{6,7},{7,6},{8,9},{9,8},{10,11... | collective-permute-start | bytes 786440 | tf_op jit(solution)/shard_map/ppermute | solution.py:87
  85.7 8.4 %collective-permute-start.8 = (bf16[256,512]{1,0:T(8,128)(2,1)S(1)}, bf16[256,512]{1,0:T(8,128)(2,1)S(1)}, u32[]{:S(2)}, u32[]{:S(2)}) collective-permute-start(bf16[256,512]{1,0:T(8,128)(2,1)S(1)} %collective-permute-done.7.refs_1_), channel_id=1, source_target_pairs={{0,1},{1,0},{2,3},{3,2},{4,5},{5,4},{6,7},{7,6},{8,9},{9,8},{10,11... | collective-permute-start | bytes 786440 | tf_op jit(solution)/shard_map/ppermute | solution.py:87
  100.2 26.2 %collective-permute-start.13 = (bf16[256,1024]{1,0:T(8,128)(2,1)S(1)}, bf16[256,1024]{1,0:T(8,128)(2,1)S(1)}, u32[]{:S(2)}, u32[]{:S(2)}) collective-permute-start(bf16[256,1024]{1,0:T(8,128)(2,1)S(1)} %get-tuple-element.60), channel_id=1, source_target_pairs={{0,1},{1,2},{2,3},{3,4},{4,5},{5,6},{6,7},{7,0},{8,9},{9,10},{10,1... | collective-permute-start | bytes 1572872 | tf_op jit(solution)/shard_map/ppermute | solution.py:122
  100.5 25.9 %collective-permute-start.14 = (bf16[256,1024]{1,0:T(8,128)(2,1)S(1)}, bf16[256,1024]{1,0:T(8,128)(2,1)S(1)}, u32[]{:S(2)}, u32[]{:S(2)}) collective-permute-start(bf16[256,1024]{1,0:T(8,128)(2,1)S(1)} %get-tuple-element.61), channel_id=1, source_target_pairs={{1,0},{2,1},{3,2},{4,3},{5,4},{6,5},{7,6},{0,7},{9,8},{10,9},{11,1... | collective-permute-start | bytes 1572872 | tf_op jit(solution)/shard_map/ppermute | solution.py:122
  109.2 25.3 %collective-permute-start.17 = (bf16[256,1024]{1,0:T(8,128)(2,1)S(1)}, bf16[256,1024]{1,0:T(8,128)(2,1)S(1)}, u32[]{:S(2)}, u32[]{:S(2)}) collective-permute-start(bf16[256,1024]{1,0:T(8,128)(2,1)S(1)} %get-tuple-element.66), channel_id=1, source_target_pairs={{0,1},{1,2},{2,3},{3,4},{4,5},{5,6},{6,7},{7,0},{8,9},{9,10},{10,1... | collective-permute-start | bytes 1572872 | tf_op jit(solution)/shard_map/ppermute | solution.py:122
  109.3 25.3 %collective-permute-start.18 = (bf16[256,1024]{1,0:T(8,128)(2,1)S(1)}, bf16[256,1024]{1,0:T(8,128)(2,1)S(1)}, u32[]{:S(2)}, u32[]{:S(2)}) collective-permute-start(bf16[256,1024]{1,0:T(8,128)(2,1)S(1)} %get-tuple-element.67), channel_id=1, source_target_pairs={{1,0},{2,1},{3,2},{4,3},{5,4},{6,5},{7,6},{0,7},{9,8},{10,9},{11,1... | collective-permute-start | bytes 1572872 | tf_op jit(solution)/shard_map/ppermute | solution.py:122
  111.9 3.9 %collective-permute-start.15 = (bf16[4,4096]{1,0:T(4,128)(2,1)S(1)}, bf16[4,4096]{1,0:T(4,128)(2,1)S(1)}, u32[]{:S(2)}, u32[]{:S(2)}) collective-permute-start(bf16[4,4096]{1,0:T(4,128)(2,1)S(1)} %get-tuple-element.62.one), channel_id=1, source_target_pairs={{0,8},{8,0},{16,24},{24,16},{1,9},{9,1},{17,25},{25,17},{2,10},{10... | collective-permute-start | bytes 98312 | tf_op jit(solution)/shard_map/ppermute | solution.py:87
  115.9 9.8 %collective-permute-start.16 = (bf16[4,4096]{1,0:T(4,128)(2,1)S(1)}, bf16[4,4096]{1,0:T(4,128)(2,1)S(1)}, u32[]{:S(2)}, u32[]{:S(2)}) collective-permute-start(bf16[4,4096]{1,0:T(4,128)(2,1)S(1)} %add_density.1.one), channel_id=1, source_target_pairs={{0,16},{8,24},{16,0},{24,8},{1,17},{9,25},{17,1},{25,9},{2,18},{10... | collective-permute-start | bytes 98312 | tf_op jit(solution)/shard_map/ppermute | solution.py:87
  139.8 5.3 %collective-permute-start.19 = (bf16[256,2048]{1,0:T(8,128)(2,1)S(1)}, bf16[256,2048]{1,0:T(8,128)(2,1)S(1)}, u32[]{:S(2)}, u32[]{:S(2)}) collective-permute-start(bf16[256,2048]{1,0:T(8,128)(2,1)S(1)} %get-tuple-element.71), channel_id=1, source_target_pairs={{0,1},{1,0},{2,3},{3,2},{4,5},{5,4},{6,7},{7,6},{8,9},{9,8},{10,11... | collective-permute-start | bytes 3145736 | tf_op jit(solution)/shard_map/ppermute | solution.py:87
  145.3 9.2 %collective-permute-start.20 = (bf16[256,512]{1,0:T(8,128)(2,1)S(1)}, bf16[256,512]{1,0:T(8,128)(2,1)S(1)}, u32[]{:S(2)}, u32[]{:S(2)}) collective-permute-start(bf16[256,512]{1,0:T(8,128)(2,1)S(1)} %get-tuple-element.73), channel_id=1, source_target_pairs={{0,2},{1,3},{2,0},{3,1},{4,6},{5,7},{6,4},{7,5},{8,10},{9,11},{10,... | collective-permute-start | bytes 786440 | tf_op jit(solution)/shard_map/ppermute | solution.py:87
  145.4 14.4 %collective-permute-start.21 = (bf16[256,512]{1,0:T(8,128)(2,1)S(1)}, bf16[256,512]{1,0:T(8,128)(2,1)S(1)}, u32[]{:S(2)}, u32[]{:S(2)}) collective-permute-start(bf16[256,512]{1,0:T(8,128)(2,1)S(1)} %get-tuple-element.74), channel_id=1, source_target_pairs={{0,4},{1,5},{2,6},{3,7},{4,0},{5,1},{6,2},{7,3},{8,12},{9,13},{10,... | collective-permute-start | bytes 786440 | tf_op jit(solution)/shard_map/ppermute | solution.py:87
  145.9 13.8 %collective-permute-start.22 = (bf16[256,512]{1,0:T(8,128)(2,1)S(1)}, bf16[256,512]{1,0:T(8,128)(2,1)S(1)}, u32[]{:S(2)}, u32[]{:S(2)}) collective-permute-start(bf16[256,512]{1,0:T(8,128)(2,1)S(1)} %get-tuple-element.75), channel_id=1, source_target_pairs={{0,6},{1,7},{2,4},{3,5},{4,2},{5,3},{6,0},{7,1},{8,14},{9,15},{10,... | collective-permute-start | bytes 786440 | tf_op jit(solution)/shard_map/ppermute | solution.py:87
  159.9 10.2 %collective-permute-start.28 = (bf16[256,512]{1,0:T(8,128)(2,1)S(1)}, bf16[256,512]{1,0:T(8,128)(2,1)S(1)}, u32[]{:S(2)}, u32[]{:S(2)}) collective-permute-start(bf16[256,512]{1,0:T(8,128)(2,1)S(1)} %add_pieces.3.refs_0_), channel_id=1, source_target_pairs={{0,6},{1,7},{2,4},{3,5},{4,2},{5,3},{6,0},{7,1},{8,14},{9,15},{10,... | collective-permute-start | bytes 786440 | tf_op jit(solution)/shard_map/ppermute | solution.py:87
  161.5 12.7 %collective-permute-start.26 = (bf16[256,512]{1,0:T(8,128)(2,1)S(1)}, bf16[256,512]{1,0:T(8,128)(2,1)S(1)}, u32[]{:S(2)}, u32[]{:S(2)}) collective-permute-start(bf16[256,512]{1,0:T(8,128)(2,1)S(1)} %add_pieces.3.refs_0_), channel_id=1, source_target_pairs={{0,4},{1,5},{2,6},{3,7},{4,0},{5,1},{6,2},{7,3},{8,12},{9,13},{10,... | collective-permute-start | bytes 786440 | tf_op jit(solution)/shard_map/ppermute | solution.py:87
  163.1 11.3 %collective-permute-start.24 = (bf16[256,512]{1,0:T(8,128)(2,1)S(1)}, bf16[256,512]{1,0:T(8,128)(2,1)S(1)}, u32[]{:S(2)}, u32[]{:S(2)}) collective-permute-start(bf16[256,512]{1,0:T(8,128)(2,1)S(1)} %add_pieces.3.refs_0_), channel_id=1, source_target_pairs={{0,2},{1,3},{2,0},{3,1},{4,6},{5,7},{6,4},{7,5},{8,10},{9,11},{10,... | collective-permute-start | bytes 786440 | tf_op jit(solution)/shard_map/ppermute | solution.py:87
  163.4 19.2 %collective-permute-start.23 = (bf16[256,512]{1,0:T(8,128)(2,1)S(1)}, bf16[256,512]{1,0:T(8,128)(2,1)S(1)}, u32[]{:S(2)}, u32[]{:S(2)}) collective-permute-start(bf16[256,512]{1,0:T(8,128)(2,1)S(1)} %add_pieces.3.refs_0_), channel_id=1, source_target_pairs={{0,1},{1,0},{2,3},{3,2},{4,5},{5,4},{6,7},{7,6},{8,9},{9,8},{10,11... | collective-permute-start | bytes 786440 | tf_op jit(solution)/shard_map/ppermute | solution.py:87
  170.1 12.6 %collective-permute-start.29 = (bf16[256,512]{1,0:T(8,128)(2,1)S(1)}, bf16[256,512]{1,0:T(8,128)(2,1)S(1)}, u32[]{:S(2)}, u32[]{:S(2)}) collective-permute-start(bf16[256,512]{1,0:T(8,128)(2,1)S(1)} %collective-permute-done.28.refs_3_), channel_id=1, source_target_pairs={{0,1},{1,0},{2,3},{3,2},{4,5},{5,4},{6,7},{7,6},{8,9},{9,8},{10,11... | collective-permute-start | bytes 786440 | tf_op jit(solution)/shard_map/ppermute | solution.py:87
  174.3 8.4 %collective-permute-start.27 = (bf16[256,512]{1,0:T(8,128)(2,1)S(1)}, bf16[256,512]{1,0:T(8,128)(2,1)S(1)}, u32[]{:S(2)}, u32[]{:S(2)}) collective-permute-start(bf16[256,512]{1,0:T(8,128)(2,1)S(1)} %collective-permute-done.26.refs_2_), channel_id=1, source_target_pairs={{0,1},{1,0},{2,3},{3,2},{4,5},{5,4},{6,7},{7,6},{8,9},{9,8},{10,11... | collective-permute-start | bytes 786440 | tf_op jit(solution)/shard_map/ppermute | solution.py:87
  174.4 8.3 %collective-permute-start.25 = (bf16[256,512]{1,0:T(8,128)(2,1)S(1)}, bf16[256,512]{1,0:T(8,128)(2,1)S(1)}, u32[]{:S(2)}, u32[]{:S(2)}) collective-permute-start(bf16[256,512]{1,0:T(8,128)(2,1)S(1)} %collective-permute-done.24.refs_1_), channel_id=1, source_target_pairs={{0,1},{1,0},{2,3},{3,2},{4,5},{5,4},{6,7},{7,6},{8,9},{9,8},{10,11... | collective-permute-start | bytes 786440 | tf_op jit(solution)/shard_map/ppermute | solution.py:87
  182.7 15.9 %copy-start.6 = (f32[4,64]{1,0:T(4,128)S(1)}, f32[4,64]{1,0:T(4,128)}, u32[]{:S(2)}) copy-start(f32[4,64]{1,0:T(4,128)} %refs_7_.1) | copy-start | bytes 3076
  190.9 1.2 collective-permute-start.30
  192.1 4.5 %collective-permute-start.33 = (f32[2,256]{1,0:T(2,128)S(1)}, f32[2,256]{1,0:T(2,128)S(1)}, u32[]{:S(2)}, u32[]{:S(2)}) collective-permute-start(f32[2,256]{1,0:T(2,128)S(1)} %norm_pair.1.refs_0_), channel_id=1, source_target_pairs={{0,6},{1,7},{2,4},{3,5},{4,2},{5,3},{6,0},{7,1},{8,14},{9,15},{10,... | collective-permute-start | bytes 6152 | tf_op jit(solution)/shard_map/ppermute | solution.py:87
  193.6 3.6 %collective-permute-start.32 = (f32[2,256]{1,0:T(2,128)S(1)}, f32[2,256]{1,0:T(2,128)S(1)}, u32[]{:S(2)}, u32[]{:S(2)}) collective-permute-start(f32[2,256]{1,0:T(2,128)S(1)} %norm_pair.1.refs_0_), channel_id=1, source_target_pairs={{0,4},{1,5},{2,6},{3,7},{4,0},{5,1},{6,2},{7,3},{8,12},{9,13},{10,... | collective-permute-start | bytes 6152 | tf_op jit(solution)/shard_map/ppermute | solution.py:87
  195.0 3.6 %collective-permute-start.31 = (f32[2,256]{1,0:T(2,128)S(1)}, f32[2,256]{1,0:T(2,128)S(1)}, u32[]{:S(2)}, u32[]{:S(2)}) collective-permute-start(f32[2,256]{1,0:T(2,128)S(1)} %norm_pair.1.refs_0_), channel_id=1, source_target_pairs={{0,2},{1,3},{2,0},{3,1},{4,6},{5,7},{6,4},{7,5},{8,10},{9,11},{10,... | collective-permute-start | bytes 6152 | tf_op jit(solution)/shard_map/ppermute | solution.py:87
